TPU v7x, 32 devices: a whole 2x2x4 slice. The times are simulated.
32 devices in a mesh: fsdp: 8 (over z, y), ctx: 4 (over x, core).
Axes of the slice: x: 2, y: 2, z: 4, core: 2. Of those that a mesh axis runs over, the one named last changes fastest.
Arguments:
- tokens: bfloat16 [8, 1024, 2048], P('fsdp', 'ctx'), may hold values from -6 to 6
- norm_gain: bfloat16 [2048], P('fsdp'), may hold values from 0.5 to 1.5
- w_in: bfloat16 [2048, 8512], P('fsdp'), may hold values from -0.125 to 0.125
- conv_w: bfloat16 [4, 4352], P(None, 'fsdp'), may hold values from -3 to 3
- conv_b: bfloat16 [4352], P('fsdp'), may hold values from -0.5 to 0.5
- dt_bias: float32 [64], replicated, may hold values from -4.5 to -3
- a_log: float32 [64], replicated, may hold values from -7 to 0.5
- d_skip: float32 [64], replicated, may hold values from 0.5 to 2
- gate_gain: bfloat16 [4096], P('fsdp'), may hold values from 0.5 to 1.5
- w_out: bfloat16 [4096, 2048], P('fsdp'), may hold values from -0.09375 to 0.09375
- cotangent: bfloat16 [8, 1024, 2048], P('fsdp', 'ctx'), may hold values from -6 to 6
Outputs:
- output: bfloat16 [8, 1024, 2048], P('fsdp', 'ctx')
- grad_tokens: float32 [8, 1024, 2048], P('fsdp', 'ctx')
- grad_norm_gain: float32 [2048], P('fsdp')
- grad_w_in: float32 [2048, 8512], P('fsdp')
- grad_conv_w: float32 [4, 4352], P(None, 'fsdp')
- grad_conv_b: float32 [4352], P('fsdp')
- grad_dt_bias: float32 [64], replicated
- grad_a_log: float32 [64], replicated
- grad_d_skip: float32 [64], replicated
- grad_gate_gain: float32 [4096], P('fsdp')
- grad_w_out: float32 [4096, 2048], P('fsdp')
All inputs are finite; a program needn't handle non-finite values.
Results may differ from a plain program's by a relative error of at most 0.0085.
The roundings to bfloat16 on the way count: a program that leaves them out, or rounds other values in their place, can miss the bound.
Values may be sent and summed in bfloat16 or wider, within the bound.
No kernel may reach another device: no remote copies, remote signals or barrier semaphores. Data moves between devices by JAX's collectives and lax.ppermute only.
A program may use at most 320 MiB of HBM per device.

v0:
```python
import jax
import jax.numpy as jnp
from jax import lax
from jax.sharding import PartitionSpec as P

HEADS = 64
HEADDIM = 64
STATE = 128
KW = 4
GROUP = 256
CONV = 4352


EPS = 1e-05


def passed_along(block, axis, distance):
    devices = range(lax.axis_size(axis))
    route = [(i - distance, i) for i in devices if i - distance in devices]
    return lax.ppermute(block, axis, route)


def carried_in(part, axis, combine, identity, reverse):
    count = lax.axis_size(axis)
    place = lax.axis_index(axis)
    ahead = count - 1 - place if reverse else place
    gathered = jax.tree.map(lambda a: lax.all_gather(a, axis), part)
    state = jax.tree.map(lambda a, e: jnp.zeros_like(a) + jnp.asarray(e, a.dtype), part, identity)

    def one(turn, state):
        source = count - 1 - turn if reverse else turn
        return combine(
            state, jax.tree.map(lambda a: lax.dynamic_index_in_dim(a, source, 0, False), gathered)
        )

    return lax.fori_loop(0, ahead, one, state)


def in_norm(values, gain_vec):
    inverse = lax.rsqrt(jnp.mean(values * values, axis=-1, keepdims=True) + EPS)
    return values * inverse * gain_vec


def gate_norm(ssd_out, gate_z, gain_vec):
    gated = ssd_out * jax.nn.silu(gate_z)
    inverse = lax.rsqrt(jnp.mean(gated * gated, axis=-1, keepdims=True) + EPS)
    return gated * inverse * gain_vec


def conv_silu(padded, taps, offsets_bias):
    length = padded.shape[0] - taps.shape[0] + 1
    summed = offsets_bias[None, :] + taps[0][None, :] * padded[0:length]
    for offset in range(1, taps.shape[0]):
        summed = summed + taps[offset][None, :] * padded[offset : offset + length]
    return jax.nn.silu(summed)


def decay_matrix(cumulative):
    count = cumulative.shape[0]
    row_index = lax.broadcasted_iota(jnp.int32, (count, count), 0)
    col_index = lax.broadcasted_iota(jnp.int32, (count, count), 1)
    lower = (row_index >= col_index)[None]
    differ = cumulative.T[:, :, None] - cumulative.T[:, None, :]
    return jnp.where(lower, jnp.exp(jnp.where(lower, differ, 0.0)), 0.0)


def block_weighted(b_block, cumulative, step_sizes):
    tail_vals = jnp.exp(cumulative[-1][None, :] - cumulative) * step_sizes
    weighted = (tail_vals.T[:, :, None] * b_block.astype(jnp.float32)[None]).astype(jnp.bfloat16)
    return (tail_vals, weighted)


def link_states(earlier, later):
    return (earlier[0] * later[0], later[0][:, None, None] * earlier[1] + later[1])


def body(
    tokens, norm_gain, w_in, conv_w, conv_b, dt_bias, a_log, d_skip, gate_gain, w_out, cotangent
):
    gathered = (
        lax.all_gather(norm_gain, "fsdp", axis=0, tiled=True),
        lax.all_gather(w_in, "fsdp", axis=0, tiled=True),
        lax.all_gather(conv_w, "fsdp", axis=1, tiled=True),
        lax.all_gather(conv_b, "fsdp", axis=0, tiled=True),
        lax.all_gather(gate_gain, "fsdp", axis=0, tiled=True),
        lax.all_gather(w_out, "fsdp", axis=0, tiled=True),
    )
    norm_full, w_in_full, conv_w_full, conv_b_full, gate_full, w_out_full = gathered
    inputs = tokens[0].astype(jnp.float32)
    length = inputs.shape[0]
    inner_width = HEADS * HEADDIM
    blocks = length // GROUP
    normed_f, norm_back = jax.vjp(in_norm, inputs, norm_full.astype(jnp.float32))
    normed = normed_f.astype(jnp.bfloat16)
    proj = jnp.dot(normed, w_in_full, preferred_element_type=jnp.float32).astype(jnp.bfloat16)
    gate_z = proj[:, :inner_width].astype(jnp.float32)
    conv_in = proj[:, inner_width : inner_width + CONV]
    dt_raw = proj[:, inner_width + CONV :].astype(jnp.float32)
    halo_rows = passed_along(conv_in[length - KW + 1 :], "ctx", 1)
    padded = jnp.concatenate([halo_rows, conv_in], axis=0).astype(jnp.float32)
    activated, conv_back_fn = jax.vjp(
        conv_silu, padded, conv_w_full.astype(jnp.float32), conv_b_full.astype(jnp.float32)
    )
    act_low = activated.astype(jnp.bfloat16)
    x_all = act_low[:, :inner_width].reshape(blocks, GROUP, HEADS, HEADDIM)
    b_all = act_low[:, inner_width : inner_width + STATE].reshape(blocks, GROUP, STATE)
    c_all = act_low[:, inner_width + STATE :].reshape(blocks, GROUP, STATE)
    dt_in = dt_raw + dt_bias[None, :]
    step_sizes = jax.nn.softplus(dt_in)
    a_neg = -jnp.exp(a_log)
    step_all = step_sizes.reshape(blocks, GROUP, HEADS)
    piece_log = jnp.sum(step_sizes * a_neg[None, :], axis=0)
    zero_state = jnp.zeros((HEADS, HEADDIM, STATE), jnp.float32)

    def cumulate(step_block):
        return jnp.cumsum(step_block * a_neg[None, :], axis=0)

    def state_step(state, pieces):
        x_block, b_block, step_block = pieces
        cumulative = cumulate(step_block)
        tail_vals, weighted = block_weighted(b_block, cumulative, step_block)
        local = jnp.einsum("jhp,hjn->hpn", x_block, weighted, preferred_element_type=jnp.float32)
        return (jnp.exp(cumulative[-1])[:, None, None] * state + local, None)

    end_state, unused = lax.scan(state_step, zero_state, (x_all, b_all, step_all))
    identity = (jnp.ones((HEADS,), jnp.float32), zero_state)
    prefix = carried_in((jnp.exp(piece_log), end_state), "ctx", link_states, identity, False)
    start_state = prefix[1]

    def forward_step(state, pieces):
        x_block, b_block, c_block, step_block = pieces
        cumulative = cumulate(step_block)
        gram = jnp.einsum("in,jn->ij", c_block, b_block, preferred_element_type=jnp.float32)
        scores = (gram[None] * decay_matrix(cumulative) * step_block.T[:, None, :]).astype(
            jnp.bfloat16
        )
        intra = jnp.einsum("hij,jhp->ihp", scores, x_block, preferred_element_type=jnp.float32)
        inner = jnp.einsum(
            "in,hpn->ihp", c_block, state.astype(jnp.bfloat16), preferred_element_type=jnp.float32
        )
        tail_vals, weighted = block_weighted(b_block, cumulative, step_block)
        local = jnp.einsum("jhp,hjn->hpn", x_block, weighted, preferred_element_type=jnp.float32)
        new_state = jnp.exp(cumulative[-1])[:, None, None] * state + local
        return (new_state, (intra + jnp.exp(cumulative)[:, :, None] * inner, state))

    unused_end, (block_out, block_starts) = lax.scan(
        forward_step, start_state, (x_all, b_all, c_all, step_all)
    )
    xs_float = x_all.reshape(length, HEADS, HEADDIM).astype(jnp.float32)
    ssd_out = (
        block_out.reshape(length, HEADS, HEADDIM) + d_skip[None, :, None] * xs_float
    ).reshape(length, inner_width)
    mixed_f, gate_back = jax.vjp(gate_norm, ssd_out, gate_z, gate_full.astype(jnp.float32))
    mixed = mixed_f.astype(jnp.bfloat16)
    branch = jnp.dot(mixed, w_out_full, preferred_element_type=jnp.float32)
    output = (inputs + branch).astype(jnp.bfloat16)[None]
    regathered = (
        lax.all_gather(norm_gain, "fsdp", axis=0, tiled=True),
        lax.all_gather(w_in, "fsdp", axis=0, tiled=True),
        lax.all_gather(conv_w, "fsdp", axis=1, tiled=True),
        lax.all_gather(conv_b, "fsdp", axis=0, tiled=True),
        lax.all_gather(gate_gain, "fsdp", axis=0, tiled=True),
        lax.all_gather(w_out, "fsdp", axis=0, tiled=True),
    )
    w_in_full = regathered[1]
    w_out_full = regathered[5]
    seed = cotangent[0]
    d_w_out = jnp.einsum("td,te->de", mixed, seed, preferred_element_type=jnp.float32)
    d_mixed = jnp.einsum("te,de->td", seed, w_out_full, preferred_element_type=jnp.float32)
    d_ssd_f, d_gate_z, d_gate_gain = gate_back(d_mixed)
    d_ssd = d_ssd_f.astype(jnp.bfloat16)
    d_ssd3 = d_ssd.astype(jnp.float32).reshape(length, HEADS, HEADDIM)
    d_skip_grad = jnp.sum(d_ssd3 * xs_float, axis=(0, 2))
    d_all = d_ssd.reshape(blocks, GROUP, HEADS, HEADDIM)

    def grad_state_step(carried, pieces):
        c_block, step_block, d_block = pieces
        cumulative = cumulate(step_block)
        d_inner = (d_block.astype(jnp.float32) * jnp.exp(cumulative)[:, :, None]).astype(
            jnp.bfloat16
        )
        from_out = jnp.einsum("ihp,in->hpn", d_inner, c_block, preferred_element_type=jnp.float32)
        return (jnp.exp(cumulative[-1])[:, None, None] * carried + from_out, None)

    grad_local, unused = lax.scan(
        grad_state_step, zero_state, (c_all, step_all, d_all), reverse=True
    )
    identity_back = (jnp.ones((HEADS,), jnp.float32), zero_state)
    suffix = carried_in((jnp.exp(piece_log), grad_local), "ctx", link_states, identity_back, True)
    end_grad = suffix[1]

    def grad_step(carried, pieces):
        x_block, b_block, c_block, step_block, d_block, state = pieces
        b_float = b_block.astype(jnp.float32)
        d_float = d_block.astype(jnp.float32)
        cumulative = cumulate(step_block)
        last_decay = jnp.exp(cumulative[-1])
        tail_vals, weighted = block_weighted(b_block, cumulative, step_block)
        d_state = last_decay[:, None, None] * carried
        d_last = jnp.sum(carried * state, axis=(1, 2)) * last_decay
        d_local = carried.astype(jnp.bfloat16)
        d_x = jnp.einsum("hjn,hpn->jhp", weighted, d_local, preferred_element_type=jnp.float32)
        d_weighted = jnp.einsum(
            "jhp,hpn->hjn", x_block, d_local, preferred_element_type=jnp.float32
        )
        d_b = jnp.sum(d_weighted * tail_vals.T[:, :, None], axis=0)
        d_tail = jnp.sum(d_weighted * b_float[None], axis=2).T
        d_step = d_tail * jnp.exp(cumulative[-1][None, :] - cumulative)
        tail_log = d_tail * tail_vals
        d_last = d_last + jnp.sum(tail_log, axis=0)
        d_cum = -tail_log
        growth = jnp.exp(cumulative)
        state_low = state.astype(jnp.bfloat16)
        inner = jnp.einsum("in,hpn->ihp", c_block, state_low, preferred_element_type=jnp.float32)
        d_cum = d_cum + jnp.sum(d_float * inner, axis=2) * growth
        d_inner = (d_float * growth[:, :, None]).astype(jnp.bfloat16)
        d_c = jnp.einsum("ihp,hpn->in", d_inner, state_low, preferred_element_type=jnp.float32)
        d_state = d_state + jnp.einsum(
            "ihp,in->hpn", d_inner, c_block, preferred_element_type=jnp.float32
        )
        gram = jnp.einsum("in,jn->ij", c_block, b_block, preferred_element_type=jnp.float32)
        decays = decay_matrix(cumulative)
        step_cols = step_block.T[:, None, :]
        scores = (gram[None] * decays * step_cols).astype(jnp.bfloat16)
        d_scores = jnp.einsum("ihp,jhp->hij", d_block, x_block, preferred_element_type=jnp.float32)
        d_x = d_x + jnp.einsum("hij,ihp->jhp", scores, d_block, preferred_element_type=jnp.float32)
        common = d_scores * decays
        d_gram = jnp.sum(common * step_cols, axis=0).astype(jnp.bfloat16)
        d_step = d_step + jnp.sum(common * gram[None], axis=1).T
        exponent = common * gram[None] * step_cols
        d_cum = d_cum + jnp.sum(exponent, axis=2).T - jnp.sum(exponent, axis=1).T
        d_c = d_c + jnp.einsum("ij,jn->in", d_gram, b_block, preferred_element_type=jnp.float32)
        d_b = d_b + jnp.einsum("ij,in->jn", d_gram, c_block, preferred_element_type=jnp.float32)
        last_row = lax.broadcasted_iota(jnp.int32, d_cum.shape, 0) == d_cum.shape[0] - 1
        d_cum = d_cum + jnp.where(last_row, d_last[None, :], 0.0)
        d_rate = jnp.cumsum(d_cum[::-1], axis=0)[::-1]
        return (d_state, (d_x, d_b, d_c, d_step, d_rate))

    unused_grad, block_grads = lax.scan(
        grad_step, end_grad, (x_all, b_all, c_all, step_all, d_all, block_starts), reverse=True
    )
    d_x_all, d_b_all, d_c_all, d_step_all, d_rate_all = block_grads
    d_rate_flat = d_rate_all.reshape(length, HEADS)
    d_x_flat = (d_x_all.reshape(length, HEADS, HEADDIM) + d_skip[None, :, None] * d_ssd3).reshape(
        length, inner_width
    )
    d_act = jnp.concatenate(
        [d_x_flat, d_b_all.reshape(length, STATE), d_c_all.reshape(length, STATE)], axis=1
    )
    d_padded, d_conv_w, d_conv_b = conv_back_fn(d_act)
    returned = passed_along(d_padded[: KW - 1].astype(jnp.bfloat16), "ctx", -1).astype(jnp.float32)
    d_conv_in = d_padded[KW - 1 :] + jnp.concatenate(
        [jnp.zeros((length - KW + 1, CONV), jnp.float32), returned], axis=0
    )
    d_step_total = d_step_all.reshape(length, HEADS) + d_rate_flat * a_neg[None, :]
    d_dt_in = d_step_total * jax.nn.sigmoid(dt_in)
    d_dt_bias = jnp.sum(d_dt_in, axis=0)
    d_a_log = jnp.sum(d_rate_flat * step_sizes, axis=0) * a_neg
    d_proj = jnp.concatenate([d_gate_z, d_conv_in, d_dt_in], axis=1).astype(jnp.bfloat16)
    d_w_in = jnp.einsum("td,tk->dk", normed, d_proj, preferred_element_type=jnp.float32)
    d_normed = jnp.einsum("tk,dk->td", d_proj, w_in_full, preferred_element_type=jnp.float32)
    d_inputs, d_norm_gain = norm_back(d_normed)
    grad_tokens = (seed.astype(jnp.float32) + d_inputs)[None]
    shares = (
        lax.psum_scatter(d_norm_gain, "fsdp", scatter_dimension=0, tiled=True),
        lax.psum_scatter(d_w_in, "fsdp", scatter_dimension=0, tiled=True),
        lax.psum_scatter(d_conv_w, "fsdp", scatter_dimension=1, tiled=True),
        lax.psum_scatter(d_conv_b, "fsdp", scatter_dimension=0, tiled=True),
        lax.psum_scatter(d_gate_gain, "fsdp", scatter_dimension=0, tiled=True),
        lax.psum_scatter(d_w_out, "fsdp", scatter_dimension=0, tiled=True),
    )
    summed = lax.psum((shares[0], shares[1], shares[2], shares[3], shares[4], shares[5]), "ctx")
    head_sums = lax.psum((d_dt_bias, d_a_log, d_skip_grad), ("fsdp", "ctx"))
    return (
        output,
        grad_tokens,
        summed[0],
        summed[1],
        summed[2],
        summed[3],
        head_sums[0],
        head_sums[1],
        head_sums[2],
        summed[4],
        summed[5],
    )


def solution(mesh):
    in_specs = (
        P("fsdp", "ctx", None),
        P("fsdp"),
        P("fsdp", None),
        P(None, "fsdp"),
        P("fsdp"),
        P(),
        P(),
        P(),
        P("fsdp"),
        P("fsdp", None),
        P("fsdp", "ctx", None),
    )
    out_specs = (
        P("fsdp", "ctx", None),
        P("fsdp", "ctx", None),
        P("fsdp"),
        P("fsdp", None),
        P(None, "fsdp"),
        P("fsdp"),
        P(),
        P(),
        P(),
        P("fsdp"),
        P("fsdp", None),
    )
    return jax.shard_map(body, mesh=mesh, in_specs=in_specs, out_specs=out_specs, check_vma=False)
```

profile of v0, /device:TPU:1, one launch (start us, length us, event | category | flops | bytes accessed | tf_op | source)
XLA Modules:
  0.0 3066.8 jit_solution(707199861307095639)
XLA Ops:
  8.1 18.7 all-gather.4
  26.8 65.1 %all-gather.3 = bf16[8,544,4]{1,2,0:T(4,128)(2,1)S(1)} all-gather(bf16[1,544,4]{1,2,0:T(4,128)(2,1)S(1)} %bitcast.174), channel_id=1, replica_groups=mesh['fsdp'=8,'ctx'=4] {'fsdp'}, dimensions={0}, use_global_device_ids=true | all-gather | bytes 39168 | tf_op jit(solution)/shard_map/all_gather | solution.py:83
  93.6 29.3 all-reduce.9
  123.5 553.5 %all-gather.11.cloned.1.call-done = bf16[2048,8512]{0,1:T(8,128)(2,1)} async-done(((bf16[256,8512]{0,1:T(8,128)(2,1)}), bf16[2048,8512]{0,1:T(8,128)(2,1)}) %all-gather.11.cloned.1.call-update) | async-done | bytes 34865168 | tf_op jit(solution)/shard_map/all_gather | solution.py:82
  677.1 17.2 convolution_convert_fusion
  720.0 21.4 all-gather.5
  742.3 8.6 all-reduce.10
  751.4 24.0 all-gather.15.cloned.1.call-done
  799.7 204.6 %all-gather.13.cloned.1.call-done = bf16[4096,2048]{1,0:T(8,128)(2,1)} async-done(((bf16[512,2048]{1,0:T(8,128)(2,1)}), bf16[4096,2048]{1,0:T(8,128)(2,1)}) %all-gather.13.cloned.1.call-update) | async-done | bytes 16777232 | tf_op jit(solution)/shard_map/all_gather | solution.py:86
  1004.4 20.1 multiply_reduce_fusion.10
  1025.2 9.7 fusion.12
  1042.9 17.9 fusion.48
  1061.8 12.5 multiply_reduce_fusion.2
  1089.8 10.3 all-gather.17.cloned.1.call-done
  1101.7 9.2 while.17
  1162.3 26.9 fusion.39
  1191.8 455.0 %reduce-scatter.8.cloned.1.call-done = f32[512,2048]{1,0:T(8,128)} async-done(((f32[4096,2048]{1,0:T(8,128)}), f32[512,2048]{1,0:T(8,128)}) %reduce-scatter.8.cloned.1.call-update) | async-done | bytes 4194320 | tf_op jit(solution)/shard_map/reduce_scatter | solution.py:270
  1646.8 1102.1 %reduce-scatter.6.cloned.1.call-done = f32[256,8512]{0,1:T(8,128)} async-done(((f32[2048,8512]{0,1:T(8,128)}), f32[256,8512]{0,1:T(8,128)}) %reduce-scatter.6.cloned.1.call-update) | async-done | bytes 8716304 | tf_op jit(solution)/shard_map/reduce_scatter | solution.py:266
  2751.2 12.6 fusion.27
  2763.8 39.0 %all-reduce.14 = (f32[64]{0:T(128)}, f32[64]{0:T(128)}, f32[64]{0:T(128)}) all-reduce(f32[64]{0:T(128)S(1)} %get-tuple-element.299, f32[64]{0:T(128)S(1)} %fusion.83, f32[64]{0:T(128)S(1)} %reduce_sum.298), channel_id=1, replica_groups=mesh['fsdp'=8,'ctx'=4] {'fsdp','ctx'}, use_global_device_ids=true, to_apply=%region_37.38 | all-reduce | flops 192 | bytes 1536 | tf_op jit(solution)/shard_map/psum | solution.py:273
  2802.8 17.6 fusion.30
  2820.5 29.4 all-reduce.15
  2855.1 20.7 all-reduce.16
  2875.8 174.3 %all-reduce.20.cloned.1.call-done = (f32[256,8512]{0,1:T(8,128)}, f32[512,2048]{1,0:T(8,128)}) async-done(((f32[256,8512]{0,1:T(8,128)}, f32[512,2048]{1,0:T(8,128)}), (f32[256,8512]{0,1:T(8,128)}, f32[512,2048]{1,0:T(8,128)})) %all-reduce.20.cloned.1.call-update) | async-done | bytes 12910608 | tf_op jit(solution)/shard_map/psum | solution.py:272
  (264 shorter events, 158.8 us)
Async XLA Ops:
  7.2 84.8 %copy-start.46 = (u32[32]{0:T(128)S(1)}, u32[32]{0:T(128)}, u32[]{:S(2)}) copy-start(u32[32]{0:T(128)} %constant.172) | copy-start | bytes 388
  7.2 86.1 %copy-start.48 = (bf16[544]{0:T(1024)(128)(2,1)S(1)}, bf16[544]{0:T(1024)(128)(2,1)}, u32[]{:S(2)}) copy-start(bf16[544]{0:T(1024)(128)(2,1)} %param.19) | copy-start | bytes 3268
  7.2 115.9 %copy-start.5 = (bf16[1,256,2048]{2,1,0:T(8,128)(2,1)S(1)}, bf16[1,256,2048]{2,1,0:T(8,128)(2,1)}, u32[]{:S(2)}) copy-start(bf16[1,256,2048]{2,1,0:T(8,128)(2,1)} %param.15) | copy-start | bytes 3145732
  7.2 116.2 %copy-start.58 = (f32[64]{0:T(128)S(1)}, f32[64]{0:T(128)}, u32[]{:S(2)}) copy-start(f32[64]{0:T(128)} %param.21) | copy-start | bytes 772
  7.2 669.8 %all-gather.11.cloned.1.call-start = ((), (), s32[]{:S(2)}) async-start(), calls=%async_computation.3 | async-start | bytes 39223296 | tf_op jit(solution)/shard_map/all_gather | solution.py:82
  8.0 767.4 %all-gather.15.cloned.1.call-start = ((), (), s32[]{:S(2)}) async-start(), calls=%async_computation.7 | async-start | bytes 10485760 | tf_op jit(solution)/shard_map/all_gather | solution.py:27
  26.8 650.3 %copy-start.10 = (f32[8,1,256]{2,1,0:T(1,128)}, f32[8,1,256]{2,1,0:T(1,128)S(1)}, u32[]{:S(2)}) copy-start(f32[8,1,256]{2,1,0:T(1,128)S(1)} %convert_element_type.136) | copy-start | bytes 24580
  123.1 579.9 %copy-start.21 = (f32[4352]{0:T(1024)}, f32[4352]{0:T(1024)S(1)}, u32[]{:S(2)}) copy-start(f32[4352]{0:T(1024)S(1)} %get-tuple-element.261) | copy-start | bytes 52228
  123.1 579.9 %copy-start.23 = (f32[4352]{0:T(1024)}, f32[4352]{0:T(1024)S(1)}, u32[]{:S(2)}) copy-start(f32[4352]{0:T(1024)S(1)} %get-tuple-element.262) | copy-start | bytes 52228
  123.1 579.9 %copy-start.25 = (f32[4352]{0:T(1024)}, f32[4352]{0:T(1024)S(1)}, u32[]{:S(2)}) copy-start(f32[4352]{0:T(1024)S(1)} %get-tuple-element.263) | copy-start | bytes 52228
  123.2 579.9 %copy-start.27 = (f32[4352]{0:T(1024)}, f32[4352]{0:T(1024)S(1)}, u32[]{:S(2)}) copy-start(f32[4352]{0:T(1024)S(1)} %get-tuple-element.264) | copy-start | bytes 52228
  123.5 553.6 %copy-start.40 = (f32[256]{0:T(256)}, f32[256]{0:T(256)S(1)}, u32[]{:S(2)}) copy-start(f32[256]{0:T(256)S(1)} %fusion.33) | copy-start | bytes 3076
  123.5 575.9 %copy-start.49 = (f32[64]{0:T(128)}, f32[64]{0:T(128)S(1)}, u32[]{:S(2)}) copy-start(f32[64]{0:T(128)S(1)} %exponential_negate_fusion) | copy-start | bytes 772
  123.5 553.6 %copy-start.12 = (f32[256]{0:T(256)}, f32[256]{0:T(256)S(1)}, u32[]{:S(2)}) copy-start(f32[256]{0:T(256)S(1)} %fusion.76) | copy-start | bytes 3076
  695.3 7.2 collective-permute-start
  717.9 286.5 %all-gather.13.cloned.1.call-start = ((), (), s32[]{:S(2)}) async-start(), calls=%async_computation.4 | async-start | bytes 18874368 | tf_op jit(solution)/shard_map/all_gather | solution.py:86
  718.6 381.5 %all-gather.17.cloned.1.call-start = ((), (), s32[]{:S(2)}) async-start(), calls=%async_computation.8 | async-start | bytes 10485760 | tf_op jit(solution)/shard_map/all_gather | solution.py:27
  792.7 211.7 %copy-start.8 = (bf16[1,256,2048]{2,1,0:T(8,128)(2,1)S(1)}, bf16[1,256,2048]{2,1,0:T(8,128)(2,1)}, u32[]{:S(2)}) copy-start(bf16[1,256,2048]{2,1,0:T(8,128)(2,1)} %param.25) | copy-start | bytes 3145732
  1042.6 604.2 %reduce-scatter.8.cloned.1.call-start = ((), (), s32[]{:S(2)}) async-start(), calls=%async_computation.6 | async-start | bytes 37748736 | tf_op jit(solution)/shard_map/reduce_scatter | solution.py:270
  1060.8 1688.1 %reduce-scatter.6.cloned.1.call-start = ((), (), s32[]{:S(2)}) async-start(), calls=%async_computation.5 | async-start | bytes 78446592 | tf_op jit(solution)/shard_map/reduce_scatter | solution.py:266
  1154.4 7.5 collective-permute-start.1
  1189.2 1664.8 %reduce-scatter.10.cloned.1.call-start = ((), (), s32[]{:S(2)}) async-start(), calls=%async_computation.9 | async-start | bytes 2506752
  1191.8 1858.3 %all-reduce.20.cloned.1.call-start = ((), (), s32[]{:S(2)}) async-start(), calls=%async_computation.10 | async-start | bytes 25821184 | tf_op jit(solution)/shard_map/psum | solution.py:272
  2802.8 47.3 %copy-start.41 = (f32[256]{0:T(256)S(1)}, f32[256]{0:T(256)}, u32[]{:S(2)}) copy-start(f32[256]{0:T(256)} %copy-done.40) | copy-start | bytes 3076
  (50 other events, 493.2 us)
Sparse Core Ops, SparseCore 0:
  9.5 667.4 all-gather.10
  718.0 57.3 all-gather.14
  777.5 226.7 all-gather.12
  1042.8 57.2 all-gather.16
  1103.7 543.0 reduce-scatter.7
  1650.6 1098.2 reduce-scatter.5
  2753.4 67.0 reduce-scatter.9
  2823.3 226.6 all-reduce.19
where the time goes:
time: 3080 us; the launch traced here: 3070 us
  waiting for transfers between devices  2530 us (82%)
  blocking collectives  232 us (8%)
  matrix products  164 us (5%)
  other arithmetic  68.2 us (2%)
  local copies, waits for them, and re-layouts  45.6 us (1%)
    reduce_scatter x1, waiting for transfers between devices, body(): lax.psum_scatter(d_w_in, 'fsdp', scatter_dimension=0, tiled=True)  1100 us
    all_gather x1, waiting for transfers between devices, body(): lax.all_gather(w_in, 'fsdp', axis=0, tiled=True)  554 us
    reduce_scatter x1, waiting for transfers between devices, body(): lax.psum_scatter(d_w_out, 'fsdp', scatter_dimension=0, tiled=True)  455 us
    all_gather x1, waiting for transfers between devices, body(): lax.all_gather(w_out, 'fsdp', axis=0, tiled=True)  205 us
    psum x1, waiting for transfers between devices, body(): lax.psum((shares[0], shares[1], shares[2], shares[3], shares[4], shares[5...  174 us
    unnamed x3, blocking collectives  67.3 us
    all_gather x1, blocking collectives, body(): lax.all_gather(conv_w, 'fsdp', axis=1, tiled=True)  65.1 us
  transfers between devices with their start and end apart: 10, of which 7 were waited for; matrix products, arithmetic and copies ran while one was open for 6% of the time, Pallas kernels for 0%

commit v1 on v0

v1 whole, which is shorter than its diff:
```python
import jax
import jax.numpy as jnp
import numpy as np
from jax import lax
from jax.experimental import pallas as pl
from jax.experimental.layout import Layout, with_layout_constraint
from jax.experimental.pallas import tpu as pltpu
from jax.sharding import PartitionSpec as P

D = 2048
HEADS = 64
HEADDIM = 64
STATE = 128
KW = 4
GROUP = 256
DI = HEADS * HEADDIM
CONV = DI + 2 * STATE
PAIR = 2 * HEADDIM
EPS = 1e-05
SEG = 256
HALO = 8
VMEM_LIMIT = 56 * 1024 * 1024
F32 = jnp.float32
BF16 = jnp.bfloat16


def ring_place(index, n):
    return jnp.where(index % 2 == 0, index // 2, n - 1 - index // 2)


def ring_member(place, n):
    place = place % n
    return jnp.where(place < n // 2, 2 * place, 2 * (n - 1 - place) + 1)


def ring_routes(n):
    order = [2 * p if p < n // 2 else 2 * (n - 1 - p) + 1 for p in range(n)]
    forward = [(order[p], order[(p + 1) % n]) for p in range(n)]
    return forward, [(b, a) for a, b in forward]


def send(block, route):
    return lax.ppermute(block, "fsdp", route)


def after(value, *earlier):
    return lax.optimization_barrier((value, *earlier))[0]


def halves(rows):
    upper = -(-rows // 256) * 128 if rows % 128 == 0 else rows // 2
    return upper, rows - upper


class Gather:
    def __init__(self, block, n):
        self.forward, self.backward = ring_routes(n)
        self.block, self.n = block, n
        self.latest = (block, block)
        self.ahead, self.behind = [], []

    def hop(self, *gates):
        right, left = self.latest
        last = len(self.ahead) == self.n // 2 - 1
        if last:
            upper, _ = halves(self.block.shape[0])
            right, left = right[:upper], left[upper:]
        right, left = after((right, left), *gates)
        self.latest = send(right, self.forward), send(left, self.backward)
        if not last:
            self.behind.insert(0, self.latest[0])
            self.ahead.append(self.latest[1])

    def parts(self):
        return [self.block] + self.ahead + list(self.latest) + self.behind


class Reduce:
    def __init__(self, chunk, n):
        self.forward, self.backward = ring_routes(n)
        self.chunk, self.n, self.step = chunk, n, n // 2
        first = chunk(n // 2).astype(BF16)
        self.upper, _ = halves(first.shape[0])
        self.right, self.left = first[: self.upper], first[self.upper :]

    def hop(self, *gates):
        right, left = self.right, self.left
        if gates:
            right, left = after((right, left), *gates)
        self.latest = send(right, self.forward), send(left, self.backward)
        self.step -= 1

    def join(self):
        right, left = (part.astype(F32) for part in self.latest)
        if self.step == 0:
            return self.chunk(0).astype(F32) + right + left
        own_right = self.chunk(self.step).astype(F32)
        own_left = self.chunk(self.n - self.step).astype(F32)
        cut = self.upper
        if self.step == self.n // 2 - 1:
            right = jnp.concatenate([own_right[:cut] + right, own_right[cut:]], axis=0)
            left = jnp.concatenate([own_left[:cut], own_left[cut:] + left], axis=0)
        else:
            right, left = own_right + right, own_left + left
        self.right, self.left = right.astype(BF16), left.astype(BF16)


def barrier(value, *earlier):
    return lax.optimization_barrier((value, earlier))[0]


def next_hop(rings, inputs, *earlier):
    pairs, inputs = barrier(([(ring.right, ring.left) for ring in rings], inputs), *earlier)
    for ring, (ring.right, ring.left) in zip(rings, pairs):
        ring.hop()
    return inputs


def ctx_route(m, flip):
    return [(i, i ^ flip) for i in range(m)]


def far_share(block, m):
    return lax.ppermute(block, "ctx", ctx_route(m, 2))


def near_share(block, other, m):
    near = lax.ppermute(block, "ctx", ctx_route(m, 1))
    far = lax.ppermute(other, "ctx", ctx_route(m, 1))
    return [block, near, other, far]


def ctx_share(block, m):
    return near_share(block, far_share(block, m), m)


class CtxReduce:
    def __init__(self, share, m):
        self.m, place = m, lax.axis_index("ctx")
        self.core, self.across = place % 2, place // 2
        split = share.reshape((m // 2, 2) + share.shape[1:])
        self.kept = lax.dynamic_index_in_dim(split, self.core, 1, False)
        sent = lax.dynamic_index_in_dim(split, 1 - self.core, 1, False)
        self.near = lax.ppermute(sent, "ctx", ctx_route(m, 1))

    def middle(self):
        self.both = self.kept.astype(F32) + self.near.astype(F32)
        self.sent = lax.dynamic_index_in_dim(self.both, 1 - self.across, 0, False).astype(BF16)

    def send_far(self):
        self.far = lax.ppermute(self.sent, "ctx", ctx_route(self.m, 2))

    def total(self):
        return lax.dynamic_index_in_dim(self.both, self.across, 0, False) + self.far.astype(F32)


def ctx_reduce(share, m):
    whole = CtxReduce(share, m)
    whole.middle()
    whole.send_far()
    return whole.total()


def axis_sum(values, axis, n):
    flip = 1
    while flip < n:
        values = values + lax.ppermute(values, axis, ctx_route(n, flip))
        flip *= 2
    return values


def ctx_sum(values, m):
    for flip in (1, 2):
        values = values + lax.ppermute(values, "ctx", ctx_route(m, flip))
    return values


def nt(a, b):
    return lax.dot_general(a, b, (((1,), (1,)), ((), ())), preferred_element_type=F32)


def nn(a, b):
    return lax.dot_general(a, b, (((1,), (0,)), ((), ())), preferred_element_type=F32)


def tn(a, b):
    return lax.dot_general(a, b, (((0,), (0,)), ((), ())), preferred_element_type=F32)


def lanes(shape):
    return lax.broadcasted_iota(jnp.int32, shape, len(shape) - 1)


def busy(us, megabytes):
    return pl.CostEstimate(
        flops=int(us * 1e9), transcendentals=0, bytes_accessed=int(megabytes * 1e6)
    )


def softplus(v):
    return jnp.maximum(v, 0.0) + jnp.log1p(jnp.exp(-jnp.abs(v)))


def sigmoid(v):
    return 1.0 / (1.0 + jnp.exp(-v))


def ones_where(keep):
    row = lax.broadcasted_iota(jnp.int32, (GROUP, GROUP), 0)
    col = lax.broadcasted_iota(jnp.int32, (GROUP, GROUP), 1)
    return keep(row, col)


def exact(a, b):
    return lax.dot_general(
        a, b, (((1,), (0,)), ((), ())), preferred_element_type=F32, precision=lax.Precision.HIGHEST
    )


def tiles(width):
    return [slice(at, at + PAIR) for at in range(0, width, PAIR)]


def conv_tile(extended, taps_ref, cols):
    total = taps_ref[KW : KW + 1, cols]
    for k in range(KW):
        at = HALO - KW + 1 + k
        total = total + taps_ref[k : k + 1, cols] * extended[at : at + GROUP]
    return total


def by_segments(weights):
    n = D // SEG
    places = list(range(n // 2)) + [n // 2] * 2 + list(range(n // 2 + 1, n))
    at = [0] * len(places)
    at[n // 2 + 1] = weights[n // 2].shape[0]
    return list(zip(places, at, weights))


def project_into(out_ref, normed_ref, weights, total):
    whole = None
    for o, at, w in by_segments(weights):
        part = nt(normed_ref[:, o * SEG : (o + 1) * SEG], w[...])
        if o == D // SEG // 2:
            total[:, at : at + w.shape[0]] = part
        else:
            whole = part if whole is None else whole + part
    out_ref[...] = (whole + total[...]).astype(BF16)


def front(members_ref, tokens_ref, gain_ref, *refs):
    weights, (normed_ref, proj_ref, total) = refs[:-3], refs[-3:]
    tokens = tokens_ref[...].astype(F32)
    inv = lax.rsqrt(jnp.mean(tokens * tokens, axis=-1, keepdims=True) + EPS)
    for o in range(D // SEG):
        at = pl.multiple_of(members_ref[o] * SEG, SEG)
        cols = slice(o * SEG, (o + 1) * SEG)
        part = tokens_ref[:, pl.ds(at, SEG)].astype(F32) * inv * gain_ref[:, cols]
        normed_ref[:, cols] = part.astype(BF16)
    project_into(proj_ref, normed_ref, weights, total)


def resident(array, grid_args=1):
    zeros = (0,) * array.ndim
    if grid_args == 2:
        return pl.BlockSpec(array.shape, lambda i, t: zeros, pipeline_mode=pl.Buffered(1))
    return pl.BlockSpec(array.shape, lambda i: zeros, pipeline_mode=pl.Buffered(1))


def run_front(members, tokens, gain, weights):
    length, cols = tokens.shape[0], weights[0].shape[0]
    return pl.pallas_call(
        front,
        grid_spec=pltpu.PrefetchScalarGridSpec(
            num_scalar_prefetch=1,
            grid=(length // GROUP,),
            in_specs=[
                pl.BlockSpec((GROUP, D), lambda i, t: (i, 0)),
                pl.BlockSpec((1, D), lambda i, t: (0, 0)),
            ]
            + [resident(w, 2) for w in weights],
            out_specs=[
                pl.BlockSpec((GROUP, D), lambda i, t: (i, 0)),
                pl.BlockSpec((GROUP, cols), lambda i, t: (i, 0)),
            ],
            scratch_shapes=[pltpu.VMEM((GROUP, cols), F32)],
        ),
        out_shape=[
            jax.ShapeDtypeStruct((length, D), BF16),
            jax.ShapeDtypeStruct((length, cols), BF16),
        ],
        compiler_params=pltpu.CompilerParams(vmem_limit_bytes=VMEM_LIMIT),
        cost_estimate=busy(12, 18),
        name="front",
    )(members, tokens, gain, *weights)


def project(normed_ref, *refs):
    project_into(refs[-2], normed_ref, refs[:-2], refs[-1])


def run_project(normed, weights):
    length, cols = normed.shape[0], weights[0].shape[0]
    return pl.pallas_call(
        project,
        grid=(length // GROUP,),
        in_specs=[pl.BlockSpec((GROUP, D), lambda i: (i, 0))] + [resident(w) for w in weights],
        out_specs=pl.BlockSpec((GROUP, cols), lambda i: (i, 0)),
        out_shape=jax.ShapeDtypeStruct((length, cols), BF16),
        scratch_shapes=[pltpu.VMEM((GROUP, cols), F32)],
        compiler_params=pltpu.CompilerParams(vmem_limit_bytes=VMEM_LIMIT),
        cost_estimate=busy(8, 10),
        name="project",
    )(normed, *weights)


def mix_forward(
    proj_ref, taps_ref, heads_ref, skip_ref, act_ref, table_ref, y_ref, start_ref, state, halo
):
    pairs = state.shape[0]
    heads, width = 2 * pairs, pairs * PAIR
    core = width + 2 * STATE

    @pl.when(pl.program_id(0) == 0)
    def _():
        state[...] = jnp.zeros_like(state)
        halo[...] = jnp.zeros_like(halo)

    for cols in tiles(core):
        current = proj_ref[:, cols].astype(F32)
        conv = conv_tile(jnp.concatenate([halo[:, cols], current], axis=0), taps_ref, cols)
        act_ref[:, cols] = (conv * sigmoid(conv)).astype(BF16)
        halo[:, cols] = current[GROUP - HALO :]

    raw = proj_ref[:, core : core + PAIR].astype(F32).T[:heads]
    dt = softplus(raw + heads_ref[:heads, 0:1])
    upto = ones_where(lambda row, col: row <= col).astype(F32)
    cum = exact(dt * heads_ref[heads:, 0:1], upto)
    last = cum[:, GROUP - 1 :]
    growth = jnp.exp(cum)
    rows = jnp.concatenate([cum, dt, jnp.exp(last - cum) * dt, growth], axis=0)
    table_ref[0] = rows
    cols_of = rows.T
    bs, cs = act_ref[:, width : width + STATE], act_ref[:, width + STATE : core]
    gram = nt(cs, bs)
    bias = jnp.where(ones_where(lambda row, col: row >= col), 0.0, -1e30)
    bs_t = bs.astype(F32).T
    for g, cols in enumerate(tiles(width)):
        x = act_ref[:, cols]
        first = lanes(x.shape) < HEADDIM
        start = state[g]
        start_ref[0, g] = start
        inner = nn(cs, start.astype(BF16))
        parts, locals_ = [], []
        for e in range(2):
            h = 2 * g + e
            decay = jnp.exp(cols_of[:, h : h + 1] - rows[h : h + 1, :] + bias)
            scores = (gram * decay * rows[heads + h : heads + h + 1, :]).astype(BF16)
            parts.append(nn(scores, x))
            at = 2 * heads + h
            locals_.append(nn((bs_t * rows[at : at + 1, :]).astype(BF16), x))
        at = 3 * heads + 2 * g
        grow = jnp.where(first, cols_of[:, at : at + 1], cols_of[:, at + 1 : at + 2])
        y_ref[:, cols] = (
            jnp.where(first, parts[0], parts[1]) + grow * inner + skip_ref[:, cols] * x.astype(F32)
        )
        shrink = jnp.where(
            first[:1], growth[2 * g : 2 * g + 1, GROUP - 1 :], growth[2 * g + 1 : 2 * g + 2, GROUP - 1 :]
        )
        state[g] = shrink * start + jnp.where(first[:STATE], locals_[0], locals_[1])


def run_mix_forward(proj, taps, heads_in, skip, pairs):
    length = proj.shape[0]
    blocks, width = length // GROUP, pairs * PAIR
    core = width + 2 * STATE
    whole = lambda i: (0, 0)
    return pl.pallas_call(
        mix_forward,
        grid=(blocks,),
        in_specs=[
            pl.BlockSpec((GROUP, proj.shape[1]), lambda i: (i, 0)),
            pl.BlockSpec(taps.shape, whole),
            pl.BlockSpec(heads_in.shape, whole),
            pl.BlockSpec(skip.shape, whole),
        ],
        out_specs=[
            pl.BlockSpec((GROUP, core), lambda i: (i, 0)),
            pl.BlockSpec((1, 8 * pairs, GROUP), lambda i: (i, 0, 0)),
            pl.BlockSpec((GROUP, width), lambda i: (i, 0)),
            pl.BlockSpec((1, pairs, STATE, PAIR), lambda i: (i, 0, 0, 0)),
        ],
        out_shape=[
            jax.ShapeDtypeStruct((length, core), BF16),
            jax.ShapeDtypeStruct((blocks, 8 * pairs, GROUP), F32),
            jax.ShapeDtypeStruct((length, width), F32),
            jax.ShapeDtypeStruct((blocks, pairs, STATE, PAIR), F32),
        ],
        scratch_shapes=[pltpu.VMEM((pairs, STATE, PAIR), F32), pltpu.VMEM((HALO, core), F32)],
        compiler_params=pltpu.CompilerParams(vmem_limit_bytes=VMEM_LIMIT),
        cost_estimate=busy(18, 15),
        name="mix_forward",
    )(proj, taps, heads_in, skip)


def mix_backward(
    top, act_ref, proj_ref, prev_ref, taps_ref, heads_ref, skip_ref, table_ref, start_ref, dy_ref,
    carry_in, halo_in, held_ref, dx_ref, grads_ref, dheads_ref, carried, halo, columns, ends,
):
    pairs = carried.shape[0]
    heads, width = 2 * pairs, pairs * PAIR
    core = width + 2 * STATE
    step = pl.program_id(0)

    @pl.when(step == 0)
    def _():
        carried[...] = carry_in[...]
        halo[...] = halo_in[...]
        grads_ref[...] = jnp.zeros_like(grads_ref)
        dheads_ref[...] = jnp.zeros_like(dheads_ref)

    has_prev = jnp.where(top - step > 0, 1.0, 0.0)
    rows = table_ref[0]
    cols_of = rows.T
    bs, cs = act_ref[:, width : width + STATE], act_ref[:, width + STATE : core]
    bs_float = bs.astype(F32)
    cs_t = cs.astype(F32).T.astype(BF16)
    gram = nt(bs, cs)
    bias = jnp.where(ones_where(lambda row, col: row <= col), 0.0, -1e30)

    def conv_back(d_act, cols):
        before = prev_ref[:, cols].astype(F32)[prev_ref.shape[0] - HALO :] * has_prev
        extended = jnp.concatenate([before, proj_ref[:, cols].astype(F32)], axis=0)
        conv = conv_tile(extended, taps_ref, cols)
        sig = sigmoid(conv)
        d_conv = d_act * (sig * (1.0 + conv * (1.0 - sig)))
        onward = jnp.concatenate([d_conv, halo[:, cols]], axis=0)
        d_in = taps_ref[KW - 1 : KW, cols] * d_conv
        for k in range(KW - 1):
            at = KW - 1 - k
            d_in = d_in + taps_ref[k : k + 1, cols] * onward[at : at + GROUP]
        dx_ref[:, cols] = d_in.astype(BF16)
        for k in range(KW):
            at = HALO - KW + 1 + k
            grads_ref[k : k + 1, cols] += jnp.sum(
                d_conv * extended[at : at + GROUP], axis=0, keepdims=True
            )
        grads_ref[KW : KW + 1, cols] += jnp.sum(d_conv, axis=0, keepdims=True)
        halo[:, cols] = d_conv[:HALO]

    dgram = jnp.zeros((GROUP, GROUP), F32)
    db = jnp.zeros((GROUP, STATE), F32)
    dc = jnp.zeros((GROUP, STATE), F32)
    sums_j = []
    for g, cols in enumerate(tiles(width)):
        x, dy = act_ref[:, cols], dy_ref[:, cols]
        first = lanes(x.shape) < HEADDIM
        dy_float = dy.astype(F32)
        start, grad = start_ref[0, g], carried[g]
        start_low, grad_low = start.astype(BF16), grad.astype(BF16)
        inner = nn(cs, start_low)
        at = 3 * heads + 2 * g
        grow = jnp.where(first, cols_of[:, at : at + 1], cols_of[:, at + 1 : at + 2])
        d_inner = (dy_float * grow).astype(BF16)
        dc = dc + nt(d_inner, start_low)
        touched = dy_float * inner
        held = jnp.sum(grad * start, axis=0, keepdims=True)
        zero = jnp.zeros_like(x)
        parts = []
        for e in range(2):
            h = 2 * g + e
            own = first if e == 0 else jnp.logical_not(first)
            x_own = jnp.where(own, x, zero)
            dt_col = cols_of[:, heads + h : heads + h + 1]
            tail_col = cols_of[:, 2 * heads + h : 2 * heads + h + 1]
            decay = jnp.exp(rows[h : h + 1, :] - cols_of[:, h : h + 1] + bias)
            common = nt(x_own, dy) * decay
            scores = (gram * decay * dt_col).astype(BF16)
            dgram = dgram + common * dt_col
            linked = common * gram
            columns[:, heads + h : heads + h + 1] = jnp.sum(linked, axis=1, keepdims=True)
            sums_j.append(jnp.sum(linked * dt_col, axis=0, keepdims=True))
            parts.append(nn(scores, dy) + nn((bs_float * tail_col).astype(BF16), grad_low))
            d_weighted = nt(x_own, grad_low)
            db = db + d_weighted * tail_col
            columns[:, h : h + 1] = jnp.sum(d_weighted * bs_float, axis=1, keepdims=True)
            columns[:, 2 * heads + h : 2 * heads + h + 1] = jnp.sum(
                jnp.where(own, touched, 0.0), axis=1, keepdims=True
            )
            ends[h : h + 1, :] = jnp.where(own[:1], held, 0.0)
        conv_back(jnp.where(first, parts[0], parts[1]) + skip_ref[:, cols] * dy_float, cols)
        shrink = jnp.where(
            first[:1],
            rows[at : at + 1, GROUP - 1 :],
            rows[at + 1 : at + 2, GROUP - 1 :],
        )
        carried[g] = shrink * grad + nn(cs_t, d_inner)
    low = dgram.astype(BF16)
    conv_back(db + nn(low, cs), slice(width, width + STATE))
    conv_back(dc + tn(low, bs), slice(width + STATE, core))

    turned = columns[...].T
    d_tail, sum_i, touched = (turned[k * heads : (k + 1) * heads] for k in range(3))
    cum, dt, tail, growth = (rows[k * heads : (k + 1) * heads] for k in range(4))
    a_neg = heads_ref[heads:, 0:1]
    sum_j = jnp.concatenate(sums_j, axis=0)
    tail_log = d_tail * tail
    d_last = jnp.sum(tail_log, axis=1, keepdims=True)
    d_last = d_last + jnp.sum(ends[...], axis=1, keepdims=True) * growth[:, GROUP - 1 :]
    d_cum = touched * growth - tail_log + sum_j - dt * sum_i
    d_cum = d_cum + jnp.where(lanes(d_cum.shape) == GROUP - 1, d_last, 0.0)
    d_rate = exact(d_cum, ones_where(lambda row, col: row >= col).astype(F32))
    raw = proj_ref[:, core : core + PAIR].astype(F32).T[:heads]
    d_step = d_tail * jnp.exp(cum[:, GROUP - 1 :] - cum) + sum_i
    d_dt = (d_step + d_rate * a_neg) * sigmoid(raw + heads_ref[:heads, 0:1])
    dheads_ref[:heads, :] += d_dt
    dheads_ref[heads:, :] += d_rate * dt
    filled = jnp.concatenate([d_dt, jnp.zeros((PAIR - heads, GROUP), F32)], axis=0)
    dx_ref[:, core : core + PAIR] = filled.T.astype(BF16)


def run_mix_backward(span, top, act, proj, taps, heads_in, skip, table, starts, dy, carry, halo, held):
    pairs = carry.shape[0]
    heads, width = 2 * pairs, pairs * PAIR
    core = width + 2 * STATE
    whole = lambda i: (0, 0)
    block = lambda i: (top - i, 0)
    before = GROUP // 16
    return pl.pallas_call(
        lambda *refs: mix_backward(top, *refs),
        grid=(span,),
        in_specs=[
            pl.BlockSpec((GROUP, core), block),
            pl.BlockSpec((GROUP, proj.shape[1]), block),
            pl.BlockSpec((16, proj.shape[1]), lambda i: (jnp.maximum((top - i) * before - 1, 0), 0)),
            pl.BlockSpec(taps.shape, whole),
            pl.BlockSpec(heads_in.shape, whole),
            pl.BlockSpec(skip.shape, whole),
            pl.BlockSpec((1, 8 * pairs, GROUP), lambda i: (top - i, 0, 0)),
            pl.BlockSpec((1, pairs, STATE, PAIR), lambda i: (top - i, 0, 0, 0)),
            pl.BlockSpec((GROUP, width), block),
            pl.BlockSpec(carry.shape, lambda i: (0, 0, 0)),
            pl.BlockSpec(halo.shape, whole),
            pl.BlockSpec(memory_space=pl.ANY),
        ],
        out_specs=[
            pl.BlockSpec((GROUP, proj.shape[1]), block),
            pl.BlockSpec((8, core), whole),
            pl.BlockSpec((2 * heads, GROUP), whole),
            pl.BlockSpec(carry.shape, lambda i: (0, 0, 0)),
            pl.BlockSpec(halo.shape, whole),
        ],
        out_shape=[
            jax.ShapeDtypeStruct(proj.shape, BF16),
            jax.ShapeDtypeStruct((8, core), F32),
            jax.ShapeDtypeStruct((2 * heads, GROUP), F32),
            jax.ShapeDtypeStruct(carry.shape, F32),
            jax.ShapeDtypeStruct(halo.shape, F32),
        ],
        scratch_shapes=[pltpu.VMEM((GROUP, PAIR), F32), pltpu.VMEM((heads, PAIR), F32)],
        compiler_params=pltpu.CompilerParams(vmem_limit_bytes=VMEM_LIMIT),
        input_output_aliases={} if held is None else {11: 0},
        cost_estimate=busy(12 * span, 5 * span),
        name="mix_backward",
    )(act, proj, proj, taps, heads_in, skip, table, starts, dy, carry, halo, dy if held is None else held)


def gate_sums(seed_ref, w_ref, z_ref, y_ref, gain_ref, scaled_ref, sums_ref, squares, along):
    step = pl.program_id(0)

    @pl.when(step == 0)
    def _():
        squares[...] = jnp.zeros_like(squares)
        along[...] = jnp.zeros_like(along)

    scaled = nt(seed_ref[...], w_ref[...])
    scaled_ref[...] = scaled
    z = z_ref[...].astype(F32)
    gated = y_ref[...] * (z * sigmoid(z))
    square = gated * gated
    lean = scaled * gain_ref[...] * gated
    for cols in tiles(square.shape[1]):
        squares[...] += square[:, cols]
        along[...] += lean[:, cols]

    @pl.when(step == pl.num_programs(0) - 1)
    def _():
        spot = lanes(squares.shape)
        both = jnp.where(
            spot == 0,
            jnp.sum(squares[...], axis=1, keepdims=True),
            jnp.where(spot == 1, jnp.sum(along[...], axis=1, keepdims=True), 0.0),
        )
        sums_ref[...] = both.T[:8]


def run_gate_sums(seed, w_o, z, y, gain):
    length, width = y.shape
    tile = 2 * PAIR
    col = pl.BlockSpec((length, tile), lambda i: (0, i))
    return pl.pallas_call(
        gate_sums,
        grid=(width // tile,),
        in_specs=[
            pl.BlockSpec(seed.shape, lambda i: (0, 0), pipeline_mode=pl.Buffered(1)),
            pl.BlockSpec((tile, D), lambda i: (i, 0)),
            col,
            col,
            pl.BlockSpec((1, tile), lambda i: (0, i)),
        ],
        out_specs=[col, pl.BlockSpec((8, length), lambda i: (0, 0))],
        out_shape=[
            jax.ShapeDtypeStruct(y.shape, F32),
            jax.ShapeDtypeStruct((8, length), F32),
        ],
        scratch_shapes=[pltpu.VMEM((length, PAIR), F32)] * 2,
        compiler_params=pltpu.CompilerParams(vmem_limit_bytes=VMEM_LIMIT),
        cost_estimate=busy(11, 20),
        name="gate_sums",
    )(seed, w_o, z, y, gain)


def gate_back(sums_ref, scaled_ref, z_ref, y_ref, x_ref, gain_ref, mixed_ref, dy_ref, dz_ref, cols_ref, turned):
    @pl.when(pl.program_id(0) == 0)
    def _():
        inv = lax.rsqrt(sums_ref[0:1, :] / DI + EPS)
        slope = inv * inv * inv * (sums_ref[1:2, :] / DI)
        rest = jnp.zeros((PAIR - 2, sums_ref.shape[1]), F32)
        turned[...] = jnp.concatenate([inv, slope, rest], axis=0).T

    inv, slope = turned[:, 0:1], turned[:, 1:2]
    z, y, scaled, gain = z_ref[...].astype(F32), y_ref[...], scaled_ref[...], gain_ref[...]
    sig = sigmoid(z)
    silu = z * sig
    gated = y * silu
    normal = gated * inv
    mixed_ref[...] = (normal * gain).astype(BF16)
    d_gated = scaled * gain * inv - gated * slope
    dy = (d_gated * silu).astype(BF16)
    dy_ref[...] = dy
    dz_ref[...] = (d_gated * y * (sig * (1.0 + z * (1.0 - sig)))).astype(BF16)
    cols_ref[0:1, :] = jnp.sum(scaled * normal, axis=0, keepdims=True)
    cols_ref[1:2, :] = jnp.sum(dy.astype(F32) * x_ref[...].astype(F32), axis=0, keepdims=True)
    cols_ref[2:, :] = jnp.zeros_like(cols_ref[2:, :])


def run_gate_back(sums, scaled, z, y, x, gain):
    length, width = y.shape
    tile = PAIR
    col = pl.BlockSpec((length, tile), lambda i: (0, i))
    low = jax.ShapeDtypeStruct(y.shape, BF16)
    return pl.pallas_call(
        gate_back,
        grid=(width // tile,),
        in_specs=[
            pl.BlockSpec(sums.shape, lambda i: (0, 0)),
            col,
            col,
            col,
            col,
            pl.BlockSpec((1, tile), lambda i: (0, i)),
        ],
        out_specs=[col, col, col, pl.BlockSpec((8, tile), lambda i: (0, i))],
        out_shape=[low, low, low, jax.ShapeDtypeStruct((8, width), F32)],
        scratch_shapes=[pltpu.VMEM((length, PAIR), F32)],
        compiler_params=pltpu.CompilerParams(vmem_limit_bytes=VMEM_LIMIT),
        cost_estimate=busy(11, 20),
        name="gate_back",
    )(sums, scaled, z, y, x, gain)


def back_norm(members_ref, tokens_ref, dz_ref, dx_ref, *refs):
    parts, (dn_ref, gain_ref) = refs[:-2], refs[-2:]
    count = len(parts) // 2

    @pl.when(pl.program_id(0) == 0)
    def _():
        gain_ref[...] = jnp.zeros_like(gain_ref)

    tokens = tokens_ref[...].astype(F32)
    inv = lax.rsqrt(jnp.mean(tokens * tokens, axis=-1, keepdims=True) + EPS)
    sums = [None] * (D // SEG)
    for source, weights in ((dz_ref, parts[:count]), (dx_ref, parts[count:])):
        for o, at, w in by_segments(weights):
            part = nn(source[:, at : at + w.shape[0]], w[...])
            sums[o] = part if sums[o] is None else sums[o] + part
    for o, d_normed in enumerate(sums):
        at = pl.multiple_of(members_ref[o] * SEG, SEG)
        dn_ref[:, pl.ds(at, SEG)] = d_normed.astype(BF16)
        scaled = tokens_ref[:, pl.ds(at, SEG)].astype(F32) * inv
        gain_ref[0:1, pl.ds(at, SEG)] += jnp.sum(d_normed * scaled, axis=0, keepdims=True)


def run_back_norm(members, tokens, dz, dx, weights_z, weights_x):
    length = tokens.shape[0]
    row = lambda i, t: (i, 0)
    return pl.pallas_call(
        back_norm,
        grid_spec=pltpu.PrefetchScalarGridSpec(
            num_scalar_prefetch=1,
            grid=(length // GROUP,),
            in_specs=[
                pl.BlockSpec((GROUP, D), row),
                pl.BlockSpec((GROUP, dz.shape[1]), row),
                pl.BlockSpec((GROUP, dx.shape[1]), row),
            ]
            + [resident(w, 2) for w in weights_z + weights_x],
            out_specs=[pl.BlockSpec((GROUP, D), row), pl.BlockSpec((8, D), lambda i, t: (0, 0))],
        ),
        out_shape=[
            jax.ShapeDtypeStruct((length, D), BF16),
            jax.ShapeDtypeStruct((8, D), F32),
        ],
        compiler_params=pltpu.CompilerParams(vmem_limit_bytes=VMEM_LIMIT),
        cost_estimate=busy(18, 24),
        name="back_norm",
    )(members, tokens, dz, dx, *weights_z, *weights_x)


def put_pairs(place_ref, refs, out_ref, g):
    m = len(refs)
    for k, ref in enumerate(refs):
        to = pl.multiple_of((place_ref[0] ^ k) * PAIR, PAIR)
        out_ref[pl.ds(to, PAIR), :] = ref[pl.ds(pl.multiple_of(g * PAIR, PAIR), PAIR), :].astype(F32)


def assemble_z(place_ref, z0, z1, z2, z3, out_ref):
    put_pairs(place_ref, (z0, z1, z2, z3), out_ref, pl.program_id(0))


def assemble_x(place_ref, order_ref, held_ref, a0, a1, a2, a3, b0, b1, b2, b3, out_ref):
    step, last = pl.program_id(0), pl.num_programs(0) - 1
    early, late = (a0, a1, a2, a3), (b0, b1, b2, b3)
    cut = a0.shape[0] // PAIR
    width = last * PAIR - a0.shape[0]
    core = width + 2 * STATE

    @pl.when(step < cut)
    def _():
        put_pairs(place_ref, early, out_ref, step)

    @pl.when((step >= cut) & (step < last))
    def _():
        put_pairs(place_ref, late, out_ref, step - cut)

    @pl.when(step == last)
    def _():
        total = jnp.zeros((2 * STATE, out_ref.shape[1]), F32)
        steps = jnp.zeros((HEADS, out_ref.shape[1]), F32)
        for k, x in enumerate(late):
            total = total + x[width:core].astype(F32)
            steps = steps + nn(order_ref[place_ref[0] ^ k], x[core : core + PAIR])
        out_ref[: 2 * STATE] = total
        out_ref[2 * STATE : 2 * STATE + HEADS] = steps


def run_assemble_z(place, shares, columns):
    m, rows = len(shares), shares[0].shape[1]
    tile = m * PAIR
    return pl.pallas_call(
        assemble_z,
        grid_spec=pltpu.PrefetchScalarGridSpec(
            num_scalar_prefetch=1,
            grid=(DI // tile,),
            in_specs=[resident(s, 2) for s in shares],
            out_specs=pl.BlockSpec((tile, rows), lambda i, t: (i, 0)),
        ),
        out_shape=jax.ShapeDtypeStruct((columns, rows), F32),
        compiler_params=pltpu.CompilerParams(vmem_limit_bytes=VMEM_LIMIT),
        cost_estimate=busy(4, 6),
        name="assemble_z",
    )(place, *shares)


def run_assemble_x(place, order, held, shares_a, shares_b):
    m, rows = len(shares_a), shares_a[0].shape[1]
    tile = m * PAIR
    steps = DI // tile
    return pl.pallas_call(
        assemble_x,
        grid_spec=pltpu.PrefetchScalarGridSpec(
            num_scalar_prefetch=1,
            grid=(steps + 1,),
            in_specs=[resident(order, 2), pl.BlockSpec(memory_space=pl.ANY)]
            + [resident(s, 2) for s in shares_a + shares_b],
            out_specs=pl.BlockSpec((tile, rows), lambda i, t: (i + steps, 0)),
        ),
        out_shape=jax.ShapeDtypeStruct(held.shape, F32),
        input_output_aliases={2: 0},
        compiler_params=pltpu.CompilerParams(vmem_limit_bytes=VMEM_LIMIT),
        cost_estimate=busy(5, 6),
        name="assemble_x",
    )(place, order, held, *shares_a, *shares_b)


def body(
    tokens, norm_gain, w_in, conv_w, conv_b, dt_bias, a_log, d_skip, gate_gain, w_out, cotangent
):
    n, m = lax.axis_size("fsdp"), lax.axis_size("ctx")
    place = lax.axis_index("ctx")
    piece = tokens.shape[1]
    length = piece * m
    blocks = length // GROUP
    pairs = DI // PAIR // m
    width = pairs * PAIR
    heads = 2 * pairs
    rows = w_in.shape[0]
    core_cols = width + 2 * STATE
    head_cols = core_cols + heads
    ring = rows == SEG and (DI // PAIR) // n == m

    def of_pairs(array, axis):
        shape = array.shape
        each = shape[axis] // (pairs * m)
        split = array.reshape(shape[:axis] + (pairs, m, each) + shape[axis + 1 :])
        mine = lax.dynamic_index_in_dim(split, place, axis + 1, False)
        return mine.reshape(shape[:axis] + (pairs * each,) + shape[axis + 1 :])

    all_tokens = lax.all_gather(tokens[0], "ctx", axis=0, tiled=True)
    seed = lax.all_gather(cotangent[0], "ctx", axis=0, tiled=True)

    dt_bias_own, a_log_own, skip_own = (of_pairs(v, 0) for v in (dt_bias, a_log, d_skip))
    a_neg = -jnp.exp(a_log_own)
    heads_in = jnp.broadcast_to(jnp.concatenate([dt_bias_own, a_neg])[:, None], (2 * heads, 128))
    skip_row = jnp.repeat(skip_own, HEADDIM)[None, :]

    columns = w_in.T
    small = jnp.concatenate([norm_gain, gate_gain, conv_b, conv_w.reshape(-1)])
    small_rows = -(-small.shape[0] // rows)
    small = jnp.pad(small, (0, small_rows * rows - small.shape[0])).reshape(small_rows, rows)
    total_cols = core_cols + PAIR
    spare = total_cols - head_cols - small_rows
    block_x = jnp.concatenate(
        [
            of_pairs(columns[DI : 2 * DI], 0),
            columns[2 * DI : 2 * DI + 2 * STATE],
            of_pairs(columns[DI + CONV :], 0),
            small,
            jnp.zeros((spare, rows), BF16),
        ],
        axis=0,
    )
    block_z = of_pairs(columns[:DI], 0)
    if ring:
        me = ring_place(lax.axis_index("fsdp"), n)
        members = ring_member(me + jnp.arange(n), n)
        offsets = (ring_place(jnp.arange(n), n) - me) % n
        block_o = lax.dynamic_slice_in_dim(w_out, place * PAIR, PAIR, 0)
        ring_x, ring_z, ring_o = Gather(block_x, n), Gather(block_z, n), Gather(block_o, n)
        ring_x.hop(heads_in, skip_row)
        for _ in range(n // 2 - 3):
            ring_x.hop()
        ring_z.hop(*ring_x.latest)
        ring_x.hop()
        ring_x.hop()
        ring_z.hop(*ring_x.latest)
        ring_o.hop(*ring_x.latest)
        parts_x = ring_x.parts()
        far_tail = parts_x[n // 2 + 1]
        tails = [p[p.shape[0] - PAIR :] for p in parts_x[: n // 2] + [far_tail] + parts_x[n // 2 + 2 :]]
        tails = jnp.stack(tails)
        tails_ring, tails = tails, tails[offsets]
    else:
        members = jnp.arange(D // SEG)

        def split(whole):
            upper, _ = halves(whole.shape[0])
            parts = [whole[:, o * SEG : (o + 1) * SEG] for o in range(D // SEG)]
            middle = parts[len(parts) // 2]
            return parts[: len(parts) // 2] + [middle[:upper], middle[upper:]] + parts[len(parts) // 2 + 1 :]

        whole_x = lax.all_gather(block_x, "fsdp", axis=1, tiled=True)
        parts_x, parts_z = split(whole_x), split(lax.all_gather(block_z, "fsdp", axis=1, tiled=True))
        w_o = of_pairs(lax.all_gather(w_out, "fsdp", axis=0, tiled=True), 0)
        tails = whole_x[core_cols:].reshape(PAIR, n, rows).transpose(1, 0, 2)
        tails_ring = tails
    members = members.astype(jnp.int32)

    def flatten(tails):
        return tails[:, heads : heads + small_rows].reshape(n, small_rows * rows)

    flat = flatten(tails)
    sizes = (norm_gain.shape[0], gate_gain.shape[0], conv_b.shape[0], KW * conv_w.shape[1])
    cuts = [0]
    for size in sizes:
        cuts.append(cuts[-1] + size)
    norm_ring = flatten(tails_ring)[:, cuts[0] : cuts[1]].reshape(1, D).astype(F32)
    norm_full = flat[:, cuts[0] : cuts[1]].reshape(1, D).astype(F32)
    gate_full = of_pairs(flat[:, cuts[1] : cuts[2]].reshape(1, DI), 1).astype(F32)
    bias_full = flat[:, cuts[2] : cuts[3]].reshape(1, CONV)
    taps_full = flat[:, cuts[3] : cuts[4]].reshape(n, KW, -1).transpose(1, 0, 2).reshape(KW, CONV)
    taps_full = jnp.concatenate([taps_full, bias_full], axis=0)
    taps = jnp.concatenate([of_pairs(taps_full[:, :DI], 1), taps_full[:, DI:]], axis=1)
    taps = jnp.pad(taps.astype(F32), ((0, 8 - KW - 1), (0, 0)))

    normed, proj_x = run_front(members, all_tokens, norm_ring, parts_x)
    if ring:
        ring_z.hop(proj_x)
        ring_o.hop(proj_x)
    act, table, ssd, starts = run_mix_forward(proj_x, taps, heads_in, skip_row, pairs)
    if ring:
        for _ in range(n // 2 - 2):
            ring_o.hop(ssd)
        for _ in range(n // 2 - 3):
            ring_z.hop(ssd)
        parts_z = ring_z.parts()
        w_o = jnp.zeros((n, PAIR, D), BF16)
        where = [members[o] for o in range(n // 2)] + [members[n // 2]] * 2
        where += [members[o] for o in range(n // 2 + 1, n)]
        for at, part in enumerate(ring_o.parts()):
            row = halves(PAIR)[0] if at == n // 2 + 1 else 0
            w_o = lax.dynamic_update_slice(w_o, part[None], (where[at], row, 0))
        w_o = w_o.reshape(width, D)
    proj_z = run_project(normed, parts_z)

    scaled, sums = run_gate_sums(seed, w_o, proj_z, ssd, gate_full)
    sums = ctx_sum(sums, m)
    mixed, dy, d_z, gate_cols = run_gate_back(sums, scaled, proj_z, ssd, act, gate_full)
    d_gate_gain = gate_cols[0]
    d_skip_own = jnp.sum(gate_cols[1].reshape(heads, HEADDIM), axis=1)

    grads_o = tn(mixed, seed).astype(BF16)
    grads_z = tn(d_z, normed).astype(BF16)
    carry = jnp.zeros((pairs, STATE, PAIR), F32)
    halo = jnp.zeros((HALO, core_cols), F32)
    conv_grads, head_grads, top, d_x = 0.0, 0.0, blocks - 1, None
    if ring:
        sum_o = Reduce(lambda o: lax.dynamic_slice_in_dim(grads_o, members[o] * PAIR, PAIR, 0), n)
        sum_z = Reduce(lambda o: grads_z[:, o * SEG : (o + 1) * SEG], n)
        sum_o.hop()
        sum_z.hop()
    for at, span in enumerate((1, 2, 1)):
        if ring and at > 0:
            sum_o.join()
            if at == 1:
                sum_z.join()
            dy, carry = next_hop([sum_o, sum_z] if at == 1 else [sum_o], (dy, carry))
        d_x, conv_part, head_part, carry, halo = run_mix_backward(
            span, top, act, proj_x, taps, heads_in, skip_row, table, starts, dy, carry, halo, d_x
        )
        conv_grads, head_grads = conv_grads + conv_part, head_grads + head_part
        top -= span
    if ring:
        sum_o.join()
        sum_z.join()
        d_x, normed_late = next_hop([sum_z], (d_x, normed), sum_o.right, sum_o.left)
    else:
        normed_late = normed
    head_sums = jnp.sum(head_grads, axis=1)
    d_dt_bias, d_a_log = head_sums[:heads], head_sums[heads:] * a_neg
    grads_x = tn(d_x, normed_late).astype(BF16)

    def spread_pairs(mine):
        shape = mine.shape[:-1]
        whole = jnp.zeros(shape + (pairs, m, mine.shape[-1] // pairs), F32)
        whole = lax.dynamic_update_index_in_dim(
            whole, mine.reshape(shape + (pairs, -1)), place, len(shape) + 1
        )
        return whole.reshape(shape + (-1,))

    d_conv = jnp.concatenate(
        [spread_pairs(conv_grads[: KW + 1, :width]), conv_grads[: KW + 1, width:]], axis=1
    )
    by_member = d_conv.reshape(KW + 1, n, -1)
    small_grads = jnp.concatenate(
        [
            jnp.zeros((n, rows), F32),
            spread_pairs(d_gate_gain).reshape(n, -1),
            by_member[KW],
            by_member[:KW].transpose(1, 0, 2).reshape(n, -1),
        ],
        axis=1,
    )
    small_grads = jnp.pad(small_grads, ((0, 0), (0, small_rows * rows - small_grads.shape[1])))
    per_head = jnp.concatenate([d_dt_bias, d_a_log, d_skip_own])
    per_head = jnp.pad(per_head, (0, rows - per_head.shape[0]))
    small_grads = jnp.concatenate(
        [small_grads.reshape(n, small_rows, rows), jnp.broadcast_to(per_head, (n, 1, rows))], axis=1
    )

    def with_small(chunk, extra):
        return chunk.astype(F32) + jnp.pad(extra, ((chunk.shape[0] - PAIR + heads, spare - 1), (0, 0)))

    mixed_late, d_x_late = mixed, d_x
    if ring:
        small_ring = small_grads[members]
        cut = halves(total_cols)[0]
        sum_a = Reduce(lambda o: grads_x[:cut, o * SEG : (o + 1) * SEG], n)
        sum_b = Reduce(
            lambda o: with_small(grads_x[cut:, o * SEG : (o + 1) * SEG], small_ring[o]), n
        )
        sum_z.join()
        d_x_late = next_hop([sum_a, sum_b, sum_o], d_x, sum_z.right, sum_z.left)
    d_normed, d_gain = run_back_norm(members, all_tokens, d_z, d_x_late, parts_z, parts_x)
    if ring:
        sum_a.join()
        sum_b.join()
        part_o = sum_o.join().astype(BF16)
        d_normed, d_gain, mixed_late, part_o = next_hop(
            [sum_a, sum_b], (d_normed, d_gain, mixed, part_o), sum_z.right, sum_z.left
        )
    d_own = CtxReduce(d_normed.reshape(m, piece, D), m)
    d_own.middle()
    d_own.send_far()
    gain_sum = axis_sum(d_gain[0:1], "ctx", m)
    branch = nn(mixed_late, w_o).astype(BF16)
    if ring:
        sum_a.join()
        sum_b.join()
        branch, d_own.far, gain_sum, part_o = next_hop(
            [sum_a, sum_b, sum_z], (branch, d_own.far, gain_sum, part_o)
        )
    branch_own = CtxReduce(branch.reshape(m, piece, D), m)
    branch_own.middle()
    branch_own.send_far()
    gain_sum = axis_sum(gain_sum, "fsdp", n)
    own = tokens[0].astype(F32)
    inv = lax.rsqrt(jnp.mean(own * own, axis=-1, keepdims=True) + EPS)
    d_direct = d_own.total() * norm_full
    along = jnp.mean(d_direct * own, axis=-1, keepdims=True)
    grad_tokens = (cotangent[0].astype(F32) + d_direct * inv - own * (inv * inv * inv * along))[None]
    if ring:
        part_z = sum_z.join().astype(BF16)
        for at in range(n // 2 - 3):
            sum_a.join()
            sum_b.join()
            branch_own.far, gain_sum, part_o, part_z = next_hop(
                [sum_a, sum_b], (branch_own.far, gain_sum, part_o, part_z), grad_tokens
            )
        other_o, other_z = far_share(part_o, m), far_share(part_z, m)
    output = (tokens[0].astype(F32) + branch_own.total()).astype(BF16)[None]
    grad_gain = lax.dynamic_slice_in_dim(gain_sum[0], lax.axis_index("fsdp") * rows, rows, 0)
    place_ref = place.reshape(1).astype(jnp.int32)
    if ring:
        part_a, part_b = sum_a.join().astype(BF16), sum_b.join().astype(BF16)
        part_a, part_b, other_o, other_z = barrier(
            (part_a, part_b, other_o, other_z), output, grad_gain
        )
        other_a, other_b = far_share(part_a, m), far_share(part_b, m)
        shares_o, shares_z = near_share(part_o, other_o, m), near_share(part_z, other_z, m)
        held = run_assemble_z(place_ref, shares_z, w_in.shape[1])
        grad_w_out = jnp.zeros((m, PAIR, D), F32)
        for k in range(m):
            grad_w_out = lax.dynamic_update_slice(
                grad_w_out, shares_o[k].astype(F32)[None], (place ^ k, 0, 0)
            )
        grad_w_out = grad_w_out.reshape(w_out.shape)
        part_a, part_b, other_a, other_b, held, grad_w_out = barrier(
            (part_a, part_b, other_a, other_b, held, grad_w_out)
        )
        shares_x = [near_share(part_a, other_a, m), near_share(part_b, other_b, m)]
    else:
        part_z = lax.psum_scatter(grads_z.astype(F32), "fsdp", scatter_dimension=1, tiled=True)
        extra = small_grads.transpose(1, 0, 2).reshape(small_rows + 1, D)
        part_x = lax.psum_scatter(with_small(grads_x, extra), "fsdp", scatter_dimension=1, tiled=True)
        whole_o = jnp.zeros((pairs, m, PAIR, D), F32)
        whole_o = lax.dynamic_update_index_in_dim(
            whole_o, grads_o.astype(F32).reshape(pairs, PAIR, D), place, 1
        )
        grad_w_out = lax.psum_scatter(whole_o.reshape(DI, D), "fsdp", scatter_dimension=0, tiled=True)
        grad_w_out = lax.psum(grad_w_out, "ctx")
        held = run_assemble_z(place_ref, ctx_share(part_z.astype(BF16), m), w_in.shape[1])
        cut = halves(total_cols)[0]
        shares_x = [ctx_share(part.astype(BF16), m) for part in (part_x[:cut], part_x[cut:])]

    order = np.zeros((m, HEADS, PAIR), np.float32)
    for member in range(m):
        for h in range(heads):
            order[member, (h // 2) * 2 * m + 2 * member + h % 2, h] = 1.0
    grad_w_in = run_assemble_x(place_ref, jnp.asarray(order, BF16), held, *shares_x).T
    first = head_cols - cut
    tail = jnp.stack([share[first : first + small_rows + 1] for share in shares_x[1]]).astype(F32)
    summed = jnp.sum(tail[:, :small_rows], axis=0).reshape(-1)
    ends = tail[:, small_rows, : 3 * heads]
    per_head = jnp.zeros((m, 3 * heads), F32)
    for k in range(m):
        per_head = lax.dynamic_update_slice(per_head, ends[k : k + 1], (place ^ k, 0))
    per_head = per_head.reshape(m, 3, pairs, 2).transpose(1, 2, 0, 3).reshape(3, HEADS)
    return (
        output,
        grad_tokens,
        grad_gain,
        grad_w_in,
        summed[cuts[3] : cuts[4]].reshape(KW, -1),
        summed[cuts[2] : cuts[3]],
        per_head[0],
        per_head[1],
        per_head[2],
        summed[cuts[1] : cuts[2]],
        grad_w_out,
    )


def solution(mesh):
    in_specs = (
        P("fsdp", "ctx", None),
        P("fsdp"),
        P("fsdp", None),
        P(None, "fsdp"),
        P("fsdp"),
        P(),
        P(),
        P(),
        P("fsdp"),
        P("fsdp", None),
        P("fsdp", "ctx", None),
    )
    out_specs = (
        P("fsdp", "ctx", None),
        P("fsdp", "ctx", None),
        P("fsdp"),
        P("fsdp", None),
        P(None, "fsdp"),
        P("fsdp"),
        P(),
        P(),
        P(),
        P("fsdp"),
        P("fsdp", None),
    )
    return jax.shard_map(body, mesh=mesh, in_specs=in_specs, out_specs=out_specs, check_vma=False)
```

time: 3080 us -> 545 us (0.18)
  waiting for transfers between devices: 2530 us -> 141 us
  blocking collectives: 232 us -> 0 us
  Pallas kernels: 0 us -> 142 us
  matrix products: 164 us -> 26.9 us
  starting transfers between devices: 11.2 us -> 82.8 us
    reduce_scatter x2 -> x0, waiting for transfers between devices: 1560 us -> none  [the longest x1 1100 us: body(): lax.psum_scatter(d_w_in, 'fsdp', scatter_dimension=0, tiled=True)]
    all_gather x4 -> x2, waiting for transfers between devices: 792 us -> 0.01 us  [the longest x1 0.01 us: body(): all_tokens = lax.all_gather(tokens[0], 'ctx', axis=0, tiled=True)]
    psum x1 -> x0, waiting for transfers between devices: 174 us -> none  [body(): lax.psum((shares[0], shares[1], shares[2], shares[3], shares[4], shares[5...]
    pallas_call x0 -> x11, Pallas kernels: none -> 142 us  [the longest x3 49.3 us: run_mix_backward(): pl.pallas_call(lambda *refs: mix_backward(top, *refs), grid=(span,), in_s...]
    ppermute x2 -> x77, waiting for transfers between devices: 0.01 us -> 141 us  [the longest x54 81.1 us: send(): return lax.ppermute(block, 'fsdp', route)]
    dot_general x18 -> x4, matrix products: 164 us -> 26.9 us  [the longest x3 20 us: tn(): lax.dot_general(a, b, (((0,), (0,)), ((), ())), preferred_element_type=F32)]
    all_gather x3 -> x0, blocking collectives: 105 us -> none  [the longest x1 65.1 us: body(): lax.all_gather(conv_w, 'fsdp', axis=1, tiled=True)]
    ppermute x2 -> x77, starting transfers between devices: 10.4 us -> 82.7 us  [the longest x54 44.8 us: send(): return lax.ppermute(block, 'fsdp', route)]
  transfers between devices with their start and end apart: 10 -> 79, of which waited for: 7 -> 29; matrix products, arithmetic and copies ran while one was open for 6% -> 20% of each run, Pallas kernels for 0% -> 21%
where the time goes in v1:
time: 545 us; the launch traced here: 535 us
  Pallas kernels  142 us (26%)
  waiting for transfers between devices  141 us (26%)
  starting transfers between devices  82.8 us (15%)
  local copies, waits for them, and re-layouts  57.7 us (11%)
  other arithmetic  48.2 us (9%)
  between operations  36.2 us (7%)
  matrix products  26.9 us (5%)
    ppermute x54, waiting for transfers between devices, send(): return lax.ppermute(block, 'fsdp', route)  81.1 us
    pallas_call x3, Pallas kernels, run_mix_backward(): pl.pallas_call(lambda *refs: mix_backward(top, *refs), grid=(span,), in_s...  49.3 us
    ppermute x54, starting transfers between devices, send(): return lax.ppermute(block, 'fsdp', route)  44.8 us
    ppermute x4, waiting for transfers between devices, far_share(): return lax.ppermute(block, 'ctx', ctx_route(m, 2))  21.3 us
    dot_general x3, matrix products, tn(): lax.dot_general(a, b, (((0,), (0,)), ((), ())), preferred_element_type=F32)  20 us
    pallas_call x1, Pallas kernels, run_back_norm(): pl.pallas_call(back_norm, grid_spec=pltpu.PrefetchScalarGridSpec(num_scal...  18.4 us
    pallas_call x1, Pallas kernels, run_mix_forward(): pl.pallas_call(mix_forward, grid=(blocks,), in_specs=[pl.BlockSpec((GROUP...  18 us
    ppermute x2, waiting for transfers between devices, send_far(): self.far = lax.ppermute(self.sent, 'ctx', ctx_route(self.m, 2))  18 us
  transfers between devices with their start and end apart: 79, of which 29 were waited for; matrix products, arithmetic and copies ran while one was open for 20% of the time, Pallas kernels for 21%

profile of v1, /device:TPU:1, one launch (start us, length us, event | category | flops | bytes accessed | tf_op | source)
XLA Modules:
  0.0 534.7 jit_solution(2339580046402765300)
XLA Ops:
  22.3 15.8 %collective-permute-done.refs_8_.refs_17_ = bf16[1408,256]{1,0:T(8,128)(2,1)} collective-permute-done((bf16[1408,256]{1,0:T(8,128)(2,1)S(1)}, bf16[1408,256]{1,0:T(8,128)(2,1)}, u32[]{:S(2)}, u32[]{:S(2)}) %collective-permute-start) | collective-permute-done | bytes 720928 | tf_op jit(solution)/shard_map/ppermute | solution.py:43
  41.2 13.7 %collective-permute-done.2.refs_7_.refs_16_ = bf16[1408,256]{1,0:T(8,128)(2,1)} collective-permute-done((bf16[1408,256]{1,0:T(8,128)(2,1)}, bf16[1408,256]{1,0:T(8,128)(2,1)}, u32[]{:S(2)}, u32[]{:S(2)}) %collective-permute-start.2) | collective-permute-done | bytes 720928 | tf_op jit(solution)/shard_map/ppermute | solution.py:43
  85.7 10.3 %collective-permute-done.7.refs_5_.refs_14_ = bf16[640,256]{1,0:T(8,128)(2,1)S(1)} collective-permute-done((bf16[640,256]{1,0:T(8,128)(2,1)S(1)}, bf16[640,256]{1,0:T(8,128)(2,1)S(1)}, u32[]{:S(2)}, u32[]{:S(2)}) %collective-permute-start.7) | collective-permute-done | bytes 327712 | tf_op jit(solution)/shard_map/ppermute | solution.py:43
  105.4 12.8 %front.1 = (bf16[1024,2048]{1,0:T(8,128)(2,1)}, bf16[1024,1408]{1,0:T(8,128)(2,1)}) custom-call(s32[8]{0:T(128)} %copy-done.37, bf16[1024,2048]{1,0:T(8,128)(2,1)} %bitcast.256, f32[1,2048]{1,0:T(1,128)} %bitcast.251, bf16[1408,256]{1,0:T(8,128)(2,1)} %copy-done.13, bf16[1408,256]{1,0:T(8,128)(2,1)} %collective-permute-done.1.refs_1_.refs_10_, ...), custom_call_target="tpu_custom_call" | custom-call | flops 12000000000 | bytes 18000000 | tf_op jit(solution)/shard_map/front/pallas_call | solution.py:272
  124.3 18.0 %mix_forward.1 = (bf16[1024,1280]{1,0:T(8,128)(2,1)}, f32[4,64,256]{2,1,0:T(8,128)}, f32[1024,1024]{1,0:T(8,128)}, f32[4,8,128,128]{3,2,1,0:T(8,128)}) custom-call(bf16[1024,1408]{1,0:T(8,128)(2,1)} %get-tuple-element.128.proj_ref.refs_1_.refs_2_, f32[8,1280]{1,0:T(8,128)} %pad_convert_fusion.taps_ref.refs_3_, ...), custom_call_target="tpu_custom_call" | custom-call | flops 17999998976 | bytes 15000000 | tf_op jit(solution)/shard_map/mix_forward/pallas_call | solution.py:378
  161.3 8.6 %project.1.z_ref = bf16[1024,1024]{1,0:T(8,128)(2,1)} custom-call(bf16[1024,2048]{1,0:T(8,128)(2,1)} %get-tuple-element.170.normed_ref, bf16[1024,256]{1,0:T(8,128)(2,1)} %bitcast.34.refs_0_, bf16[1024,256]{1,0:T(8,128)(2,1)} %collective-permute-done.15.refs_1_, bf16[1024,256]{1,0:T(8,128)(2,1)} %copy-done.40, bf16[1024,256]{1,0:T(8,128)(2,1)} %copy-done.27, ...), custom_call_target="tpu_custom_call" | custom-call | flops 8000000000 | bytes 10000000 | tf_op jit(solution)/shard_map/project/pallas_call | solution.py:304
  175.1 11.8 %gate_sums.1 = (f32[1024,1024]{1,0:T(8,128)}, f32[8,1024]{1,0:T(8,128)}) custom-call(bf16[1024,2048]{1,0:T(8,128)(2,1)} %bitcast.258, bf16[1024,2048]{1,0:T(8,128)(2,1)} %bitcast.32.w_ref, bf16[1024,1024]{1,0:T(8,128)(2,1)} %project.1.z_ref, f32[1024,1024]{1,0:T(8,128)} %get-tuple-element.131.y_ref, f32[1,1024]{1,0:T(1,128)} %bitcast.252), custom_call_target="tpu_custom_call" | custom-call | flops 11000000512 | bytes 20000000 | tf_op jit(solution)/shard_map/gate_sums/pallas_call | solution.py:601
  186.9 11.7 %collective-permute-start.23 = (f32[8,1024]{1,0:T(8,128)}, f32[8,1024]{1,0:T(8,128)S(1)}, u32[]{:S(2)}, u32[]{:S(2)}) collective-permute-start(f32[8,1024]{1,0:T(8,128)} %get-tuple-element.144), channel_id=1, source_target_pairs={{0,1},{1,0},{2,3},{3,2},{4,5},{5,4},{6,7},{7,6},{8,9},{9,8},{10,11... | collective-permute-start | bytes 98312 | tf_op jit(solution)/shard_map/ppermute | solution.py:174
  207.4 11.5 %gate_back.1 = (bf16[1024,1024]{1,0:T(8,128)(2,1)}, bf16[1024,1024]{1,0:T(8,128)(2,1)}, bf16[1024,1024]{1,0:T(8,128)(2,1)}, f32[8,1024]{1,0:T(8,128)}) custom-call(f32[8,1024]{1,0:T(8,128)} %add.437.sums_ref, f32[1024,1024]{1,0:T(8,128)} %get-tuple-element.145.scaled_ref, bf16[1024,1024]{1,0:T(8,128)(2,1)} %project.1.z_ref, ...), custom_call_target="tpu_custom_call" | custom-call | flops 11000000512 | bytes 20000000 | tf_op jit(solution)/shard_map/gate_back/pallas_call | solution.py:652
  218.9 6.6 %convolution_convert_fusion.3 = bf16[1024,2048]{1,0:T(8,128)(2,1)S(1)} fusion(bf16[1024,1024]{1,0:T(8,128)(2,1)} %get-tuple-element.147.dz_ref, bf16[1024,2048]{1,0:T(8,128)(2,1)S(1)} %copy-done.47), kind=kOutput, calls=%fused_computation.7 | convolution fusion | flops 4297064448 | bytes 10485760 | tf_op jit(solution)/shard_map/dot_general | solution.py:187
  237.2 12.9 %mix_backward.3 = (bf16[1024,1408]{1,0:T(8,128)(2,1)}, f32[8,1280]{1,0:T(8,128)}, f32[32,256]{1,0:T(8,128)}, f32[8,128,128]{2,1,0:T(8,128)}, f32[8,1280]{1,0:T(8,128)}) custom-call(bf16[1024,1280]{1,0:T(8,128)(2,1)} %get-tuple-element.146.x_ref.refs_0_, bf16[1024,1408]{1,0:T(8,128)(2,1)} %get-tuple-element.128.proj_ref.refs_1_.refs_2_, ...), custom_call_target="tpu_custom_call" | custom-call | flops 12000000000 | bytes 5000000 | tf_op jit(solution)/shard_map/mix_backward/pallas_call | solution.py:529
  257.0 23.5 %mix_backward.4 = (bf16[1024,1408]{1,0:T(8,128)(2,1)}, f32[8,1280]{1,0:T(8,128)}, f32[32,256]{1,0:T(8,128)}, f32[8,128,128]{2,1,0:T(8,128)}, f32[8,1280]{1,0:T(8,128)}) custom-call(bf16[1024,1280]{1,0:T(8,128)(2,1)} %get-tuple-element.146.x_ref.refs_0_, ...), custom_call_target="tpu_custom_call", output_to_operand_aliasing={{0}: (11, {})} | custom-call | flops 24000000000 | bytes 10000000 | tf_op jit(solution)/shard_map/mix_backward/pallas_call | solution.py:529
  282.9 12.9 %mix_backward.5 = (bf16[1024,1408]{1,0:T(8,128)(2,1)}, f32[8,1280]{1,0:T(8,128)}, f32[32,256]{1,0:T(8,128)}, f32[8,128,128]{2,1,0:T(8,128)}, f32[8,1280]{1,0:T(8,128)}) custom-call(bf16[1024,1280]{1,0:T(8,128)(2,1)} %get-tuple-element.146.x_ref.refs_0_, ...), custom_call_target="tpu_custom_call", output_to_operand_aliasing={{0}: (11, {})} | custom-call | flops 12000000000 | bytes 5000000 | tf_op jit(solution)/shard_map/mix_backward/pallas_call | solution.py:529
  313.1 8.5 %convolution_convert_fusion = bf16[1408,2048]{1,0:T(8,128)(2,1)S(1)} fusion(bf16[1024,1408]{1,0:T(8,128)(2,1)} %get-tuple-element.184.dx_ref, bf16[1024,2048]{1,0:T(8,128)(2,1)S(1)} %copy-done.48), kind=kOutput, calls=%fused_computation.2 | convolution fusion | flops 5908463616 | bytes 12845056 | tf_op jit(solution)/shard_map/dot_general | solution.py:187
  331.5 18.4 %back_norm.1 = (bf16[1024,2048]{1,0:T(8,128)(2,1)}, f32[8,2048]{1,0:T(8,128)}) custom-call(s32[8]{0:T(128)} %copy-done.37, bf16[1024,2048]{1,0:T(8,128)(2,1)} %bitcast.257, bf16[1024,1024]{1,0:T(8,128)(2,1)} %get-tuple-element.147.dz_ref, bf16[1024,1408]{1,0:T(8,128)(2,1)} %get-tuple-element.184.dx_ref, bf16[1024,256]{1,0:T(8,128)(2,1)} %bitcast.34.refs_0_, ...), custom_call_target="tpu_custom_call" | custom-call | flops 17999998976 | bytes 24000000 | tf_op jit(solution)/shard_map/back_norm/pallas_call | solution.py:697
  358.9 7.0 %collective-permute-start.46 = (bf16[2,256,2048]{2,1,0:T(8,128)(2,1)S(1)}, bf16[2,256,2048]{2,1,0:T(8,128)(2,1)}, u32[]{:S(2)}, u32[]{:S(2)}) collective-permute-start(bf16[2,256,2048]{2,1,0:T(8,128)(2,1)S(1)} %dynamic-slice_bitcast_fusion.1), channel_id=1, source_target_pairs={{0,1},{1,0},{2,3},{3,2},{4,5},{5,4},{6,7},{7,6},{8,9},{9,8},{10,11... | collective-permute-start | bytes 6291464 | tf_op jit(solution)/shard_map/ppermute | solution.py:144
  377.6 6.9 %convolution_convert_fusion.1 = bf16[1024,2048]{1,0:T(8,128)(2,1)S(1)} fusion(bf16[1024,1024]{1,0:T(8,128)(2,1)S(1)} %copy-done.50, bf16[1024,2048]{1,0:T(8,128)(2,1)} %bitcast.32.w_ref), kind=kOutput, calls=%fused_computation.5 | convolution fusion | flops 4297064448 | bytes 10485760 | tf_op jit(solution)/shard_map/dot_general | solution.py:183
  388.6 10.9 %collective-permute-done.47 = bf16[256,2048]{1,0:T(8,128)(2,1)S(1)} collective-permute-done((bf16[256,2048]{1,0:T(8,128)(2,1)S(1)}, bf16[256,2048]{1,0:T(8,128)(2,1)S(1)}, u32[]{:S(2)}, u32[]{:S(2)}) %collective-permute-start.47) | collective-permute-done | bytes 1048608 | tf_op jit(solution)/shard_map/ppermute | solution.py:151
  410.4 11.3 %collective-permute-done.57 = f32[1,2048]{1,0:T(1,128)S(1)} collective-permute-done((f32[1,2048]{1,0:T(1,128)S(1)}, f32[1,2048]{1,0:T(1,128)S(1)}, u32[]{:S(2)}, u32[]{:S(2)}) %collective-permute-start.57) | collective-permute-done | bytes 8224 | tf_op jit(solution)/shard_map/ppermute | solution.py:167
  440.6 7.0 %collective-permute-done.59 = bf16[1024,256]{1,0:T(8,128)(2,1)S(1)} collective-permute-done((bf16[1024,256]{1,0:T(8,128)(2,1)S(1)}, bf16[1024,256]{1,0:T(8,128)(2,1)S(1)}, u32[]{:S(2)}, u32[]{:S(2)}) %collective-permute-start.59) | collective-permute-done | bytes 524320 | tf_op jit(solution)/shard_map/ppermute | solution.py:43
  448.9 7.1 %collective-permute-done.55 = bf16[256,2048]{1,0:T(8,128)(2,1)S(1)} collective-permute-done((bf16[256,2048]{1,0:T(8,128)(2,1)S(1)}, bf16[256,2048]{1,0:T(8,128)(2,1)S(1)}, u32[]{:S(2)}, u32[]{:S(2)}) %collective-permute-start.55) | collective-permute-done | bytes 1048608 | tf_op jit(solution)/shard_map/ppermute | solution.py:151
  480.6 11.2 %collective-permute-done.66.z2 = bf16[1024,256]{1,0:T(8,128)(2,1)S(1)} collective-permute-done((bf16[1024,256]{1,0:T(8,128)(2,1)S(1)}, bf16[1024,256]{1,0:T(8,128)(2,1)S(1)}, u32[]{:S(2)}, u32[]{:S(2)}) %collective-permute-start.66) | collective-permute-done | bytes 524320 | tf_op jit(solution)/shard_map/ppermute | solution.py:124
  502.9 8.2 %collective-permute-done.68.b2 = bf16[640,256]{1,0:T(8,128)(2,1)S(1)} collective-permute-done((bf16[640,256]{1,0:T(8,128)(2,1)S(1)}, bf16[640,256]{1,0:T(8,128)(2,1)S(1)}, u32[]{:S(2)}, u32[]{:S(2)}) %collective-permute-start.68) | collective-permute-done | bytes 327712 | tf_op jit(solution)/shard_map/ppermute | solution.py:124
  521.3 6.1 %assemble_x.1 = f32[8512,256]{1,0:T(8,128)} custom-call(s32[1]{0:T(128)} %bitcast.65.place_ref, bf16[4,64,128]{2,1,0:T(8,128)(2,1)} %constant.194.clone.order_ref, f32[8512,256]{1,0:T(8,128)} %assemble_z.1.held_ref, bf16[768,256]{1,0:T(8,128)(2,1)} %copy-done.11, bf16[768,256]{1,0:T(8,128)(2,1)} %copy-done.20, ...), custom_call_target="tpu_custom_call", output_to_operand_aliasing={{}: (2, {})} | custom-call | flops 5000000000 | bytes 6000000 | tf_op jit(solution)/shard_map/assemble_x/pallas_call | solution.py:779
  (445 shorter events, 225.8 us)
Async XLA Ops:
  7.2 98.2 %all-gather.7.cloned.1.call-start = ((), (), s32[]{:S(2)}) async-start(), calls=%async_computation.1 | async-start | bytes 5242880 | tf_op jit(solution)/shard_map/all_gather | solution.py:819
  7.9 167.2 %all-gather.5.cloned.1.call-start = ((), (), s32[]{:S(2)}) async-start(), calls=%async_computation | async-start | bytes 5242880 | tf_op jit(solution)/shard_map/all_gather | solution.py:820
  56.1 24.4 %collective-permute-start.4 = (bf16[1408,256]{1,0:T(8,128)(2,1)}, bf16[1408,256]{1,0:T(8,128)(2,1)}, u32[]{:S(2)}, u32[]{:S(2)}) collective-permute-start(bf16[1408,256]{1,0:T(8,128)(2,1)} %collective-permute-done.2.refs_7_.refs_16_), channel_id=1, source_target_pairs={{0,8},{8,16},{16,24},{24,28},{28,20},{20,12},{12,4},{4,0},{1,9},{9... | collective-permute-start | bytes 2162696 | tf_op jit(solution)/shard_map/ppermute | solution.py:43
  57.5 24.0 %collective-permute-start.5 = (bf16[1408,256]{1,0:T(8,128)(2,1)}, bf16[1408,256]{1,0:T(8,128)(2,1)}, u32[]{:S(2)}, u32[]{:S(2)}) collective-permute-start(bf16[1408,256]{1,0:T(8,128)(2,1)} %collective-permute-done.3.refs_2_.refs_11_), channel_id=1, source_target_pairs={{8,0},{16,8},{24,16},{28,24},{20,28},{12,20},{4,12},{0,4},{9,1},{1... | collective-permute-start | bytes 2162696 | tf_op jit(solution)/shard_map/ppermute | solution.py:43
  79.0 23.3 %collective-permute-start.15 = (bf16[1024,256]{1,0:T(8,128)(2,1)}, bf16[1024,256]{1,0:T(8,128)(2,1)}, u32[]{:S(2)}, u32[]{:S(2)}) collective-permute-start(bf16[1024,256]{1,0:T(8,128)(2,1)} %bitcast.34.refs_0_), channel_id=1, source_target_pairs={{8,0},{16,8},{24,16},{28,24},{20,28},{12,20},{4,12},{0,4},{9,1},{1... | collective-permute-start | bytes 1572872 | tf_op jit(solution)/shard_map/ppermute | solution.py:43
  79.1 23.2 %collective-permute-start.16 = (bf16[1024,256]{1,0:T(8,128)(2,1)}, bf16[1024,256]{1,0:T(8,128)(2,1)}, u32[]{:S(2)}, u32[]{:S(2)}) collective-permute-start(bf16[1024,256]{1,0:T(8,128)(2,1)} %bitcast.34.refs_0_), channel_id=1, source_target_pairs={{0,8},{8,16},{16,24},{24,28},{28,20},{20,12},{12,4},{4,0},{1,9},{9... | collective-permute-start | bytes 1572872 | tf_op jit(solution)/shard_map/ppermute | solution.py:43
  118.2 29.4 %collective-permute-start.20 = (bf16[1024,256]{1,0:T(8,128)(2,1)S(1)}, bf16[1024,256]{1,0:T(8,128)(2,1)S(1)}, u32[]{:S(2)}, u32[]{:S(2)}) collective-permute-start(bf16[1024,256]{1,0:T(8,128)(2,1)S(1)} %collective-permute-done.18.refs_7_), channel_id=1, source_target_pairs={{0,8},{8,16},{16,24},{24,28},{28,20},{20,12},{12,4},{4,0},{1,9},{9... | collective-permute-start | bytes 1572872 | tf_op jit(solution)/shard_map/ppermute | solution.py:43
  119.6 28.0 %collective-permute-start.19 = (bf16[1024,256]{1,0:T(8,128)(2,1)S(1)}, bf16[1024,256]{1,0:T(8,128)(2,1)S(1)}, u32[]{:S(2)}, u32[]{:S(2)}) collective-permute-start(bf16[1024,256]{1,0:T(8,128)(2,1)S(1)} %collective-permute-done.17.refs_2_), channel_id=1, source_target_pairs={{8,0},{16,8},{24,16},{28,24},{20,28},{12,20},{4,12},{0,4},{9,1},{1... | collective-permute-start | bytes 1572872 | tf_op jit(solution)/shard_map/ppermute | solution.py:43
  225.6 25.6 %collective-permute-start.26 = (bf16[512,256]{1,0:T(8,128)(2,1)S(1)}, bf16[512,256]{1,0:T(8,128)(2,1)S(1)}, u32[]{:S(2)}, u32[]{:S(2)}) collective-permute-start(bf16[512,256]{1,0:T(8,128)(2,1)S(1)} %get-tuple-element.259), channel_id=1, source_target_pairs={{0,8},{8,16},{16,24},{24,28},{28,20},{20,12},{12,4},{4,0},{1,9},{9... | collective-permute-start | bytes 786440 | tf_op jit(solution)/shard_map/ppermute | solution.py:43
  227.1 24.1 %collective-permute-start.27 = (bf16[512,256]{1,0:T(8,128)(2,1)S(1)}, bf16[512,256]{1,0:T(8,128)(2,1)S(1)}, u32[]{:S(2)}, u32[]{:S(2)}) collective-permute-start(bf16[512,256]{1,0:T(8,128)(2,1)S(1)} %get-tuple-element.257), channel_id=1, source_target_pairs={{8,0},{16,8},{24,16},{28,24},{20,28},{12,20},{4,12},{0,4},{9,1},{1... | collective-permute-start | bytes 786440 | tf_op jit(solution)/shard_map/ppermute | solution.py:43
  253.6 26.9 %collective-permute-start.30 = (bf16[128,2048]{1,0:T(8,128)(2,1)S(1)}, bf16[128,2048]{1,0:T(8,128)(2,1)S(1)}, u32[]{:S(2)}, u32[]{:S(2)}) collective-permute-start(bf16[128,2048]{1,0:T(8,128)(2,1)S(1)} %add_convert_fusion.10), channel_id=1, source_target_pairs={{0,8},{8,16},{16,24},{24,28},{28,20},{20,12},{12,4},{4,0},{1,9},{9... | collective-permute-start | bytes 1572872 | tf_op jit(solution)/shard_map/ppermute | solution.py:43
  255.1 25.4 %collective-permute-start.31 = (bf16[128,2048]{1,0:T(8,128)(2,1)S(1)}, bf16[128,2048]{1,0:T(8,128)(2,1)S(1)}, u32[]{:S(2)}, u32[]{:S(2)}) collective-permute-start(bf16[128,2048]{1,0:T(8,128)(2,1)S(1)} %get-tuple-element.156), channel_id=1, source_target_pairs={{8,0},{16,8},{24,16},{28,24},{20,28},{12,20},{4,12},{0,4},{9,1},{1... | collective-permute-start | bytes 1572872 | tf_op jit(solution)/shard_map/ppermute | solution.py:43
  255.1 46.1 %collective-permute-start.28 = (bf16[1024,256]{1,0:T(8,128)(2,1)S(1)}, bf16[1024,256]{1,0:T(8,128)(2,1)S(1)}, u32[]{:S(2)}, u32[]{:S(2)}) collective-permute-start(bf16[1024,256]{1,0:T(8,128)(2,1)S(1)} %pad_maximum_fusion), channel_id=1, source_target_pairs={{0,8},{8,16},{16,24},{24,28},{28,20},{20,12},{12,4},{4,0},{1,9},{9... | collective-permute-start | bytes 1572872 | tf_op jit(solution)/shard_map/ppermute | solution.py:43
  256.5 44.7 %collective-permute-start.29 = (bf16[1024,256]{1,0:T(8,128)(2,1)S(1)}, bf16[1024,256]{1,0:T(8,128)(2,1)S(1)}, u32[]{:S(2)}, u32[]{:S(2)}) collective-permute-start(bf16[1024,256]{1,0:T(8,128)(2,1)S(1)} %pad_maximum_fusion.1), channel_id=1, source_target_pairs={{8,0},{16,8},{24,16},{28,24},{20,28},{12,20},{4,12},{0,4},{9,1},{1... | collective-permute-start | bytes 1572872 | tf_op jit(solution)/shard_map/ppermute | solution.py:43
  327.2 30.0 %collective-permute-start.40 = (bf16[128,2048]{1,0:T(8,128)(2,1)}, bf16[128,2048]{1,0:T(8,128)(2,1)S(1)}, u32[]{:S(2)}, u32[]{:S(2)}) collective-permute-start(bf16[128,2048]{1,0:T(8,128)(2,1)} %get-tuple-element.187), channel_id=1, source_target_pairs={{0,8},{8,16},{16,24},{24,28},{28,20},{20,12},{12,4},{4,0},{1,9},{9... | collective-permute-start | bytes 1572872 | tf_op jit(solution)/shard_map/ppermute | solution.py:43
  328.5 28.7 %collective-permute-start.41 = (bf16[128,2048]{1,0:T(8,128)(2,1)}, bf16[128,2048]{1,0:T(8,128)(2,1)}, u32[]{:S(2)}, u32[]{:S(2)}) collective-permute-start(bf16[128,2048]{1,0:T(8,128)(2,1)} %get-tuple-element.188), channel_id=1, source_target_pairs={{8,0},{16,8},{24,16},{28,24},{20,28},{12,20},{4,12},{0,4},{9,1},{1... | collective-permute-start | bytes 1572872 | tf_op jit(solution)/shard_map/ppermute | solution.py:43
  328.8 23.2 %collective-permute-start.38 = (bf16[384,256]{1,0:T(8,128)(2,1)}, bf16[384,256]{1,0:T(8,128)(2,1)}, u32[]{:S(2)}, u32[]{:S(2)}) collective-permute-start(bf16[384,256]{1,0:T(8,128)(2,1)} %slice.526), channel_id=1, source_target_pairs={{0,8},{8,16},{16,24},{24,28},{28,20},{20,12},{12,4},{4,0},{1,9},{9... | collective-permute-start | bytes 589832 | tf_op jit(solution)/shard_map/ppermute | solution.py:43
  330.2 23.5 %collective-permute-start.36 = (bf16[384,256]{1,0:T(8,128)(2,1)}, bf16[384,256]{1,0:T(8,128)(2,1)}, u32[]{:S(2)}, u32[]{:S(2)}) collective-permute-start(bf16[384,256]{1,0:T(8,128)(2,1)} %get-tuple-element.180), channel_id=1, source_target_pairs={{0,8},{8,16},{16,24},{24,28},{28,20},{20,12},{12,4},{4,0},{1,9},{9... | collective-permute-start | bytes 589832 | tf_op jit(solution)/shard_map/ppermute | solution.py:43
  376.4 23.1 %collective-permute-start.47 = (bf16[256,2048]{1,0:T(8,128)(2,1)S(1)}, bf16[256,2048]{1,0:T(8,128)(2,1)S(1)}, u32[]{:S(2)}, u32[]{:S(2)}) collective-permute-start(bf16[256,2048]{1,0:T(8,128)(2,1)S(1)} %fusion.6), channel_id=1, source_target_pairs={{0,2},{1,3},{2,0},{3,1},{4,6},{5,7},{6,4},{7,5},{8,10},{9,11},{10,... | collective-permute-start | bytes 3145736 | tf_op jit(solution)/shard_map/ppermute | solution.py:151
  401.1 22.7 %collective-permute-start.50 = (bf16[2,256,2048]{2,1,0:T(8,128)(2,1)}, bf16[2,256,2048]{2,1,0:T(8,128)(2,1)}, u32[]{:S(2)}, u32[]{:S(2)}) collective-permute-start(bf16[2,256,2048]{2,1,0:T(8,128)(2,1)} %dynamic-slice_bitcast_fusion), channel_id=1, source_target_pairs={{0,1},{1,0},{2,3},{3,2},{4,5},{5,4},{6,7},{7,6},{8,9},{9,8},{10,11... | collective-permute-start | bytes 6291464 | tf_op jit(solution)/shard_map/ppermute | solution.py:144
  404.5 32.0 %collective-permute-start.53 = (bf16[640,256]{1,0:T(8,128)(2,1)}, bf16[640,256]{1,0:T(8,128)(2,1)S(1)}, u32[]{:S(2)}, u32[]{:S(2)}) collective-permute-start(bf16[640,256]{1,0:T(8,128)(2,1)} %get-tuple-element.200), channel_id=1, source_target_pairs={{0,8},{8,16},{16,24},{24,28},{28,20},{20,12},{12,4},{4,0},{1,9},{9... | collective-permute-start | bytes 983048 | tf_op jit(solution)/shard_map/ppermute | solution.py:43
  405.7 30.8 %collective-permute-start.54 = (bf16[640,256]{1,0:T(8,128)(2,1)}, bf16[640,256]{1,0:T(8,128)(2,1)S(1)}, u32[]{:S(2)}, u32[]{:S(2)}) collective-permute-start(bf16[640,256]{1,0:T(8,128)(2,1)} %get-tuple-element.201), channel_id=1, source_target_pairs={{8,0},{16,8},{24,16},{28,24},{20,28},{12,20},{4,12},{0,4},{9,1},{1... | collective-permute-start | bytes 983048 | tf_op jit(solution)/shard_map/ppermute | solution.py:43
  405.9 33.3 %collective-permute-start.51 = (bf16[768,256]{1,0:T(8,128)(2,1)S(1)}, bf16[768,256]{1,0:T(8,128)(2,1)S(1)}, u32[]{:S(2)}, u32[]{:S(2)}) collective-permute-start(bf16[768,256]{1,0:T(8,128)(2,1)S(1)} %get-tuple-element.198), channel_id=1, source_target_pairs={{0,8},{8,16},{16,24},{24,28},{28,20},{20,12},{12,4},{4,0},{1,9},{9... | collective-permute-start | bytes 1179656 | tf_op jit(solution)/shard_map/ppermute | solution.py:43
  456.0 39.0 %collective-permute-start.71 = (bf16[128,2048]{1,0:T(8,128)(2,1)S(1)}, bf16[128,2048]{1,0:T(8,128)(2,1)S(1)}, u32[]{:S(2)}, u32[]{:S(2)}) collective-permute-start(bf16[128,2048]{1,0:T(8,128)(2,1)S(1)} %add_convert_fusion.1), channel_id=1, source_target_pairs={{0,1},{1,0},{2,3},{3,2},{4,5},{5,4},{6,7},{7,6},{8,9},{9,8},{10,11... | collective-permute-start | bytes 1572872 | tf_op jit(solution)/shard_map/ppermute | solution.py:128
  (106 other events, 1396.9 us)
Sparse Core Ops, SparseCore 0:
  9.6 36.9 all-gather.6
  48.1 34.4 all-gather.4

commit v2 on v1

v2 whole, which is shorter than its diff:
```python
import jax
import jax.numpy as jnp
import numpy as np
from jax import lax
from jax.experimental import pallas as pl
from jax.experimental.pallas import tpu as pltpu
from jax.sharding import PartitionSpec as P

D = 2048
HEADS = 64
HEADDIM = 64
STATE = 128
KW = 4
GROUP = 256
DI = HEADS * HEADDIM
CONV = DI + 2 * STATE
PAIR = 2 * HEADDIM
EPS = 1e-05
SEG = 256
HALO = 8
SMALL = 32
VMEM_LIMIT = 56 * 1024 * 1024
F32 = jnp.float32
BF16 = jnp.bfloat16


def ring_place(index, n):
    return jnp.where(index % 2 == 0, index // 2, n - 1 - index // 2)


def ring_member(place, n):
    place = place % n
    return jnp.where(place < n // 2, 2 * place, 2 * (n - 1 - place) + 1)


def ring_routes(n):
    order = [2 * p if p < n // 2 else 2 * (n - 1 - p) + 1 for p in range(n)]
    forward = [(order[p], order[(p + 1) % n]) for p in range(n)]
    return forward, [(b, a) for a, b in forward]


def send(block, route):
    return lax.ppermute(block, "fsdp", route)


def after(value, *earlier):
    return lax.optimization_barrier((value, *earlier))[0]


def halves(rows):
    upper = -(-rows // 256) * 128 if rows >= 512 else rows // 2
    return upper, rows - upper


class Gather:
    def __init__(self, block, n):
        self.forward, self.backward = ring_routes(n)
        self.block, self.n = block, n
        self.latest = (block, block)
        self.ahead, self.behind = [], []

    def load(self):
        right, left = self.latest
        if len(self.ahead) == self.n // 2 - 1:
            upper, _ = halves(self.block.shape[0])
            return right[:upper], left[upper:]
        return right, left

    def fire(self, right, left):
        last = len(self.ahead) == self.n // 2 - 1
        self.latest = send(right, self.forward), send(left, self.backward)
        if not last:
            self.behind.insert(0, self.latest[0])
            self.ahead.append(self.latest[1])

    def parts(self):
        return [self.block] + self.ahead + list(self.latest) + self.behind


class Reduce:
    def __init__(self, chunk, n):
        self.forward, self.backward = ring_routes(n)
        self.chunk, self.n, self.step = chunk, n, n // 2
        first = chunk(n // 2).astype(BF16)
        self.upper, _ = halves(first.shape[0])
        self.right, self.left = first[: self.upper], first[self.upper :]

    def load(self):
        return self.right, self.left

    def fire(self, right, left):
        self.latest = send(right, self.forward), send(left, self.backward)
        self.step -= 1

    def join(self):
        right, left = (part.astype(F32) for part in self.latest)
        if self.step == 0:
            return self.chunk(0).astype(F32) + right + left
        own_right = self.chunk(self.step).astype(F32)
        own_left = self.chunk(self.n - self.step).astype(F32)
        cut = self.upper
        if self.step == self.n // 2 - 1:
            right = jnp.concatenate([own_right[:cut] + right, own_right[cut:]], axis=0)
            left = jnp.concatenate([own_left[:cut], own_left[cut:] + left], axis=0)
        else:
            right, left = own_right + right, own_left + left
        self.right, self.left = right.astype(BF16), left.astype(BF16)


def barrier(value, *earlier):
    return lax.optimization_barrier((value, earlier))[0]


def next_hop(rings, inputs, *earlier):
    loads, inputs = barrier(([ring.load() for ring in rings], inputs), *earlier)
    for ring, load in zip(rings, loads):
        ring.fire(*load)
    return inputs


def arrivals(*rings):
    return sum((ring.latest for ring in rings), ())


def ctx_route(m, flip):
    return [(i, i ^ flip) for i in range(m)]


def far_share(block, m):
    return lax.ppermute(block, "ctx", ctx_route(m, 2))


def near_share(block, other, m):
    near = lax.ppermute(block, "ctx", ctx_route(m, 1))
    far = lax.ppermute(other, "ctx", ctx_route(m, 1))
    return [block, near, other, far]


def ctx_share(block, m):
    return near_share(block, far_share(block, m), m)


class CtxReduce:
    def __init__(self, share, m):
        self.m, place = m, lax.axis_index("ctx")
        self.core, self.across = place % 2, place // 2
        split = share.reshape((m // 2, 2) + share.shape[1:])
        self.kept = lax.dynamic_index_in_dim(split, self.core, 1, False)
        sent = lax.dynamic_index_in_dim(split, 1 - self.core, 1, False)
        self.near = lax.ppermute(sent, "ctx", ctx_route(m, 1))

    def middle(self):
        self.both = self.kept.astype(F32) + self.near.astype(F32)
        self.sent = lax.dynamic_index_in_dim(self.both, 1 - self.across, 0, False).astype(BF16)

    def send_far(self):
        self.far = lax.ppermute(self.sent, "ctx", ctx_route(self.m, 2))

    def total(self):
        return lax.dynamic_index_in_dim(self.both, self.across, 0, False) + self.far.astype(F32)


def ctx_sum(values, m):
    for flip in (1, 2):
        values = values + lax.ppermute(values, "ctx", ctx_route(m, flip))
    return values


def nt(a, b):
    return lax.dot_general(a, b, (((1,), (1,)), ((), ())), preferred_element_type=F32)


def nn(a, b):
    return lax.dot_general(a, b, (((1,), (0,)), ((), ())), preferred_element_type=F32)


def tn(a, b):
    return lax.dot_general(a, b, (((0,), (0,)), ((), ())), preferred_element_type=F32)


def lanes(shape):
    return lax.broadcasted_iota(jnp.int32, shape, len(shape) - 1)


def busy(us, megabytes):
    return pl.CostEstimate(
        flops=int(us * 1e9), transcendentals=0, bytes_accessed=int(megabytes * 1e6)
    )


def softplus(v):
    return jnp.maximum(v, 0.0) + jnp.log1p(jnp.exp(-jnp.abs(v)))


def sigmoid(v):
    return 1.0 / (1.0 + jnp.exp(-v))


def ones_where(keep):
    row = lax.broadcasted_iota(jnp.int32, (GROUP, GROUP), 0)
    col = lax.broadcasted_iota(jnp.int32, (GROUP, GROUP), 1)
    return keep(row, col)


def exact(a, b):
    return lax.dot_general(
        a, b, (((1,), (0,)), ((), ())), preferred_element_type=F32, precision=lax.Precision.HIGHEST
    )


def tiles(width):
    return [slice(at, at + PAIR) for at in range(0, width, PAIR)]


def conv_tile(extended, taps_ref, cols):
    total = taps_ref[KW : KW + 1, cols]
    for k in range(KW):
        at = HALO - KW + 1 + k
        total = total + taps_ref[k : k + 1, cols] * extended[at : at + GROUP]
    return total


def by_segments(weights):
    n = D // SEG
    places = list(range(n // 2)) + [n // 2] * 2 + list(range(n // 2 + 1, n))
    at = [0] * len(places)
    at[n // 2 + 1] = weights[n // 2].shape[0]
    return list(zip(places, at, weights))


def project_into(out_ref, normed_ref, weights, total):
    whole = None
    for o, at, w in by_segments(weights):
        part = nt(normed_ref[:, o * SEG : (o + 1) * SEG], w[...])
        if o == D // SEG // 2:
            total[:, at : at + w.shape[0]] = part
        else:
            whole = part if whole is None else whole + part
    out_ref[...] = (whole + total[...]).astype(BF16)


def pack(
    place_ref, columns_ref, out_ref, small_ref, x_ref, z_ref, o_ref, steps, rows, sems,
):
    place = place_ref[0]
    pairs, m = z_ref.shape[0] // PAIR, out_ref.shape[0] // PAIR
    core = pairs * PAIR + 2 * STATE
    copies = [
        (columns_ref.at[pl.ds(DI + CONV, HEADS)], steps),
        (columns_ref.at[pl.ds(2 * DI, 2 * STATE)], x_ref.at[pl.ds(pairs * PAIR, 2 * STATE)]),
        (out_ref.at[pl.ds(pl.multiple_of(place * PAIR, PAIR), PAIR)], o_ref),
    ]
    for g in range(pairs):
        here = pl.ds(g * PAIR, PAIR)
        for start, ref in ((DI, x_ref), (0, z_ref)):
            at = pl.multiple_of(start + (g * m + place) * PAIR, PAIR)
            copies.append((columns_ref.at[pl.ds(at, PAIR)], ref.at[here]))
    copies = [pltpu.make_async_copy(*pair, sems.at[k]) for k, pair in enumerate(copies)]
    for copy in copies:
        copy.start()
    rows[...] = jnp.zeros_like(rows)
    rows[SMALL : SMALL + small_ref.shape[0], :] = small_ref[...].astype(F32)
    copies[0].wait()
    want = lax.broadcasted_iota(jnp.int32, (2 * pairs, HEADS), 0)
    have = lax.broadcasted_iota(jnp.int32, (2 * pairs, HEADS), 1)
    head = (want % pairs) * 2 * m + 2 * place + want // pairs
    rows[: 2 * pairs, :] = nn((have == head).astype(BF16), steps[...])
    x_ref[core : core + PAIR, :] = rows[...].astype(BF16)
    for copy in copies[1:]:
        copy.wait()


def run_pack(place, columns, w_out, small, pairs):
    rows = columns.shape[1]
    core = pairs * PAIR + 2 * STATE
    anywhere = pl.BlockSpec(memory_space=pl.ANY)
    shapes = [(core + PAIR, rows), (pairs * PAIR, rows), (PAIR, D)]
    return pl.pallas_call(
        pack,
        grid_spec=pltpu.PrefetchScalarGridSpec(
            num_scalar_prefetch=1,
            grid=(1,),
            in_specs=[anywhere, anywhere, pl.BlockSpec(small.shape, lambda i, t: (0, 0))],
            out_specs=[pl.BlockSpec(shape, lambda i, t: (0, 0)) for shape in shapes],
            scratch_shapes=[
                pltpu.VMEM((HEADS, rows), BF16),
                pltpu.VMEM((PAIR, rows), F32),
                pltpu.SemaphoreType.DMA((2 * pairs + 3,)),
            ],
        ),
        out_shape=[jax.ShapeDtypeStruct(shape, BF16) for shape in shapes],
        compiler_params=pltpu.CompilerParams(vmem_limit_bytes=VMEM_LIMIT),
        name="pack",
    )(place, columns, w_out, small)


def collect(members_ref, *refs):
    out_ref = refs[-1]
    for o, ref in enumerate(refs[:-1]):
        out_ref[members_ref[o]] = ref[...].astype(F32)


def run_collect(members, parts):
    n = len(parts) - 1
    lasts = parts[: n // 2] + parts[n // 2 + 1 :]
    at = lambda part: (part.shape[0] - PAIR + SMALL) // 32
    return pl.pallas_call(
        collect,
        grid_spec=pltpu.PrefetchScalarGridSpec(
            num_scalar_prefetch=1,
            grid=(1,),
            in_specs=[pl.BlockSpec((32, SEG), lambda i, t, k=at(p): (k, 0)) for p in lasts],
            out_specs=pl.BlockSpec((n, 32, SEG), lambda i, t: (0, 0, 0)),
        ),
        out_shape=jax.ShapeDtypeStruct((n, 32, SEG), F32),
        compiler_params=pltpu.CompilerParams(vmem_limit_bytes=VMEM_LIMIT),
        name="collect",
    )(members, *lasts)


def front(members_ref, tokens_ref, *refs):
    weights, (normed_ref, proj_ref, total) = refs[:-3], refs[-3:]
    tokens = tokens_ref[...].astype(F32)
    inv = lax.rsqrt(jnp.mean(tokens * tokens, axis=-1, keepdims=True) + EPS)
    for o in range(D // SEG):
        at = pl.multiple_of(members_ref[o] * SEG, SEG)
        cols = slice(o * SEG, (o + 1) * SEG)
        last = weights[o if o < D // SEG // 2 else o + 1]
        row = last.shape[0] - PAIR + SMALL
        gain = last[row : row + 16, :].astype(F32)[0:1]
        part = tokens_ref[:, pl.ds(at, SEG)].astype(F32) * inv * gain
        normed_ref[:, cols] = part.astype(BF16)
    project_into(proj_ref, normed_ref, weights, total)


def resident(array, grid_args=1):
    zeros = (0,) * array.ndim
    if grid_args == 2:
        return pl.BlockSpec(array.shape, lambda i, t: zeros, pipeline_mode=pl.Buffered(1))
    return pl.BlockSpec(array.shape, lambda i: zeros, pipeline_mode=pl.Buffered(1))


def run_front(members, tokens, weights):
    length, cols = tokens.shape[0], weights[0].shape[0]
    return pl.pallas_call(
        front,
        grid_spec=pltpu.PrefetchScalarGridSpec(
            num_scalar_prefetch=1,
            grid=(length // GROUP,),
            in_specs=[
                pl.BlockSpec((GROUP, D), lambda i, t: (i, 0)),
            ]
            + [resident(w, 2) for w in weights],
            out_specs=[
                pl.BlockSpec((GROUP, D), lambda i, t: (i, 0)),
                pl.BlockSpec((GROUP, cols), lambda i, t: (i, 0)),
            ],
            scratch_shapes=[pltpu.VMEM((GROUP, cols), F32)],
        ),
        out_shape=[
            jax.ShapeDtypeStruct((length, D), BF16),
            jax.ShapeDtypeStruct((length, cols), BF16),
        ],
        compiler_params=pltpu.CompilerParams(vmem_limit_bytes=VMEM_LIMIT),
        cost_estimate=busy(12, 18),
        name="front",
    )(members, tokens, *weights)


def project(normed_ref, *refs):
    project_into(refs[-2], normed_ref, refs[:-2], refs[-1])


def run_project(normed, weights):
    length, cols = normed.shape[0], weights[0].shape[0]
    return pl.pallas_call(
        project,
        grid=(length // GROUP,),
        in_specs=[pl.BlockSpec((GROUP, D), lambda i: (i, 0))] + [resident(w) for w in weights],
        out_specs=pl.BlockSpec((GROUP, cols), lambda i: (i, 0)),
        out_shape=jax.ShapeDtypeStruct((length, cols), BF16),
        scratch_shapes=[pltpu.VMEM((GROUP, cols), F32)],
        compiler_params=pltpu.CompilerParams(vmem_limit_bytes=VMEM_LIMIT),
        cost_estimate=busy(8, 10),
        name="project",
    )(normed, *weights)


def spread_rows(ref, index, rows):
    count = rows.shape[0]
    ref[pl.ds(index, count), :] = rows[:, :128]
    ref[pl.ds(ref.shape[0] // 2 + index, count), :] = rows[:, 128:]


def all_rows(stack):
    half = stack.shape[0] // 2
    return jnp.concatenate([stack[:half], stack[half:]], axis=1)


def pair_rows(ref, g, pairs):
    half = 8 * pairs
    return jnp.concatenate(
        [ref[pl.ds(g, 8, stride=pairs), :], ref[pl.ds(half + g, 8, stride=pairs), :]], axis=1
    )


def high_low(v):
    high = v.astype(BF16)
    return high, (v - high.astype(F32)).astype(BF16)


def tri_units(back):
    units = []
    for r in range(GROUP // 64):
        for t in range(GROUP // 128):
            if (t >= r // 2) if back else (t <= r // 2):
                units.append((slice(64 * r, 64 * r + 64), slice(128 * t, 128 * t + 128), t == r // 2))
    return units


def diagonal(keep):
    row = lax.broadcasted_iota(jnp.int32, (128, 128), 0)
    col = lax.broadcasted_iota(jnp.int32, (128, 128), 1)
    return jnp.where(keep(row, col), 0.0, -1e30)


def mix_forward(
    proj_ref, taps_ref, heads_ref, skip_ref, act_ref, table_ref, y_ref, start_ref,
    state, halo, gram, bias, scores,
):
    pairs = state.shape[0]
    heads, width = 2 * pairs, pairs * PAIR
    core = width + 2 * STATE

    @pl.when(pl.program_id(0) == 0)
    def _():
        state[...] = jnp.zeros_like(state)
        halo[...] = jnp.zeros_like(halo)
        scores[...] = jnp.zeros_like(scores)
        bias[...] = diagonal(lambda row, col: row >= col)

    def activate(cols):
        current = proj_ref[:, cols].astype(F32)
        conv = conv_tile(jnp.concatenate([halo[:, cols], current], axis=0), taps_ref, cols)
        halo[:, cols] = current[GROUP - HALO :]
        act = (conv * sigmoid(conv)).astype(BF16)
        act_ref[:, cols] = act
        return act

    bs = activate(slice(width, width + STATE))
    cs = activate(slice(width + STATE, core))
    raw = proj_ref[:, core : core + PAIR].astype(F32).T[:heads]
    dt = softplus(raw + heads_ref[:heads, 0:1])
    upto = ones_where(lambda row, col: row <= col).astype(F32)
    cum = exact(dt * heads_ref[heads:, 0:1], upto)
    last = cum[:, GROUP - 1 :]
    table = jnp.concatenate([cum, dt, jnp.exp(last - cum) * dt, jnp.exp(cum)], axis=0)
    spread_rows(table_ref.at[0], 0, table)
    gram[...] = nt(cs, bs)
    bs_t = bs.astype(F32).T

    def one(g, unused):
        cols = pl.ds(pl.multiple_of(g * PAIR, PAIR), PAIR)
        rows = pair_rows(table_ref.at[0], g, pairs)
        turned = rows.T
        x = activate(cols)
        first = lanes(x.shape) < HEADDIM
        start = state[g]
        start_ref[0, g] = start
        inner = nn(cs, start.astype(BF16))
        parts, locals_ = [], []
        for e in range(2):
            for at, to, on in tri_units(False):
                differ = turned[at, e : e + 1] - rows[e : e + 1, to]
                if on:
                    differ = differ + bias[at.start % 128 : at.start % 128 + 64, :]
                decay = jnp.exp(differ)
                scores[e, at, to] = (gram[at, to] * decay * rows[2 + e : 3 + e, to]).astype(BF16)
            parts.append(nn(scores[e], x))
            locals_.append(nn((bs_t * rows[4 + e : 5 + e, :]).astype(BF16), x))
        grow = jnp.where(first, turned[:, 6:7], turned[:, 7:8])
        y_ref[:, cols] = (
            jnp.where(first, parts[0], parts[1]) + grow * inner + skip_ref[:, cols] * x.astype(F32)
        )
        shrink = jnp.where(first[:1], rows[6:7, GROUP - 1 :], rows[7:8, GROUP - 1 :])
        state[g] = shrink * start + jnp.where(first[:STATE], locals_[0], locals_[1])
        return unused

    lax.fori_loop(0, pairs, one, 0, unroll=2)


def run_mix_forward(proj, taps, heads_in, skip, pairs):
    length = proj.shape[0]
    blocks, width = length // GROUP, pairs * PAIR
    core = width + 2 * STATE
    whole = lambda i: (0, 0)
    return pl.pallas_call(
        mix_forward,
        grid=(blocks,),
        in_specs=[
            pl.BlockSpec((GROUP, proj.shape[1]), lambda i: (i, 0)),
            pl.BlockSpec(taps.shape, whole),
            pl.BlockSpec(heads_in.shape, whole),
            pl.BlockSpec(skip.shape, whole),
        ],
        out_specs=[
            pl.BlockSpec((GROUP, core), lambda i: (i, 0)),
            pl.BlockSpec((1, 16 * pairs, 128), lambda i: (i, 0, 0)),
            pl.BlockSpec((GROUP, width), lambda i: (i, 0)),
            pl.BlockSpec((1, pairs, STATE, PAIR), lambda i: (i, 0, 0, 0)),
        ],
        out_shape=[
            jax.ShapeDtypeStruct((length, core), BF16),
            jax.ShapeDtypeStruct((blocks, 16 * pairs, 128), F32),
            jax.ShapeDtypeStruct((length, width), F32),
            jax.ShapeDtypeStruct((blocks, pairs, STATE, PAIR), F32),
        ],
        scratch_shapes=[
            pltpu.VMEM((pairs, STATE, PAIR), F32),
            pltpu.VMEM((HALO, core), F32),
            pltpu.VMEM((GROUP, GROUP), F32),
            pltpu.VMEM((128, 128), F32),
            pltpu.VMEM((2, GROUP, GROUP), BF16),
        ],
        compiler_params=pltpu.CompilerParams(vmem_limit_bytes=VMEM_LIMIT),
        cost_estimate=busy(18, 15),
        name="mix_forward",
    )(proj, taps, heads_in, skip)


def mix_backward(
    top, act_ref, proj_ref, prev_ref, taps_ref, heads_ref, skip_ref, table_ref, start_ref, dy_ref,
    carry_in, halo_in, held_ref, dx_ref, grads_ref, dheads_ref, carried, halo,
    gram, dgram, bias, d_scores, scores, db, dc, found, ends,
):
    pairs = carried.shape[0]
    heads, width = 2 * pairs, pairs * PAIR
    core = width + 2 * STATE
    step = pl.program_id(0)

    @pl.when(step == 0)
    def _():
        carried[...] = carry_in[...]
        halo[...] = halo_in[...]
        grads_ref[...] = jnp.zeros_like(grads_ref)
        dheads_ref[...] = jnp.zeros_like(dheads_ref)
        scores[...] = jnp.zeros_like(scores)
        bias[...] = diagonal(lambda row, col: row <= col)

    has_prev = jnp.where(top - step > 0, 1.0, 0.0)
    bs, cs = act_ref[:, width : width + STATE], act_ref[:, width + STATE : core]
    bs_float = bs.astype(F32)
    cs_t = cs.astype(F32).T.astype(BF16)
    gram[...] = nt(bs, cs)
    for ref in (dgram, db, dc):
        ref[...] = jnp.zeros_like(ref)

    def conv_back(d_act, cols):
        before = prev_ref[:, cols].astype(F32)[prev_ref.shape[0] - HALO :] * has_prev
        extended = jnp.concatenate([before, proj_ref[:, cols].astype(F32)], axis=0)
        conv = conv_tile(extended, taps_ref, cols)
        sig = sigmoid(conv)
        d_conv = d_act * (sig * (1.0 + conv * (1.0 - sig)))
        onward = jnp.concatenate([d_conv, halo[:, cols]], axis=0)
        d_in = taps_ref[KW - 1 : KW, cols] * d_conv
        for k in range(KW - 1):
            at = KW - 1 - k
            d_in = d_in + taps_ref[k : k + 1, cols] * onward[at : at + GROUP]
        dx_ref[:, cols] = d_in.astype(BF16)
        sums = []
        for k in range(KW):
            at = HALO - KW + 1 + k
            sums.append(jnp.sum(d_conv * extended[at : at + GROUP], axis=0, keepdims=True))
        sums.append(jnp.sum(d_conv, axis=0, keepdims=True))
        sums.append(jnp.zeros((8 - KW - 1, sums[0].shape[1]), F32))
        grads_ref[:, cols] += jnp.concatenate(sums, axis=0)
        halo[:, cols] = d_conv[:HALO]

    def one(g, unused):
        cols = pl.ds(pl.multiple_of(g * PAIR, PAIR), PAIR)
        rows = pair_rows(table_ref.at[0], g, pairs)
        turned = rows.T
        x, dy = act_ref[:, cols], dy_ref[:, cols]
        first = lanes(x.shape) < HEADDIM
        dy_float = dy.astype(F32)
        start, grad = start_ref[0, g], carried[g]
        start_low, grad_low = start.astype(BF16), grad.astype(BF16)
        inner = nn(cs, start_low)
        grow = jnp.where(first, turned[:, 6:7], turned[:, 7:8])
        d_inner = (dy_float * grow).astype(BF16)
        dc[...] += nt(d_inner, start_low)
        touched = dy_float * inner
        held = jnp.sum(grad * start, axis=0, keepdims=True)
        zero = jnp.zeros_like(x)
        reach = nn(bs, grad_low)
        sent = x.astype(F32) * jnp.where(first, turned[:, 4:5], turned[:, 5:6])
        for half in high_low(sent):
            db[...] += nt(half, grad_low)
        parts, sums_j, linked = [], [], []
        for e in range(2):
            own = first if e == 0 else jnp.logical_not(first)
            d_scores[e] = nt(jnp.where(own, x, zero), dy)
            linked_i, linked_j = {}, {}
            for at, to, on in tri_units(True):
                dt_col = turned[at, 2 + e : 3 + e]
                differ = rows[e : e + 1, to] - turned[at, e : e + 1]
                if on:
                    differ = differ + bias[at.start % 128 : at.start % 128 + 64, :]
                decay = jnp.exp(differ)
                grown = gram[at, to] * decay
                d_score = d_scores[e, at, to]
                score = grown * dt_col
                scores[e, at, to] = score.astype(BF16)
                dgram[at, to] += d_score * decay * dt_col
                along_i = d_score * grown
                along_j = jnp.sum(d_score * score, axis=0, keepdims=True)
                key_i, key_j = at.start, to.start
                linked_i[key_i] = along_i if key_i not in linked_i else linked_i[key_i] + along_i
                linked_j[key_j] = along_j if key_j not in linked_j else linked_j[key_j] + along_j
            sums_j.append(jnp.concatenate([linked_j[k] for k in sorted(linked_j)], axis=1))
            linked.append(jnp.concatenate([linked_i[k] for k in sorted(linked_i)], axis=0))
            tail_col = turned[:, 4 + e : 5 + e]
            parts.append(nn(scores[e], dy) + nn((bs_float * tail_col).astype(BF16), grad_low))
        pick = lax.broadcasted_iota(jnp.int32, (8, 2 * PAIR), 0)
        lane = lanes((8, 2 * PAIR))
        by_head = (pick == lane // HEADDIM).astype(BF16)
        by_pair = (pick == 4 + lane // PAIR).astype(BF16)
        kept = jnp.zeros((8, GROUP), F32)
        for sums, select in (
            ((x.astype(F32) * reach, touched), by_head),
            (linked, by_pair),
        ):
            for half in high_low(jnp.concatenate(sums, axis=1)):
                kept = kept + nt(select, half)
        kept = jnp.concatenate([kept[:6]] + sums_j, axis=0)
        found[pl.ds(g, 8, stride=pairs), :] = kept[:, :128]
        found[pl.ds(8 * pairs + g, 8, stride=pairs), :] = kept[:, 128:]
        ends[pl.ds(g, 2, stride=pairs), :] = jnp.concatenate(
            [jnp.where(first[:1], held, 0.0), jnp.where(first[:1], 0.0, held)], axis=0
        )
        conv_back(jnp.where(first, parts[0], parts[1]) + skip_ref[:, cols] * dy_float, cols)
        shrink = jnp.where(first[:1], rows[6:7, GROUP - 1 :], rows[7:8, GROUP - 1 :])
        carried[g] = shrink * grad + nn(cs_t, d_inner)
        return unused

    lax.fori_loop(0, pairs, one, 0, unroll=2)
    low = dgram[...].astype(BF16)
    conv_back(db[...] + nn(low, cs), slice(width, width + STATE))
    conv_back(dc[...] + tn(low, bs), slice(width + STATE, core))

    rows, sums = all_rows(table_ref[0]), all_rows(found[...])
    d_tail, touched, sum_i, sum_j = (sums[k * heads : (k + 1) * heads] for k in range(4))
    cum, dt, tail, growth = (rows[k * heads : (k + 1) * heads] for k in range(4))
    a_neg = heads_ref[heads:, 0:1]
    tail_log = d_tail * tail
    d_last = jnp.sum(tail_log, axis=1, keepdims=True)
    d_last = d_last + jnp.sum(ends[...], axis=1, keepdims=True) * growth[:, GROUP - 1 :]
    d_cum = touched * growth - tail_log + sum_j - dt * sum_i
    d_cum = d_cum + jnp.where(lanes(d_cum.shape) == GROUP - 1, d_last, 0.0)
    d_rate = exact(d_cum, ones_where(lambda row, col: row >= col).astype(F32))
    raw = proj_ref[:, core : core + PAIR].astype(F32).T[:heads]
    d_step = d_tail * jnp.exp(cum[:, GROUP - 1 :] - cum) + sum_i
    d_dt = (d_step + d_rate * a_neg) * sigmoid(raw + heads_ref[:heads, 0:1])
    dheads_ref[:heads, :] += d_dt
    dheads_ref[heads:, :] += d_rate * dt
    filled = jnp.concatenate([d_dt, jnp.zeros((PAIR - heads, GROUP), F32)], axis=0)
    dx_ref[:, core : core + PAIR] = filled.T.astype(BF16)


def run_mix_backward(span, top, act, proj, taps, heads_in, skip, table, starts, dy, carry, halo, held):
    pairs = carry.shape[0]
    heads, width = 2 * pairs, pairs * PAIR
    core = width + 2 * STATE
    whole = lambda i: (0, 0)
    block = lambda i: (top - i, 0)
    before = GROUP // 16
    return pl.pallas_call(
        lambda *refs: mix_backward(top, *refs),
        grid=(span,),
        in_specs=[
            pl.BlockSpec((GROUP, core), block),
            pl.BlockSpec((GROUP, proj.shape[1]), block),
            pl.BlockSpec((16, proj.shape[1]), lambda i: (jnp.maximum((top - i) * before - 1, 0), 0)),
            pl.BlockSpec(taps.shape, whole),
            pl.BlockSpec(heads_in.shape, whole),
            pl.BlockSpec(skip.shape, whole),
            pl.BlockSpec((1, 16 * pairs, 128), lambda i: (top - i, 0, 0)),
            pl.BlockSpec((1, pairs, STATE, PAIR), lambda i: (top - i, 0, 0, 0)),
            pl.BlockSpec((GROUP, width), block),
            pl.BlockSpec(carry.shape, lambda i: (0, 0, 0)),
            pl.BlockSpec(halo.shape, whole),
            pl.BlockSpec(memory_space=pl.ANY),
        ],
        out_specs=[
            pl.BlockSpec((GROUP, proj.shape[1]), block),
            pl.BlockSpec((8, core), whole),
            pl.BlockSpec((2 * heads, GROUP), whole),
            pl.BlockSpec(carry.shape, lambda i: (0, 0, 0)),
            pl.BlockSpec(halo.shape, whole),
        ],
        out_shape=[
            jax.ShapeDtypeStruct(proj.shape, BF16),
            jax.ShapeDtypeStruct((8, core), F32),
            jax.ShapeDtypeStruct((2 * heads, GROUP), F32),
            jax.ShapeDtypeStruct(carry.shape, F32),
            jax.ShapeDtypeStruct(halo.shape, F32),
        ],
        scratch_shapes=[
            pltpu.VMEM((GROUP, GROUP), F32),
            pltpu.VMEM((GROUP, GROUP), F32),
            pltpu.VMEM((128, 128), F32),
            pltpu.VMEM((2, GROUP, GROUP), F32),
            pltpu.VMEM((2, GROUP, GROUP), BF16),
            pltpu.VMEM((GROUP, STATE), F32),
            pltpu.VMEM((GROUP, STATE), F32),
            pltpu.VMEM((8 * heads, 128), F32),
            pltpu.VMEM((heads, PAIR), F32),
        ],
        compiler_params=pltpu.CompilerParams(vmem_limit_bytes=VMEM_LIMIT),
        input_output_aliases={} if held is None else {11: 0},
        cost_estimate=busy(12 * span, 5 * span),
        name="mix_backward",
    )(act, proj, proj, taps, heads_in, skip, table, starts, dy, carry, halo, dy if held is None else held)


def gate_sums(members_ref, seed_ref, z_ref, y_ref, gain_ref, *refs):
    parts, (w_ref, scaled_ref, sums_ref, squares, along) = refs[:-5], refs[-5:]
    step, n = pl.program_id(0), len(refs[:-5]) - 1

    @pl.when(step == 0)
    def _():
        squares[...] = jnp.zeros_like(squares)
        along[...] = jnp.zeros_like(along)
        places = list(range(n // 2)) + [n // 2] * 2 + list(range(n // 2 + 1, n))
        for k, (o, part) in enumerate(zip(places, parts)):
            at = pl.multiple_of(members_ref[o] * PAIR, PAIR)
            if k == n // 2 + 1:
                at = at + PAIR - part.shape[0]
            w_ref[pl.ds(at, part.shape[0]), :] = part[...]

    tile = z_ref.shape[1]
    scaled = nt(seed_ref[...], w_ref[pl.ds(pl.multiple_of(step * tile, tile), tile), :])
    scaled_ref[...] = scaled
    z = z_ref[...].astype(F32)
    gated = y_ref[...] * (z * sigmoid(z))
    square = gated * gated
    lean = scaled * gain_ref[...] * gated
    for cols in tiles(square.shape[1]):
        squares[...] += square[:, cols]
        along[...] += lean[:, cols]

    @pl.when(step == pl.num_programs(0) - 1)
    def _():
        spot = lanes(squares.shape)
        both = jnp.where(
            spot == 0,
            jnp.sum(squares[...], axis=1, keepdims=True),
            jnp.where(spot == 1, jnp.sum(along[...], axis=1, keepdims=True), 0.0),
        )
        sums_ref[...] = both.T[:8]


def run_gate_sums(members, seed, parts, z, y, gain):
    length, width = y.shape
    tile = 2 * PAIR
    col = pl.BlockSpec((length, tile), lambda i, t: (0, i))
    return pl.pallas_call(
        gate_sums,
        grid_spec=pltpu.PrefetchScalarGridSpec(
            num_scalar_prefetch=1,
            grid=(width // tile,),
            in_specs=[resident(seed, 2), col, col, pl.BlockSpec((1, tile), lambda i, t: (0, i))]
            + [resident(part, 2) for part in parts],
            out_specs=[
                pl.BlockSpec((width, D), lambda i, t: (0, 0)),
                col,
                pl.BlockSpec((8, length), lambda i, t: (0, 0)),
            ],
            scratch_shapes=[pltpu.VMEM((length, PAIR), F32)] * 2,
        ),
        out_shape=[
            jax.ShapeDtypeStruct((width, D), BF16),
            jax.ShapeDtypeStruct(y.shape, F32),
            jax.ShapeDtypeStruct((8, length), F32),
        ],
        compiler_params=pltpu.CompilerParams(vmem_limit_bytes=VMEM_LIMIT),
        cost_estimate=busy(11, 20),
        name="gate_sums",
    )(members, seed, z, y, gain, *parts)


def gate_back(sums_ref, scaled_ref, z_ref, y_ref, x_ref, gain_ref, mixed_ref, dy_ref, dz_ref, cols_ref, turned):
    @pl.when(pl.program_id(0) == 0)
    def _():
        inv = lax.rsqrt(sums_ref[0:1, :] / DI + EPS)
        slope = inv * inv * inv * (sums_ref[1:2, :] / DI)
        rest = jnp.zeros((PAIR - 2, sums_ref.shape[1]), F32)
        turned[...] = jnp.concatenate([inv, slope, rest], axis=0).T

    inv, slope = turned[:, 0:1], turned[:, 1:2]
    z, y, scaled, gain = z_ref[...].astype(F32), y_ref[...], scaled_ref[...], gain_ref[...]
    sig = sigmoid(z)
    silu = z * sig
    gated = y * silu
    normal = gated * inv
    mixed_ref[...] = (normal * gain).astype(BF16)
    d_gated = scaled * gain * inv - gated * slope
    dy = (d_gated * silu).astype(BF16)
    dy_ref[...] = dy
    dz_ref[...] = (d_gated * y * (sig * (1.0 + z * (1.0 - sig)))).astype(BF16)
    cols_ref[0:1, :] = jnp.sum(scaled * normal, axis=0, keepdims=True)
    cols_ref[1:2, :] = jnp.sum(dy.astype(F32) * x_ref[...].astype(F32), axis=0, keepdims=True)
    cols_ref[2:, :] = jnp.zeros_like(cols_ref[2:, :])


def run_gate_back(sums, scaled, z, y, x, gain):
    length, width = y.shape
    tile = PAIR
    col = pl.BlockSpec((length, tile), lambda i: (0, i))
    low = jax.ShapeDtypeStruct(y.shape, BF16)
    return pl.pallas_call(
        gate_back,
        grid=(width // tile,),
        in_specs=[
            pl.BlockSpec(sums.shape, lambda i: (0, 0)),
            col,
            col,
            col,
            col,
            pl.BlockSpec((1, tile), lambda i: (0, i)),
        ],
        out_specs=[col, col, col, pl.BlockSpec((8, tile), lambda i: (0, i))],
        out_shape=[low, low, low, jax.ShapeDtypeStruct((8, width), F32)],
        scratch_shapes=[pltpu.VMEM((length, PAIR), F32)],
        compiler_params=pltpu.CompilerParams(vmem_limit_bytes=VMEM_LIMIT),
        cost_estimate=busy(11, 20),
        name="gate_back",
    )(sums, scaled, z, y, x, gain)


def back_norm(members_ref, tokens_ref, dz_ref, dx_ref, *refs):
    parts, (dn_ref, gain_ref) = refs[:-2], refs[-2:]
    count = len(parts) // 2

    @pl.when(pl.program_id(0) == 0)
    def _():
        gain_ref[...] = jnp.zeros_like(gain_ref)

    tokens = tokens_ref[...].astype(F32)
    inv = lax.rsqrt(jnp.mean(tokens * tokens, axis=-1, keepdims=True) + EPS)
    sums = [None] * (D // SEG)
    for source, weights in ((dz_ref, parts[:count]), (dx_ref, parts[count:])):
        for o, at, w in by_segments(weights):
            part = nn(source[:, at : at + w.shape[0]], w[...])
            sums[o] = part if sums[o] is None else sums[o] + part
    for o, d_normed in enumerate(sums):
        at = pl.multiple_of(members_ref[o] * SEG, SEG)
        dn_ref[:, pl.ds(at, SEG)] = d_normed.astype(BF16)
        scaled = tokens_ref[:, pl.ds(at, SEG)].astype(F32) * inv
        gain_ref[0:1, pl.ds(at, SEG)] += jnp.sum(d_normed * scaled, axis=0, keepdims=True)


def run_back_norm(members, tokens, dz, dx, weights_z, weights_x):
    length = tokens.shape[0]
    row = lambda i, t: (i, 0)
    return pl.pallas_call(
        back_norm,
        grid_spec=pltpu.PrefetchScalarGridSpec(
            num_scalar_prefetch=1,
            grid=(length // GROUP,),
            in_specs=[
                pl.BlockSpec((GROUP, D), row),
                pl.BlockSpec((GROUP, dz.shape[1]), row),
                pl.BlockSpec((GROUP, dx.shape[1]), row),
            ]
            + [resident(w, 2) for w in weights_z + weights_x],
            out_specs=[pl.BlockSpec((GROUP, D), row), pl.BlockSpec((8, D), lambda i, t: (0, 0))],
        ),
        out_shape=[
            jax.ShapeDtypeStruct((length, D), BF16),
            jax.ShapeDtypeStruct((8, D), F32),
        ],
        compiler_params=pltpu.CompilerParams(vmem_limit_bytes=VMEM_LIMIT),
        cost_estimate=busy(18, 24),
        name="back_norm",
    )(members, tokens, dz, dx, *weights_z, *weights_x)


def put_pairs(place_ref, refs, out_ref, g):
    m = len(refs)
    for k, ref in enumerate(refs):
        to = pl.multiple_of((place_ref[0] ^ k) * PAIR, PAIR)
        out_ref[pl.ds(to, PAIR), :] = ref[pl.ds(pl.multiple_of(g * PAIR, PAIR), PAIR), :].astype(F32)


def assemble_z(place_ref, z0, z1, z2, z3, out_ref):
    put_pairs(place_ref, (z0, z1, z2, z3), out_ref, pl.program_id(0))


def assemble_a(place_ref, held_ref, a0, a1, a2, a3, out_ref):
    put_pairs(place_ref, (a0, a1, a2, a3), out_ref, pl.program_id(0))


def assemble_b(place_ref, order_ref, held_ref, b0, b1, b2, b3, out_ref):
    step, last = pl.program_id(0), pl.num_programs(0) - 1
    refs = (b0, b1, b2, b3)
    width = last * PAIR
    core = width + 2 * STATE

    @pl.when(step < last)
    def _():
        put_pairs(place_ref, refs, out_ref, step)

    @pl.when(step == last)
    def _():
        total = jnp.zeros((2 * STATE, out_ref.shape[1]), F32)
        steps = jnp.zeros((HEADS, out_ref.shape[1]), F32)
        for k, x in enumerate(refs):
            total = total + x[width:core].astype(F32)
            steps = steps + nn(order_ref[place_ref[0] ^ k], x[core : core + PAIR])
        out_ref[: 2 * STATE] = total
        out_ref[2 * STATE : 2 * STATE + HEADS] = steps


def run_assemble_z(place, shares, columns):
    m, rows = len(shares), shares[0].shape[1]
    tile = m * PAIR
    return pl.pallas_call(
        assemble_z,
        grid_spec=pltpu.PrefetchScalarGridSpec(
            num_scalar_prefetch=1,
            grid=(DI // tile,),
            in_specs=[resident(s, 2) for s in shares],
            out_specs=pl.BlockSpec((tile, rows), lambda i, t: (i, 0)),
        ),
        out_shape=jax.ShapeDtypeStruct((columns, rows), F32),
        compiler_params=pltpu.CompilerParams(vmem_limit_bytes=VMEM_LIMIT),
        cost_estimate=busy(4, 6),
        name="assemble_z",
    )(place, *shares)


def run_assemble_b(place, order, held, shares, count):
    m, rows = len(shares), shares[0].shape[1]
    tile = m * PAIR
    first = 2 * (DI // tile) - count
    return pl.pallas_call(
        assemble_b,
        grid_spec=pltpu.PrefetchScalarGridSpec(
            num_scalar_prefetch=1,
            grid=(count + 1,),
            in_specs=[resident(order, 2), pl.BlockSpec(memory_space=pl.ANY)]
            + [resident(s, 2) for s in shares],
            out_specs=pl.BlockSpec((tile, rows), lambda i, t: (i + first, 0)),
        ),
        out_shape=jax.ShapeDtypeStruct(held.shape, F32),
        input_output_aliases={2: 0},
        compiler_params=pltpu.CompilerParams(vmem_limit_bytes=VMEM_LIMIT),
        cost_estimate=busy(3, 2),
        name="assemble_b",
    )(place, order, held, *shares)


def run_assemble_a(place, held, shares):
    m, rows = len(shares), shares[0].shape[1]
    tile = m * PAIR
    return pl.pallas_call(
        assemble_a,
        grid_spec=pltpu.PrefetchScalarGridSpec(
            num_scalar_prefetch=1,
            grid=(shares[0].shape[0] // PAIR,),
            in_specs=[pl.BlockSpec(memory_space=pl.ANY)] + [resident(s, 2) for s in shares],
            out_specs=pl.BlockSpec((tile, rows), lambda i, t: (i + DI // tile, 0)),
        ),
        out_shape=jax.ShapeDtypeStruct(held.shape, F32),
        input_output_aliases={1: 0},
        compiler_params=pltpu.CompilerParams(vmem_limit_bytes=VMEM_LIMIT),
        cost_estimate=busy(4, 5),
        name="assemble_a",
    )(place, held, *shares)


def body(
    tokens, norm_gain, w_in, conv_w, conv_b, dt_bias, a_log, d_skip, gate_gain, w_out, cotangent
):
    n, m = lax.axis_size("fsdp"), lax.axis_size("ctx")
    place = lax.axis_index("ctx")
    piece = tokens.shape[1]
    length = piece * m
    blocks = length // GROUP
    pairs = DI // PAIR // m
    width = pairs * PAIR
    heads = 2 * pairs
    rows = w_in.shape[0]
    core_cols = width + 2 * STATE
    head_cols = core_cols + heads
    ring = rows == SEG and (DI // PAIR) // n == m

    def of_pairs(array, axis):
        shape = array.shape
        each = shape[axis] // (pairs * m)
        split = array.reshape(shape[:axis] + (pairs, m, each) + shape[axis + 1 :])
        mine = lax.dynamic_index_in_dim(split, place, axis + 1, False)
        return mine.reshape(shape[:axis] + (pairs * each,) + shape[axis + 1 :])

    def of_heads(array):
        mine = of_pairs(array, 0)
        split = mine.reshape((pairs, 2) + mine.shape[1:]).swapaxes(0, 1)
        return split.reshape(mine.shape)

    all_tokens = lax.all_gather(tokens[0], "ctx", axis=0, tiled=True)
    seed = lax.all_gather(cotangent[0], "ctx", axis=0, tiled=True)

    dt_bias_own, a_log_own = of_heads(dt_bias), of_heads(a_log)
    skip_own = of_pairs(d_skip, 0)
    a_neg = -jnp.exp(a_log_own)
    heads_in = jnp.broadcast_to(jnp.concatenate([dt_bias_own, a_neg])[:, None], (2 * heads, 128))
    skip_row = jnp.repeat(skip_own, HEADDIM)[None, :]

    columns = w_in.T
    total_cols = core_cols + PAIR
    cut = halves(total_cols)[0]
    place_ref = place.reshape(1).astype(jnp.int32)
    smalls = [norm_gain[None], gate_gain[None], conv_b[None], conv_w]
    small_rows = [-(-v.shape[1] // SEG) for v in smalls]

    def split(whole):
        upper, _ = halves(whole.shape[0])
        parts = [whole[:, o * SEG : (o + 1) * SEG] for o in range(D // SEG)]
        middle = parts[len(parts) // 2]
        return parts[: len(parts) // 2] + [middle[:upper], middle[upper:]] + parts[len(parts) // 2 + 1 :]

    if ring:
        me = ring_place(lax.axis_index("fsdp"), n)
        members = ring_member(me + jnp.arange(n), n).astype(jnp.int32)
        padded = [jnp.pad(v, ((0, 0), (0, k * SEG - v.shape[1]))) for v, k in zip(smalls, small_rows)]
        small = jnp.concatenate([v.reshape(-1) for v in padded]).reshape(-1, SEG)
        block_x, block_z, block_o = run_pack(place_ref, columns, w_out, small, pairs)
        ring_x, ring_z, ring_o = Gather(block_x, n), Gather(block_z, n), Gather(block_o, n)
        next_hop([ring_x], (), heads_in, skip_row)
        for _ in range(n // 2 - 3):
            next_hop([ring_x], ())
        next_hop([ring_x, ring_z], ())
        next_hop([ring_x], (), *arrivals(ring_z))
        parts_x = ring_x.parts()
        all_tokens = next_hop([ring_z, ring_o], all_tokens, *arrivals(ring_x))
    else:
        members = jnp.arange(D // SEG, dtype=jnp.int32)
        block_x = jnp.concatenate(
            [
                of_pairs(columns[DI : 2 * DI], 0),
                columns[2 * DI : 2 * DI + 2 * STATE],
                of_heads(columns[DI + CONV :]),
                jnp.zeros((PAIR - heads, rows), BF16),
            ],
            axis=0,
        )
        whole_x = lax.all_gather(block_x, "fsdp", axis=1, tiled=True)
        norm_whole = lax.all_gather(norm_gain[None], "fsdp", axis=1, tiled=True)
        at = core_cols + SMALL
        whole_x = jnp.concatenate([whole_x[:at], norm_whole, whole_x[at + 1 :]], axis=0)
        parts_x, parts_z = split(whole_x), split(lax.all_gather(of_pairs(columns[:DI], 0), "fsdp", axis=1, tiled=True))
        w_o = of_pairs(lax.all_gather(w_out, "fsdp", axis=0, tiled=True), 0)
        parts_o = [w_o[o * PAIR : (o + 1) * PAIR] for o in range(pairs)]
        middle, upper = parts_o[pairs // 2], halves(PAIR)[0]
        parts_o = parts_o[: pairs // 2] + [middle[:upper], middle[upper:]] + parts_o[pairs // 2 + 1 :]

    if ring:
        kept = run_collect(members, parts_x)
        spans, at = [], 0
        for v, each in zip(smalls, small_rows):
            here = kept[:, at : at + v.shape[0] * each].reshape(n, v.shape[0], each * SEG)
            spans.append(here[:, :, : v.shape[1]].transpose(1, 0, 2).reshape(v.shape[0], -1))
            at += v.shape[0] * each
        norm_full, gate_full, bias_full, taps_full = spans
    else:
        norm_full, gate_full, bias_full, taps_full = (
            lax.all_gather(v, "fsdp", axis=1, tiled=True).astype(F32) for v in smalls
        )
    gate_full = of_pairs(gate_full, 1)
    taps_full = jnp.concatenate([taps_full, bias_full], axis=0)
    taps = jnp.concatenate([of_pairs(taps_full[:, :DI], 1), taps_full[:, DI:]], axis=1)
    taps = jnp.pad(taps, ((0, 8 - KW - 1), (0, 0)))

    normed, proj_x = run_front(members, all_tokens, parts_x)
    if ring:
        proj_x = next_hop([ring_z, ring_o], proj_x, *arrivals(ring_z, ring_o))
    act, table, ssd, starts = run_mix_forward(proj_x, taps, heads_in, skip_row, pairs)
    normed_z = normed
    if ring:
        for _ in range(n // 2 - 3):
            next_hop([ring_z, ring_o], (), ssd, *arrivals(ring_z, ring_o))
        normed_z = next_hop([ring_o], normed, *arrivals(ring_z))
        parts_z, parts_o = ring_z.parts(), ring_o.parts()
    proj_z = run_project(normed_z, parts_z)

    w_o, scaled, sums = run_gate_sums(members, seed, parts_o, proj_z, ssd, gate_full)
    sums = ctx_sum(sums, m)
    mixed, dy, d_z, gate_cols = run_gate_back(sums, scaled, proj_z, ssd, act, gate_full)

    grads_o = tn(mixed, seed).astype(BF16)
    carry = jnp.zeros((pairs, STATE, PAIR), F32)
    halo = jnp.zeros((HALO, core_cols), F32)
    conv_grads, head_grads, top, d_x, d_z_late, mixed_late = [], [], blocks - 1, None, d_z, mixed
    if ring:
        sum_o = Reduce(lambda o: lax.dynamic_slice_in_dim(grads_o, members[o] * PAIR, PAIR, 0), n)
        d_z_late, mixed_late = next_hop([sum_o], (d_z, mixed))
    grads_z = tn(d_z_late, normed).astype(BF16)
    branch = nn(mixed_late, w_o).astype(BF16)
    if ring:
        sum_z = Reduce(lambda o: grads_z[:, o * SEG : (o + 1) * SEG], n)
    for at in range(2):
        if ring:
            sum_o.join()
            if at > 0:
                sum_z.join()
                branch_own.middle()
                dy, carry, branch_own.sent = next_hop(
                    [sum_o, sum_z], (dy, carry, branch_own.sent)
                )
                branch_own.send_far()
            else:
                dy, carry, branch = next_hop([sum_o, sum_z], (dy, carry, branch))
                branch_own = CtxReduce(branch.reshape(m, piece, D), m)
        span = blocks // 2
        d_x, conv_part, head_part, carry, halo = run_mix_backward(
            span, top, act, proj_x, taps, heads_in, skip_row, table, starts, dy, carry, halo, d_x
        )
        conv_grads.append(conv_part)
        head_grads.append(head_part)
        top -= span
    normed_late = normed
    if ring:
        sum_o.join()
        sum_z.join()
        d_x, normed_late, conv_grads, head_grads, gate_cols, branch_own.far = next_hop(
            [sum_o, sum_z], (d_x, normed, conv_grads, head_grads, gate_cols, branch_own.far)
        )
    else:
        branch_own = CtxReduce(branch.reshape(m, piece, D), m)
        branch_own.middle()
        branch_own.send_far()
    grads_x = tn(d_x, normed_late).astype(BF16)
    d_normed, d_gain = run_back_norm(
        members, all_tokens, d_z, after(d_x, grads_x), parts_z, parts_x
    )
    if ring:
        part_o = sum_o.join().astype(BF16)
        sum_z.join()
        sum_a = Reduce(lambda o: grads_x[:cut, o * SEG : (o + 1) * SEG], n)
        sum_b = Reduce(lambda o: grads_x[cut:, o * SEG : (o + 1) * SEG], n)
        d_normed, d_gain, part_o, conv_grads, head_grads, gate_cols, branch_own.far = next_hop(
            [sum_a, sum_b, sum_z],
            (d_normed, d_gain, part_o, conv_grads, head_grads, gate_cols, branch_own.far),
        )
    d_own = CtxReduce(d_normed.reshape(m, piece, D), m)
    d_own.middle()
    d_own.send_far()

    head_sums = jnp.sum(head_grads[0] + head_grads[1], axis=1)
    d_skip_own = jnp.sum(gate_cols[1].reshape(pairs, 2, HEADDIM), axis=2).T.reshape(heads)
    per_head = jnp.concatenate([head_sums[:heads], head_sums[heads:] * a_neg, d_skip_own])
    conv_grads = (conv_grads[0] + conv_grads[1])[: KW + 1]
    lines = [conv_grads, gate_cols[0:1], d_gain[0:1], per_head[None]]
    wide = max(line.shape[1] for line in lines)
    small = jnp.concatenate(
        [jnp.pad(line, ((0, 0), (0, wide - line.shape[1]))) for line in lines], axis=0
    )
    flip = 1
    steps = []
    while flip < n:
        steps.append(flip)
        flip *= 2

    def small_step(small):
        if steps:
            small = small + lax.ppermute(small, "fsdp", ctx_route(n, steps.pop()))
        return small

    small = small_step(small)
    if ring:
        sum_a.join()
        sum_b.join()
        part_z = sum_z.join().astype(BF16)
        d_own.far, small, part_o, part_z, branch_own.far = next_hop(
            [sum_a, sum_b], (d_own.far, small, part_o, part_z, branch_own.far)
        )
        other_o = far_share(part_o, m)
    small = small_step(small)
    output = (tokens[0].astype(F32) + branch_own.total()).astype(BF16)[None]
    if ring:
        sum_a.join()
        sum_b.join()
        small, other_o, part_z, d_own.far = next_hop(
            [sum_a, sum_b], (small, other_o, part_z, d_own.far), output
        )
        shares_o, other_z = near_share(part_o, other_o, m), far_share(part_z, m)
    while steps:
        small = small_step(small)
    own = tokens[0].astype(F32)
    inv = lax.rsqrt(jnp.mean(own * own, axis=-1, keepdims=True) + EPS)
    d_direct = d_own.total() * norm_full
    along = jnp.mean(d_direct * own, axis=-1, keepdims=True)
    grad_tokens = (cotangent[0].astype(F32) + d_direct * inv - own * (inv * inv * inv * along))[None]
    if ring:
        for at in range(n // 2 - 3):
            sum_a.join()
            sum_b.join()
            small, shares_o, part_z, other_z = next_hop(
                [sum_a, sum_b], (small, shares_o, part_z, other_z), grad_tokens
            )
    smalls_of = ctx_share(small, m)
    by_place = jnp.zeros((m,) + small.shape, F32)
    for k in range(m):
        by_place = lax.dynamic_update_slice(by_place, smalls_of[k][None], (place ^ k, 0, 0))
    mine = lax.axis_index("fsdp")

    def own_columns(rows_first, rows_last, extra):
        part = by_place[:, rows_first:rows_last, :width].reshape(m, -1, pairs, PAIR)
        whole = part.transpose(1, 2, 0, 3).reshape(-1, DI)
        if extra:
            shared = jnp.sum(by_place[:, rows_first:rows_last, width:core_cols], axis=0)
            whole = jnp.concatenate([whole, shared], axis=1)
        each = whole.shape[1] // n
        return lax.dynamic_slice_in_dim(whole, mine * each, each, 1)

    grad_conv = own_columns(0, KW + 1, True)
    grad_conv_w, grad_conv_b = grad_conv[:KW], grad_conv[KW]
    grad_gate_gain = own_columns(KW + 1, KW + 2, False)[0]
    grad_gain = jnp.sum(by_place[:, KW + 2, :D], axis=0)
    grad_gain = lax.dynamic_slice_in_dim(grad_gain, mine * rows, rows, 0)
    per_head = by_place[:, KW + 3, : 3 * heads]
    per_head = per_head.reshape(m, 3, 2, pairs).transpose(1, 3, 0, 2).reshape(3, HEADS)
    small_outputs = (grad_gain, grad_conv_w, grad_conv_b, per_head, grad_gate_gain)
    if ring:
        shares_z = near_share(part_z, other_z, m)
        held = run_assemble_z(place_ref, shares_z, w_in.shape[1])
        grad_w_out = jnp.zeros((m, PAIR, D), F32)
        for k in range(m):
            grad_w_out = lax.dynamic_update_slice(
                grad_w_out, shares_o[k].astype(F32)[None], (place ^ k, 0, 0)
            )
        grad_w_out = grad_w_out.reshape(w_out.shape)
        part_b, part_a = sum_b.join().astype(BF16), sum_a.join().astype(BF16)
        part_a, part_b, held, small_outputs = barrier((part_a, part_b, held, small_outputs), grad_w_out)
    else:
        part_z = lax.psum_scatter(grads_z.astype(F32), "fsdp", scatter_dimension=1, tiled=True)
        part_x = lax.psum_scatter(grads_x.astype(F32), "fsdp", scatter_dimension=1, tiled=True)
        whole_o = jnp.zeros((pairs, m, PAIR, D), F32)
        whole_o = lax.dynamic_update_index_in_dim(
            whole_o, grads_o.astype(F32).reshape(pairs, PAIR, D), place, 1
        )
        grad_w_out = lax.psum_scatter(whole_o.reshape(DI, D), "fsdp", scatter_dimension=0, tiled=True)
        grad_w_out = lax.psum(grad_w_out, "ctx")
        held = run_assemble_z(place_ref, ctx_share(part_z.astype(BF16), m), w_in.shape[1])
        part_a, part_b = part_x[:cut].astype(BF16), part_x[cut:].astype(BF16)
    other_b, other_a = far_share(part_b, m), far_share(part_a, m)
    grad_gain, grad_conv_w, grad_conv_b, per_head, grad_gate_gain = small_outputs
    order = np.zeros((m, HEADS, PAIR), np.float32)
    for member in range(m):
        for h in range(heads):
            order[member, (h % pairs) * 2 * m + 2 * member + h // pairs, h] = 1.0
    shares_b = near_share(part_b, other_b, m)
    held = run_assemble_b(place_ref, jnp.asarray(order, BF16), held, shares_b, pairs - cut // PAIR)
    shares_a = near_share(part_a, other_a, m)
    grad_w_in = run_assemble_a(place_ref, held, shares_a)
    return (
        output,
        grad_tokens,
        grad_gain,
        grad_w_in.T,
        grad_conv_w,
        grad_conv_b,
        per_head[0],
        per_head[1],
        per_head[2],
        grad_gate_gain,
        grad_w_out,
    )


def solution(mesh):
    in_specs = (
        P("fsdp", "ctx", None),
        P("fsdp"),
        P("fsdp", None),
        P(None, "fsdp"),
        P("fsdp"),
        P(),
        P(),
        P(),
        P("fsdp"),
        P("fsdp", None),
        P("fsdp", "ctx", None),
    )
    out_specs = (
        P("fsdp", "ctx", None),
        P("fsdp", "ctx", None),
        P("fsdp"),
        P("fsdp", None),
        P(None, "fsdp"),
        P("fsdp"),
        P(),
        P(),
        P(),
        P("fsdp"),
        P("fsdp", None),
    )
    return jax.shard_map(body, mesh=mesh, in_specs=in_specs, out_specs=out_specs, check_vma=False)
```

time: 545 us -> 496 us (0.910)
  local copies, waits for them, and re-layouts: 57.7 us -> 33.9 us
  between operations: 36.2 us -> 20.6 us
  other arithmetic: 48.2 us -> 41 us
  starting transfers between devices: 82.8 us -> 88.8 us
    ppermute x54 -> x56, waiting for transfers between devices: 81.1 us -> 108 us  [send(): return lax.ppermute(block, 'fsdp', route)]
    ppermute x5 -> x3, waiting for transfers between devices: 17.6 us -> 2.9 us  [small_step(): small = small + lax.ppermute(small, 'fsdp', ctx_route(n, steps.pop()))]
    ppermute x2, waiting for transfers between devices: 18 us -> 3.94 us  [send_far(): self.far = lax.ppermute(self.sent, 'ctx', ctx_route(self.m, 2))]
    pallas_call x2 -> x5, Pallas kernels: 17.9 us -> 27.2 us  [the longest x1 14.4 us: run_gate_sums(): pl.pallas_call(gate_sums, grid_spec=pltpu.PrefetchScalarGridSpec(num_scal...]
    pallas_call x3 -> x2, Pallas kernels: 49.3 us -> 40.6 us  [run_mix_backward(): pl.pallas_call(lambda *refs: mix_backward(top, *refs), grid=(span,), in_s...]
    ppermute x4 -> x5, starting transfers between devices: 3.64 us -> 12.2 us  [near_share(): far = lax.ppermute(other, 'ctx', ctx_route(m, 1))]
    unnamed x121 -> x104, local copies, waits for them, and re-layouts: 14.2 us -> 7.49 us
    dynamic_update_slice x14 -> x4, local copies, waits for them, and re-layouts: 8.76 us -> 2.27 us  [body(): lax.dynamic_update_slice(by_place, smalls_of[k][None], (place ^ k, 0, 0))]
  transfers between devices with their start and end apart: 79 -> 82, of which waited for: 29 -> 32; matrix products, arithmetic and copies ran while one was open for 20% -> 15% of each run, Pallas kernels for 21% -> 22%
where the time goes in v2:
time: 496 us; the launch traced here: 489 us
  Pallas kernels  143 us (29%)
  waiting for transfers between devices  137 us (28%)
  starting transfers between devices  88.8 us (18%)
  other arithmetic  41 us (8%)
  local copies, waits for them, and re-layouts  33.9 us (7%)
  matrix products  24.5 us (5%)
  between operations  20.6 us (4%)
    ppermute x56, waiting for transfers between devices, send(): return lax.ppermute(block, 'fsdp', route)  108 us
    ppermute x56, starting transfers between devices, send(): return lax.ppermute(block, 'fsdp', route)  43.5 us
    pallas_call x2, Pallas kernels, run_mix_backward(): pl.pallas_call(lambda *refs: mix_backward(top, *refs), grid=(span,), in_s...  40.6 us
    ppermute x5, waiting for transfers between devices, far_share(): return lax.ppermute(block, 'ctx', ctx_route(m, 2))  20.6 us
    dot_general x3, matrix products, tn(): lax.dot_general(a, b, (((0,), (0,)), ((), ())), preferred_element_type=F32)  19.8 us
    pallas_call x1, Pallas kernels, run_mix_forward(): pl.pallas_call(mix_forward, grid=(blocks,), in_specs=[pl.BlockSpec((GROUP...  19.1 us
    pallas_call x1, Pallas kernels, run_back_norm(): pl.pallas_call(back_norm, grid_spec=pltpu.PrefetchScalarGridSpec(num_scal...  18.3 us
    pallas_call x1, Pallas kernels, run_gate_sums(): pl.pallas_call(gate_sums, grid_spec=pltpu.PrefetchScalarGridSpec(num_scal...  14.4 us
  transfers between devices with their start and end apart: 82, of which 32 were waited for; matrix products, arithmetic and copies ran while one was open for 15% of the time, Pallas kernels for 22%

profile of v2, /device:TPU:1, one launch (start us, length us, event | category | flops | bytes accessed | tf_op | source)
XLA Modules:
  0.0 489.0 jit_solution(4007958574194078777)
XLA Ops:
  20.6 16.1 %collective-permute-done.refs_8_.refs_7_.refs_17_ = bf16[1408,256]{1,0:T(8,128)(2,1)S(1)} collective-permute-done((bf16[1408,256]{1,0:T(8,128)(2,1)}, bf16[1408,256]{1,0:T(8,128)(2,1)S(1)}, u32[]{:S(2)}, u32[]{:S(2)}) %collective-permute-start) | collective-permute-done | bytes 720928 | tf_op jit(solution)/shard_map/ppermute | solution.py:43
  39.1 14.5 %collective-permute-done.2.refs_7_.refs_6_.refs_16_ = bf16[1408,256]{1,0:T(8,128)(2,1)} collective-permute-done((bf16[1408,256]{1,0:T(8,128)(2,1)S(1)}, bf16[1408,256]{1,0:T(8,128)(2,1)}, u32[]{:S(2)}, u32[]{:S(2)}) %collective-permute-start.2) | collective-permute-done | bytes 720928 | tf_op jit(solution)/shard_map/ppermute | solution.py:43
  58.4 12.2 %collective-permute-done.6.refs_6_.refs_5_.refs_15_ = bf16[1408,256]{1,0:T(8,128)(2,1)S(1)} collective-permute-done((bf16[1408,256]{1,0:T(8,128)(2,1)}, bf16[1408,256]{1,0:T(8,128)(2,1)S(1)}, u32[]{:S(2)}, u32[]{:S(2)}) %collective-permute-start.6) | collective-permute-done | bytes 720928 | tf_op jit(solution)/shard_map/ppermute | solution.py:43
  72.3 9.4 %collective-permute-done.4.refs_8_ = bf16[1024,256]{1,0:T(8,128)(2,1)} collective-permute-done((bf16[1024,256]{1,0:T(8,128)(2,1)}, bf16[1024,256]{1,0:T(8,128)(2,1)}, u32[]{:S(2)}, u32[]{:S(2)}) %collective-permute-start.4) | collective-permute-done | bytes 524320 | tf_op jit(solution)/shard_map/ppermute | solution.py:43
  97.8 12.8 %front.1 = (bf16[1024,2048]{1,0:T(8,128)(2,1)}, bf16[1024,1408]{1,0:T(8,128)(2,1)}) custom-call(s32[8]{0:T(128)} %compare_select_fusion.2.members_ref, bf16[1024,2048]{1,0:T(8,128)(2,1)} %bitcast.149, bf16[1408,256]{1,0:T(8,128)(2,1)} %get-tuple-element.148.refs_0_.refs_9_, bf16[1408,256]{1,0:T(8,128)(2,1)} %copy-done.17, bf16[1408,256]{1,0:T(8,128)(2,1)} %copy-done.18, ...), custom_call_target="tpu_custom_call" | custom-call | flops 12000000000 | bytes 18000000 | tf_op jit(solution)/shard_map/front/pallas_call | solution.py:345
  118.5 19.1 %mix_forward.1 = (bf16[1024,1280]{1,0:T(8,128)(2,1)}, f32[4,128,128]{2,1,0:T(8,128)}, f32[1024,1024]{1,0:T(8,128)}, f32[4,8,128,128]{3,2,1,0:T(8,128)}) custom-call(bf16[1024,1408]{1,0:T(8,128)(2,1)} %get-tuple-element.169.proj_ref.refs_1_.refs_2_, f32[8,1280]{1,0:T(8,128)} %pad.26.taps_ref.refs_3_, f32[32,128]{1,0:T(8,128)} %broadcast_in_dim.74.heads_ref.refs_4_, ...), custom_call_target="tpu_custom_call" | custom-call | flops 17999998976 | bytes 15000000 | tf_op jit(solution)/shard_map/mix_forward/pallas_call | solution.py:497
  142.2 5.8 %collective-permute-done.18.refs_6_ = bf16[128,2048]{1,0:T(8,128)(2,1)S(1)} collective-permute-done((bf16[128,2048]{1,0:T(8,128)(2,1)}, bf16[128,2048]{1,0:T(8,128)(2,1)S(1)}, u32[]{:S(2)}, u32[]{:S(2)}) %collective-permute-start.18) | collective-permute-done | bytes 524320 | tf_op jit(solution)/shard_map/ppermute | solution.py:43
  154.3 8.6 %project.1.z_ref = bf16[1024,1024]{1,0:T(8,128)(2,1)} custom-call(bf16[1024,2048]{1,0:T(8,128)(2,1)} %get-tuple-element.216.normed_ref, bf16[1024,256]{1,0:T(8,128)(2,1)} %get-tuple-element.153.refs_0_, bf16[1024,256]{1,0:T(8,128)(2,1)} %collective-permute-done.5.refs_1_, bf16[1024,256]{1,0:T(8,128)(2,1)} %copy-done.37, bf16[1024,256]{1,0:T(8,128)(2,1)} %copy-done.28, ...), custom_call_target="tpu_custom_call" | custom-call | flops 8000000000 | bytes 10000000 | tf_op jit(solution)/shard_map/project/pallas_call | solution.py:376
  163.7 14.4 %gate_sums.1 = (bf16[1024,2048]{1,0:T(8,128)(2,1)}, f32[1024,1024]{1,0:T(8,128)}, f32[8,1024]{1,0:T(8,128)}) custom-call(s32[8]{0:T(128)} %compare_select_fusion.2.members_ref, bf16[1024,2048]{1,0:T(8,128)(2,1)} %bitcast.151, bf16[1024,1024]{1,0:T(8,128)(2,1)} %project.1.z_ref, f32[1024,1024]{1,0:T(8,128)} %get-tuple-element.170.y_ref, ...), custom_call_target="tpu_custom_call" | custom-call | flops 11000000512 | bytes 20000000 | tf_op jit(solution)/shard_map/gate_sums/pallas_call | solution.py:767
  178.1 12.1 %collective-permute-start.24 = (f32[8,1024]{1,0:T(8,128)}, f32[8,1024]{1,0:T(8,128)S(1)}, u32[]{:S(2)}, u32[]{:S(2)}) collective-permute-start(f32[8,1024]{1,0:T(8,128)} %get-tuple-element.179), channel_id=1, source_target_pairs={{0,1},{1,0},{2,3},{3,2},{4,5},{5,4},{6,7},{7,6},{8,9},{9,8},{10,11... | collective-permute-start | bytes 98312 | tf_op jit(solution)/shard_map/ppermute | solution.py:165
  199.8 11.5 %gate_back.1 = (bf16[1024,1024]{1,0:T(8,128)(2,1)}, bf16[1024,1024]{1,0:T(8,128)(2,1)}, bf16[1024,1024]{1,0:T(8,128)(2,1)}, f32[8,1024]{1,0:T(8,128)}) custom-call(f32[8,1024]{1,0:T(8,128)} %add.270.sums_ref, f32[1024,1024]{1,0:T(8,128)} %get-tuple-element.180.scaled_ref, bf16[1024,1024]{1,0:T(8,128)(2,1)} %project.1.z_ref, ...), custom_call_target="tpu_custom_call" | custom-call | flops 11000000512 | bytes 20000000 | tf_op jit(solution)/shard_map/gate_back/pallas_call | solution.py:821
  211.4 6.6 %convolution_convert_fusion.3 = bf16[1024,2048]{1,0:T(8,128)(2,1)S(1)} fusion(bf16[1024,1024]{1,0:T(8,128)(2,1)} %get-tuple-element.188, bf16[1,1024,2048]{2,1,0:T(8,128)(2,1)S(1)} %copy-done.35), kind=kOutput, calls=%fused_computation.5 | convolution fusion | flops 4297064448 | bytes 10485760 | tf_op jit(solution)/shard_map/dot_general | solution.py:178
  218.1 4.9 %convolution_convert_fusion.2 = bf16[1024,2048]{1,0:T(8,128)(2,1)S(1)} fusion(bf16[1024,1024]{1,0:T(8,128)(2,1)S(1)} %copy-done.46, bf16[1024,2048]{1,0:T(8,128)(2,1)S(1)} %copy-done.44), kind=kOutput, calls=%fused_computation.4 | convolution fusion | flops 4297064448 | bytes 10485760 | tf_op jit(solution)/shard_map/dot_general | solution.py:178
  239.2 20.3 %mix_backward.2 = (bf16[1024,1408]{1,0:T(8,128)(2,1)}, f32[8,1280]{1,0:T(8,128)}, f32[32,256]{1,0:T(8,128)}, f32[8,128,128]{2,1,0:T(8,128)}, f32[8,1280]{1,0:T(8,128)}) custom-call(bf16[1024,1280]{1,0:T(8,128)(2,1)} %get-tuple-element.181.x_ref.refs_0_, bf16[1024,1408]{1,0:T(8,128)(2,1)} %get-tuple-element.169.proj_ref.refs_1_.refs_2_, ...), custom_call_target="tpu_custom_call" | custom-call | flops 24000000000 | bytes 10000000 | tf_op jit(solution)/shard_map/mix_backward/pallas_call | solution.py:677
  270.4 20.3 %mix_backward.3 = (bf16[1024,1408]{1,0:T(8,128)(2,1)}, f32[8,1280]{1,0:T(8,128)}, f32[32,256]{1,0:T(8,128)}, f32[8,128,128]{2,1,0:T(8,128)}, f32[8,1280]{1,0:T(8,128)}) custom-call(bf16[1024,1280]{1,0:T(8,128)(2,1)} %get-tuple-element.181.x_ref.refs_0_, ...), custom_call_target="tpu_custom_call", output_to_operand_aliasing={{0}: (11, {})} | custom-call | flops 24000000000 | bytes 10000000 | tf_op jit(solution)/shard_map/mix_backward/pallas_call | solution.py:677
  298.2 8.3 %convolution_convert_fusion = bf16[1408,2048]{1,0:T(8,128)(2,1)S(1)} fusion(bf16[1024,1408]{1,0:T(8,128)(2,1)} %get-tuple-element.219.dx_ref, bf16[1024,2048]{1,0:T(8,128)(2,1)S(1)} %copy-done.45), kind=kOutput, calls=%fused_computation | convolution fusion | flops 5908463616 | bytes 12845056 | tf_op jit(solution)/shard_map/dot_general | solution.py:178
  308.1 18.3 %back_norm.1 = (bf16[1024,2048]{1,0:T(8,128)(2,1)}, f32[8,2048]{1,0:T(8,128)}) custom-call(s32[8]{0:T(128)} %compare_select_fusion.2.members_ref, bf16[1024,2048]{1,0:T(8,128)(2,1)} %bitcast.150, bf16[1024,1024]{1,0:T(8,128)(2,1)} %get-tuple-element.186.dz_ref, bf16[1024,1408]{1,0:T(8,128)(2,1)} %get-tuple-element.219.dx_ref, ...), custom_call_target="tpu_custom_call" | custom-call | flops 17999998976 | bytes 24000000 | tf_op jit(solution)/shard_map/back_norm/pallas_call | solution.py:866
  353.9 5.3 %collective-permute-done.42 = bf16[384,256]{1,0:T(8,128)(2,1)S(1)} collective-permute-done((bf16[384,256]{1,0:T(8,128)(2,1)}, bf16[384,256]{1,0:T(8,128)(2,1)S(1)}, u32[]{:S(2)}, u32[]{:S(2)}) %collective-permute-start.42) | collective-permute-done | bytes 196640 | tf_op jit(solution)/shard_map/ppermute | solution.py:43
  363.7 7.1 %collective-permute-done.50 = bf16[1024,256]{1,0:T(8,128)(2,1)S(1)} collective-permute-done((bf16[1024,256]{1,0:T(8,128)(2,1)S(1)}, bf16[1024,256]{1,0:T(8,128)(2,1)S(1)}, u32[]{:S(2)}, u32[]{:S(2)}) %collective-permute-start.50) | collective-permute-done | bytes 524320 | tf_op jit(solution)/shard_map/ppermute | solution.py:43
  385.4 6.2 %collective-permute-done.51 = bf16[768,256]{1,0:T(8,128)(2,1)S(1)} collective-permute-done((bf16[768,256]{1,0:T(8,128)(2,1)S(1)}, bf16[768,256]{1,0:T(8,128)(2,1)S(1)}, u32[]{:S(2)}, u32[]{:S(2)}) %collective-permute-start.51) | collective-permute-done | bytes 393248 | tf_op jit(solution)/shard_map/ppermute | solution.py:43
  404.0 5.1 %collective-permute-start.63 = (bf16[128,2048]{1,0:T(8,128)(2,1)S(1)}, bf16[128,2048]{1,0:T(8,128)(2,1)S(1)}, u32[]{:S(2)}, u32[]{:S(2)}) collective-permute-start(bf16[128,2048]{1,0:T(8,128)(2,1)S(1)} %collective-permute-done.56), channel_id=1, source_target_pairs={{0,1},{1,0},{2,3},{3,2},{4,5},{5,4},{6,7},{7,6},{8,9},{9,8},{10,11... | collective-permute-start | bytes 1572872 | tf_op jit(solution)/shard_map/ppermute | solution.py:135
  411.5 11.0 %collective-permute-done.64.z2 = bf16[1024,256]{1,0:T(8,128)(2,1)S(1)} collective-permute-done((bf16[1024,256]{1,0:T(8,128)(2,1)S(1)}, bf16[1024,256]{1,0:T(8,128)(2,1)S(1)}, u32[]{:S(2)}, u32[]{:S(2)}) %collective-permute-start.64) | collective-permute-done | bytes 524320 | tf_op jit(solution)/shard_map/ppermute | solution.py:130
  447.7 5.2 %assemble_z.1.held_ref = f32[8512,256]{1,0:T(8,128)} custom-call(s32[1]{0:T(128)} %bitcast.2.place_ref, bf16[1024,256]{1,0:T(8,128)(2,1)} %copy-done.19, bf16[1024,256]{1,0:T(8,128)(2,1)} %collective-permute-done.69.z1, bf16[1024,256]{1,0:T(8,128)(2,1)} %copy-done.38, bf16[1024,256]{1,0:T(8,128)(2,1)} %collective-permute-done.70.z3), custom_call_target="tpu_custom_call" | custom-call | flops 4000000000 | bytes 6000000 | tf_op jit(solution)/shard_map/assemble_z/pallas_call | solution.py:928
  456.0 5.0 %collective-permute-done.75.b2 = bf16[640,256]{1,0:T(8,128)(2,1)S(1)} collective-permute-done((bf16[640,256]{1,0:T(8,128)(2,1)S(1)}, bf16[640,256]{1,0:T(8,128)(2,1)S(1)}, u32[]{:S(2)}, u32[]{:S(2)}) %collective-permute-start.75) | collective-permute-done | bytes 327712 | tf_op jit(solution)/shard_map/ppermute | solution.py:130
  (397 shorter events, 208.3 us)
Async XLA Ops:
  7.2 87.7 %all-gather.7.cloned.1.call-start = ((), (), s32[]{:S(2)}) async-start(), calls=%async_computation.1 | async-start | bytes 5242880 | tf_op jit(solution)/shard_map/all_gather | solution.py:1011
  7.9 155.0 %all-gather.5.cloned.1.call-start = ((), (), s32[]{:S(2)}) async-start(), calls=%async_computation | async-start | bytes 5242880 | tf_op jit(solution)/shard_map/all_gather | solution.py:1012
  56.9 24.9 %collective-permute-start.4 = (bf16[1024,256]{1,0:T(8,128)(2,1)}, bf16[1024,256]{1,0:T(8,128)(2,1)}, u32[]{:S(2)}, u32[]{:S(2)}) collective-permute-start(bf16[1024,256]{1,0:T(8,128)(2,1)} %get-tuple-element.153.refs_0_), channel_id=1, source_target_pairs={{0,8},{8,16},{16,24},{24,28},{28,20},{20,12},{12,4},{4,0},{1,9},{9... | collective-permute-start | bytes 1572872 | tf_op jit(solution)/shard_map/ppermute | solution.py:43
  58.2 24.6 %collective-permute-start.5 = (bf16[1024,256]{1,0:T(8,128)(2,1)}, bf16[1024,256]{1,0:T(8,128)(2,1)}, u32[]{:S(2)}, u32[]{:S(2)}) collective-permute-start(bf16[1024,256]{1,0:T(8,128)(2,1)} %get-tuple-element.153.refs_0_), channel_id=1, source_target_pairs={{8,0},{16,8},{24,16},{28,24},{20,28},{12,20},{4,12},{0,4},{9,1},{1... | collective-permute-start | bytes 1572872 | tf_op jit(solution)/shard_map/ppermute | solution.py:43
  115.5 22.1 %collective-permute-start.14 = (bf16[1024,256]{1,0:T(8,128)(2,1)S(1)}, bf16[1024,256]{1,0:T(8,128)(2,1)S(1)}, u32[]{:S(2)}, u32[]{:S(2)}) collective-permute-start(bf16[1024,256]{1,0:T(8,128)(2,1)S(1)} %collective-permute-done.10.refs_7_), channel_id=1, source_target_pairs={{0,8},{8,16},{16,24},{24,28},{28,20},{20,12},{12,4},{4,0},{1,9},{9... | collective-permute-start | bytes 1572872 | tf_op jit(solution)/shard_map/ppermute | solution.py:43
  116.3 21.4 %collective-permute-start.15 = (bf16[1024,256]{1,0:T(8,128)(2,1)S(1)}, bf16[1024,256]{1,0:T(8,128)(2,1)S(1)}, u32[]{:S(2)}, u32[]{:S(2)}) collective-permute-start(bf16[1024,256]{1,0:T(8,128)(2,1)S(1)} %collective-permute-done.11.refs_2_), channel_id=1, source_target_pairs={{8,0},{16,8},{24,16},{28,24},{20,28},{12,20},{4,12},{0,4},{9,1},{1... | collective-permute-start | bytes 1572872 | tf_op jit(solution)/shard_map/ppermute | solution.py:43
  117.0 20.7 %collective-permute-start.16 = (bf16[128,2048]{1,0:T(8,128)(2,1)S(1)}, bf16[128,2048]{1,0:T(8,128)(2,1)}, u32[]{:S(2)}, u32[]{:S(2)}) collective-permute-start(bf16[128,2048]{1,0:T(8,128)(2,1)S(1)} %collective-permute-done.12.refs_8_), channel_id=1, source_target_pairs={{0,8},{8,16},{16,24},{24,28},{28,20},{20,12},{12,4},{4,0},{1,9},{9... | collective-permute-start | bytes 1572872 | tf_op jit(solution)/shard_map/ppermute | solution.py:43
  232.5 30.1 %collective-permute-start.28 = (bf16[2,256,2048]{2,1,0:T(8,128)(2,1)S(1)}, bf16[2,256,2048]{2,1,0:T(8,128)(2,1)}, u32[]{:S(2)}, u32[]{:S(2)}) collective-permute-start(bf16[2,256,2048]{2,1,0:T(8,128)(2,1)S(1)} %dynamic-slice_bitcast_fusion.1), channel_id=1, source_target_pairs={{0,1},{1,0},{2,3},{3,2},{4,5},{5,4},{6,7},{7,6},{8,9},{9,8},{10,11... | collective-permute-start | bytes 6291464 | tf_op jit(solution)/shard_map/ppermute | solution.py:150
  234.4 25.1 %collective-permute-start.31 = (bf16[512,256]{1,0:T(8,128)(2,1)S(1)}, bf16[512,256]{1,0:T(8,128)(2,1)S(1)}, u32[]{:S(2)}, u32[]{:S(2)}) collective-permute-start(bf16[512,256]{1,0:T(8,128)(2,1)S(1)} %get-tuple-element.193), channel_id=1, source_target_pairs={{0,8},{8,16},{16,24},{24,28},{28,20},{20,12},{12,4},{4,0},{1,9},{9... | collective-permute-start | bytes 786440 | tf_op jit(solution)/shard_map/ppermute | solution.py:43
  234.7 24.8 %collective-permute-start.32 = (bf16[512,256]{1,0:T(8,128)(2,1)S(1)}, bf16[512,256]{1,0:T(8,128)(2,1)S(1)}, u32[]{:S(2)}, u32[]{:S(2)}) collective-permute-start(bf16[512,256]{1,0:T(8,128)(2,1)S(1)} %get-tuple-element.194), channel_id=1, source_target_pairs={{8,0},{16,8},{24,16},{28,24},{20,28},{12,20},{4,12},{0,4},{9,1},{1... | collective-permute-start | bytes 786440 | tf_op jit(solution)/shard_map/ppermute | solution.py:43
  235.9 23.9 %collective-permute-start.29 = (bf16[128,2048]{1,0:T(8,128)(2,1)}, bf16[128,2048]{1,0:T(8,128)(2,1)}, u32[]{:S(2)}, u32[]{:S(2)}) collective-permute-start(bf16[128,2048]{1,0:T(8,128)(2,1)} %pad_maximum_fusion), channel_id=1, source_target_pairs={{0,8},{8,16},{16,24},{24,28},{28,20},{20,12},{12,4},{4,0},{1,9},{9... | collective-permute-start | bytes 1572872 | tf_op jit(solution)/shard_map/ppermute | solution.py:43
  236.2 23.6 %collective-permute-start.30 = (bf16[128,2048]{1,0:T(8,128)(2,1)}, bf16[128,2048]{1,0:T(8,128)(2,1)}, u32[]{:S(2)}, u32[]{:S(2)}) collective-permute-start(bf16[128,2048]{1,0:T(8,128)(2,1)} %pad_maximum_fusion.1), channel_id=1, source_target_pairs={{8,0},{16,8},{24,16},{28,24},{20,28},{12,20},{4,12},{0,4},{9,1},{1... | collective-permute-start | bytes 1572872 | tf_op jit(solution)/shard_map/ppermute | solution.py:43
  267.1 23.5 %collective-permute-start.35 = (bf16[1024,256]{1,0:T(8,128)(2,1)S(1)}, bf16[1024,256]{1,0:T(8,128)(2,1)}, u32[]{:S(2)}, u32[]{:S(2)}) collective-permute-start(bf16[1024,256]{1,0:T(8,128)(2,1)S(1)} %pad_maximum_fusion.2), channel_id=1, source_target_pairs={{0,8},{8,16},{16,24},{24,28},{28,20},{20,12},{12,4},{4,0},{1,9},{9... | collective-permute-start | bytes 1572872 | tf_op jit(solution)/shard_map/ppermute | solution.py:43
  267.5 23.2 %collective-permute-start.36 = (bf16[1024,256]{1,0:T(8,128)(2,1)S(1)}, bf16[1024,256]{1,0:T(8,128)(2,1)}, u32[]{:S(2)}, u32[]{:S(2)}) collective-permute-start(bf16[1024,256]{1,0:T(8,128)(2,1)S(1)} %pad_maximum_fusion.3), channel_id=1, source_target_pairs={{8,0},{16,8},{24,16},{28,24},{20,28},{12,20},{4,12},{0,4},{9,1},{1... | collective-permute-start | bytes 1572872 | tf_op jit(solution)/shard_map/ppermute | solution.py:43
  268.6 24.8 %collective-permute-start.33 = (bf16[128,2048]{1,0:T(8,128)(2,1)}, bf16[128,2048]{1,0:T(8,128)(2,1)}, u32[]{:S(2)}, u32[]{:S(2)}) collective-permute-start(bf16[128,2048]{1,0:T(8,128)(2,1)} %get-tuple-element.200), channel_id=1, source_target_pairs={{0,8},{8,16},{16,24},{24,28},{28,20},{20,12},{12,4},{4,0},{1,9},{9... | collective-permute-start | bytes 1572872 | tf_op jit(solution)/shard_map/ppermute | solution.py:43
  268.9 24.5 %collective-permute-start.34 = (bf16[128,2048]{1,0:T(8,128)(2,1)S(1)}, bf16[128,2048]{1,0:T(8,128)(2,1)}, u32[]{:S(2)}, u32[]{:S(2)}) collective-permute-start(bf16[128,2048]{1,0:T(8,128)(2,1)S(1)} %get-tuple-element.201), channel_id=1, source_target_pairs={{8,0},{16,8},{24,16},{28,24},{20,28},{12,20},{4,12},{0,4},{9,1},{1... | collective-permute-start | bytes 1572872 | tf_op jit(solution)/shard_map/ppermute | solution.py:43
  270.1 26.2 %collective-permute-start.37 = (bf16[256,2048]{1,0:T(8,128)(2,1)S(1)}, bf16[256,2048]{1,0:T(8,128)(2,1)S(1)}, u32[]{:S(2)}, u32[]{:S(2)}) collective-permute-start(bf16[256,2048]{1,0:T(8,128)(2,1)S(1)} %fusion.6), channel_id=1, source_target_pairs={{0,2},{1,3},{2,0},{3,1},{4,6},{5,7},{6,4},{7,5},{8,10},{9,11},{10,... | collective-permute-start | bytes 3145736 | tf_op jit(solution)/shard_map/ppermute | solution.py:157
  296.3 34.3 %collective-permute-start.40 = (bf16[128,2048]{1,0:T(8,128)(2,1)}, bf16[128,2048]{1,0:T(8,128)(2,1)S(1)}, u32[]{:S(2)}, u32[]{:S(2)}) collective-permute-start(bf16[128,2048]{1,0:T(8,128)(2,1)} %get-tuple-element.222), channel_id=1, source_target_pairs={{0,8},{8,16},{16,24},{24,28},{28,20},{20,12},{12,4},{4,0},{1,9},{9... | collective-permute-start | bytes 1572872 | tf_op jit(solution)/shard_map/ppermute | solution.py:43
  297.3 33.3 %collective-permute-start.41 = (bf16[128,2048]{1,0:T(8,128)(2,1)}, bf16[128,2048]{1,0:T(8,128)(2,1)S(1)}, u32[]{:S(2)}, u32[]{:S(2)}) collective-permute-start(bf16[128,2048]{1,0:T(8,128)(2,1)} %get-tuple-element.223), channel_id=1, source_target_pairs={{8,0},{16,8},{24,16},{28,24},{20,28},{12,20},{4,12},{0,4},{9,1},{1... | collective-permute-start | bytes 1572872 | tf_op jit(solution)/shard_map/ppermute | solution.py:43
  306.5 21.0 %collective-permute-start.38 = (bf16[1024,256]{1,0:T(8,128)(2,1)}, bf16[1024,256]{1,0:T(8,128)(2,1)S(1)}, u32[]{:S(2)}, u32[]{:S(2)}) collective-permute-start(bf16[1024,256]{1,0:T(8,128)(2,1)} %get-tuple-element.217), channel_id=1, source_target_pairs={{0,8},{8,16},{16,24},{24,28},{28,20},{20,12},{12,4},{4,0},{1,9},{9... | collective-permute-start | bytes 1572872 | tf_op jit(solution)/shard_map/ppermute | solution.py:43
  307.1 20.3 %collective-permute-start.39 = (bf16[1024,256]{1,0:T(8,128)(2,1)}, bf16[1024,256]{1,0:T(8,128)(2,1)}, u32[]{:S(2)}, u32[]{:S(2)}) collective-permute-start(bf16[1024,256]{1,0:T(8,128)(2,1)} %get-tuple-element.218), channel_id=1, source_target_pairs={{8,0},{16,8},{24,16},{28,24},{20,28},{12,20},{4,12},{0,4},{9,1},{1... | collective-permute-start | bytes 1572872 | tf_op jit(solution)/shard_map/ppermute | solution.py:43
  341.5 22.1 %collective-permute-start.49 = (bf16[1024,256]{1,0:T(8,128)(2,1)}, bf16[1024,256]{1,0:T(8,128)(2,1)S(1)}, u32[]{:S(2)}, u32[]{:S(2)}) collective-permute-start(bf16[1024,256]{1,0:T(8,128)(2,1)} %get-tuple-element.242), channel_id=1, source_target_pairs={{0,8},{8,16},{16,24},{24,28},{28,20},{20,12},{12,4},{4,0},{1,9},{9... | collective-permute-start | bytes 1572872 | tf_op jit(solution)/shard_map/ppermute | solution.py:43
  352.6 23.4 %collective-permute-start.47 = (bf16[256,2048]{1,0:T(8,128)(2,1)S(1)}, bf16[256,2048]{1,0:T(8,128)(2,1)S(1)}, u32[]{:S(2)}, u32[]{:S(2)}) collective-permute-start(bf16[256,2048]{1,0:T(8,128)(2,1)S(1)} %fusion.7), channel_id=1, source_target_pairs={{0,2},{1,3},{2,0},{3,1},{4,6},{5,7},{6,4},{7,5},{8,10},{9,11},{10,... | collective-permute-start | bytes 3145736 | tf_op jit(solution)/shard_map/ppermute | solution.py:157
  424.6 23.1 %collective-permute-start.69 = (bf16[1024,256]{1,0:T(8,128)(2,1)S(1)}, bf16[1024,256]{1,0:T(8,128)(2,1)}, u32[]{:S(2)}, u32[]{:S(2)}) collective-permute-start(bf16[1024,256]{1,0:T(8,128)(2,1)S(1)} %add_convert_fusion.z0), channel_id=1, source_target_pairs={{0,1},{1,0},{2,3},{3,2},{4,5},{5,4},{6,7},{7,6},{8,9},{9,8},{10,11... | collective-permute-start | bytes 1572872 | tf_op jit(solution)/shard_map/ppermute | solution.py:134
  (109 other events, 1455.4 us)
Sparse Core Ops, SparseCore 0:
  9.6 36.9 all-gather.6
  48.1 34.4 all-gather.4

commit v3 on v2

--- a/solution.py
+++ b/solution.py
@@ -19,6 +19,7 @@
 SEG = 256
 HALO = 8
 SMALL = 32
+TAIL = 32
 VMEM_LIMIT = 56 * 1024 * 1024
 F32 = jnp.float32
 BF16 = jnp.bfloat16
@@ -78,12 +79,15 @@
 
 
 class Reduce:
-    def __init__(self, chunk, n):
+    def __init__(self, chunk, n, pieces=None):
         self.forward, self.backward = ring_routes(n)
         self.chunk, self.n, self.step = chunk, n, n // 2
-        first = chunk(n // 2).astype(BF16)
-        self.upper, _ = halves(first.shape[0])
-        self.right, self.left = first[: self.upper], first[self.upper :]
+        if pieces is None:
+            first = chunk(n // 2).astype(BF16)
+            upper, _ = halves(first.shape[0])
+            pieces = first[:upper], first[upper:]
+        self.right, self.left = pieces
+        self.upper = self.right.shape[0]
 
     def load(self):
         return self.right, self.left
@@ -107,6 +111,25 @@
         self.right, self.left = right.astype(BF16), left.astype(BF16)
 
 
+def cut_in_two(grads_ref, right_ref, left_ref):
+    upper = right_ref.shape[0]
+    right_ref[...] = grads_ref[:upper]
+    left_ref[...] = grads_ref[upper:]
+
+
+def run_cut(grads, rows, block):
+    shapes = [(half, SEG) for half in halves(rows)]
+    return pl.pallas_call(
+        cut_in_two,
+        grid=(1,),
+        in_specs=[pl.BlockSpec((rows, SEG), lambda i: (0, block))],
+        out_specs=[pl.BlockSpec(shape, lambda i: (0, 0)) for shape in shapes],
+        out_shape=[jax.ShapeDtypeStruct(shape, BF16) for shape in shapes],
+        cost_estimate=busy(1, 1),
+        name="cut_in_two",
+    )(grads)
+
+
 def barrier(value, *earlier):
     return lax.optimization_barrier((value, earlier))[0]
 
@@ -140,14 +163,43 @@
     return near_share(block, far_share(block, m), m)
 
 
+def gather_small(conv0, conv1, heads0, heads1, gate_ref, gain_ref, out_ref):
+    out_ref[...] = jnp.zeros_like(out_ref)
+    lines = [(conv0, k, conv1) for k in range(KW + 1)]
+    lines += [(gate_ref, 0, None), (gate_ref, 1, None), (gain_ref, 0, None)]
+    at = 0
+    for ref, row, other in lines:
+        for start in range(0, ref.shape[1], SEG):
+            line = ref[row : row + 1, start : start + SEG]
+            if other is not None:
+                line = line + other[row : row + 1, start : start + SEG]
+            out_ref[at : at + 1, :] = line
+            at += 1
+    at = out_ref.shape[0] - heads0.shape[0]
+    out_ref[at:, :] = heads0[...] + heads1[...]
+
+
+def run_gather_small(conv_grads, head_grads, gate_cols, d_gain):
+    arrays = [*conv_grads, *head_grads, gate_cols, d_gain]
+    lines = (KW + 1) * conv_grads[0].shape[1] + 2 * gate_cols.shape[1] + d_gain.shape[1]
+    rows = -(-lines // SEG // 8) * 8 + head_grads[0].shape[0]
+    return pl.pallas_call(
+        gather_small,
+        grid=(1,),
+        in_specs=[pl.BlockSpec(v.shape, lambda i: (0, 0)) for v in arrays],
+        out_specs=pl.BlockSpec((rows, SEG), lambda i: (0, 0)),
+        out_shape=jax.ShapeDtypeStruct((rows, SEG), F32),
+        cost_estimate=busy(1, 1),
+        name="gather_small",
+    )(*arrays)
+
+
 class CtxReduce:
-    def __init__(self, share, m):
+    def __init__(self, kept, given, m):
         self.m, place = m, lax.axis_index("ctx")
         self.core, self.across = place % 2, place // 2
-        split = share.reshape((m // 2, 2) + share.shape[1:])
-        self.kept = lax.dynamic_index_in_dim(split, self.core, 1, False)
-        sent = lax.dynamic_index_in_dim(split, 1 - self.core, 1, False)
-        self.near = lax.ppermute(sent, "ctx", ctx_route(m, 1))
+        self.kept = kept
+        self.near = lax.ppermute(given, "ctx", ctx_route(m, 1))
 
     def middle(self):
         self.both = self.kept.astype(F32) + self.near.astype(F32)
@@ -160,10 +212,18 @@
         return lax.dynamic_index_in_dim(self.both, self.across, 0, False) + self.far.astype(F32)
 
 
+def by_core(share, m):
+    core = lax.axis_index("ctx") % 2
+    split = share.reshape((m // 2, 2) + share.shape[1:])
+    return (
+        lax.dynamic_index_in_dim(split, core, 1, False),
+        lax.dynamic_index_in_dim(split, 1 - core, 1, False),
+    )
+
+
 def ctx_sum(values, m):
-    for flip in (1, 2):
-        values = values + lax.ppermute(values, "ctx", ctx_route(m, flip))
-    return values
+    near, across, far = (lax.ppermute(values, "ctx", ctx_route(m, flip)) for flip in (1, 2, 3))
+    return (values + near) + (across + far)
 
 
 def nt(a, b):
@@ -314,6 +374,7 @@
         ),
         out_shape=jax.ShapeDtypeStruct((n, 32, SEG), F32),
         compiler_params=pltpu.CompilerParams(vmem_limit_bytes=VMEM_LIMIT),
+        cost_estimate=busy(1, 1),
         name="collect",
     )(members, *lasts)
 
@@ -335,9 +396,8 @@
 
 def resident(array, grid_args=1):
     zeros = (0,) * array.ndim
-    if grid_args == 2:
-        return pl.BlockSpec(array.shape, lambda i, t: zeros, pipeline_mode=pl.Buffered(1))
-    return pl.BlockSpec(array.shape, lambda i: zeros, pipeline_mode=pl.Buffered(1))
+    maps = {1: lambda i: zeros, 2: lambda i, t: zeros, 3: lambda i, t, p: zeros}
+    return pl.BlockSpec(array.shape, maps[grid_args], pipeline_mode=pl.Buffered(1))
 
 
 def run_front(members, tokens, weights):
@@ -529,7 +589,7 @@
 
 
 def mix_backward(
-    top, act_ref, proj_ref, prev_ref, taps_ref, heads_ref, skip_ref, table_ref, start_ref, dy_ref,
+    top, follows, act_ref, proj_ref, prev_ref, taps_ref, heads_ref, skip_ref, table_ref, start_ref, dy_ref,
     carry_in, halo_in, held_ref, dx_ref, grads_ref, dheads_ref, carried, halo,
     gram, dgram, bias, d_scores, scores, db, dc, found, ends,
 ):
@@ -540,8 +600,8 @@
 
     @pl.when(step == 0)
     def _():
-        carried[...] = carry_in[...]
-        halo[...] = halo_in[...]
+        carried[...] = carry_in[...] if follows else jnp.zeros_like(carried)
+        halo[...] = halo_in[...] if follows else jnp.zeros_like(halo)
         grads_ref[...] = jnp.zeros_like(grads_ref)
         dheads_ref[...] = jnp.zeros_like(dheads_ref)
         scores[...] = jnp.zeros_like(scores)
@@ -667,27 +727,29 @@
     dx_ref[:, core : core + PAIR] = filled.T.astype(BF16)
 
 
-def run_mix_backward(span, top, act, proj, taps, heads_in, skip, table, starts, dy, carry, halo, held):
-    pairs = carry.shape[0]
+def run_mix_backward(span, top, act, proj, taps, heads_in, skip, table, starts, dy, before):
+    pairs = starts.shape[1]
+    follows = before is not None
+    held, carry, halo = before if follows else (dy, skip[:, :128], skip[:, :128])
     heads, width = 2 * pairs, pairs * PAIR
     core = width + 2 * STATE
     whole = lambda i: (0, 0)
     block = lambda i: (top - i, 0)
-    before = GROUP // 16
+    above = GROUP // 16
     return pl.pallas_call(
-        lambda *refs: mix_backward(top, *refs),
+        lambda *refs: mix_backward(top, follows, *refs),
         grid=(span,),
         in_specs=[
             pl.BlockSpec((GROUP, core), block),
             pl.BlockSpec((GROUP, proj.shape[1]), block),
-            pl.BlockSpec((16, proj.shape[1]), lambda i: (jnp.maximum((top - i) * before - 1, 0), 0)),
+            pl.BlockSpec((16, proj.shape[1]), lambda i: (jnp.maximum((top - i) * above - 1, 0), 0)),
             pl.BlockSpec(taps.shape, whole),
             pl.BlockSpec(heads_in.shape, whole),
             pl.BlockSpec(skip.shape, whole),
             pl.BlockSpec((1, 16 * pairs, 128), lambda i: (top - i, 0, 0)),
             pl.BlockSpec((1, pairs, STATE, PAIR), lambda i: (top - i, 0, 0, 0)),
             pl.BlockSpec((GROUP, width), block),
-            pl.BlockSpec(carry.shape, lambda i: (0, 0, 0)),
+            pl.BlockSpec(carry.shape, lambda i: (0,) * carry.ndim),
             pl.BlockSpec(halo.shape, whole),
             pl.BlockSpec(memory_space=pl.ANY),
         ],
@@ -695,15 +757,15 @@
             pl.BlockSpec((GROUP, proj.shape[1]), block),
             pl.BlockSpec((8, core), whole),
             pl.BlockSpec((2 * heads, GROUP), whole),
-            pl.BlockSpec(carry.shape, lambda i: (0, 0, 0)),
-            pl.BlockSpec(halo.shape, whole),
+            pl.BlockSpec((pairs, STATE, PAIR), lambda i: (0, 0, 0)),
+            pl.BlockSpec((HALO, core), whole),
         ],
         out_shape=[
             jax.ShapeDtypeStruct(proj.shape, BF16),
             jax.ShapeDtypeStruct((8, core), F32),
             jax.ShapeDtypeStruct((2 * heads, GROUP), F32),
-            jax.ShapeDtypeStruct(carry.shape, F32),
-            jax.ShapeDtypeStruct(halo.shape, F32),
+            jax.ShapeDtypeStruct((pairs, STATE, PAIR), F32),
+            jax.ShapeDtypeStruct((HALO, core), F32),
         ],
         scratch_shapes=[
             pltpu.VMEM((GROUP, GROUP), F32),
@@ -717,10 +779,10 @@
             pltpu.VMEM((heads, PAIR), F32),
         ],
         compiler_params=pltpu.CompilerParams(vmem_limit_bytes=VMEM_LIMIT),
-        input_output_aliases={} if held is None else {11: 0},
+        input_output_aliases={11: 0} if follows else {},
         cost_estimate=busy(12 * span, 5 * span),
         name="mix_backward",
-    )(act, proj, proj, taps, heads_in, skip, table, starts, dy, carry, halo, dy if held is None else held)
+    )(act, proj, proj, taps, heads_in, skip, table, starts, dy, carry, halo, held)
 
 
 def gate_sums(members_ref, seed_ref, z_ref, y_ref, gain_ref, *refs):
@@ -795,9 +857,11 @@
         inv = lax.rsqrt(sums_ref[0:1, :] / DI + EPS)
         slope = inv * inv * inv * (sums_ref[1:2, :] / DI)
         rest = jnp.zeros((PAIR - 2, sums_ref.shape[1]), F32)
-        turned[...] = jnp.concatenate([inv, slope, rest], axis=0).T
-
-    inv, slope = turned[:, 0:1], turned[:, 1:2]
+        both = jnp.concatenate([inv, slope, rest], axis=0).T
+        turned[0] = jnp.broadcast_to(both[:, 0:1], turned.shape[1:])
+        turned[1] = jnp.broadcast_to(both[:, 1:2], turned.shape[1:])
+
+    inv, slope = turned[0], turned[1]
     z, y, scaled, gain = z_ref[...].astype(F32), y_ref[...], scaled_ref[...], gain_ref[...]
     sig = sigmoid(z)
     silu = z * sig
@@ -831,15 +895,27 @@
         ],
         out_specs=[col, col, col, pl.BlockSpec((8, tile), lambda i: (0, i))],
         out_shape=[low, low, low, jax.ShapeDtypeStruct((8, width), F32)],
-        scratch_shapes=[pltpu.VMEM((length, PAIR), F32)],
+        scratch_shapes=[pltpu.VMEM((2, length, PAIR), F32)],
         compiler_params=pltpu.CompilerParams(vmem_limit_bytes=VMEM_LIMIT),
         cost_estimate=busy(11, 20),
         name="gate_back",
     )(sums, scaled, z, y, x, gain)
 
 
-def back_norm(members_ref, tokens_ref, dz_ref, dx_ref, *refs):
-    parts, (dn_ref, gain_ref) = refs[:-2], refs[-2:]
+def keep_or_give(place_ref, value, keep_ref, give_ref):
+    mine = place_ref[0] % 2 == pl.program_id(0) % 2
+
+    @pl.when(mine)
+    def _():
+        keep_ref[0] = value
+
+    @pl.when(jnp.logical_not(mine))
+    def _():
+        give_ref[0] = value
+
+
+def back_norm(members_ref, place_ref, tokens_ref, dz_ref, dx_ref, *refs):
+    parts, (keep_ref, give_ref, gain_ref, dn_ref) = refs[:-4], refs[-4:]
     count = len(parts) // 2
 
     @pl.when(pl.program_id(0) == 0)
@@ -858,32 +934,58 @@
         dn_ref[:, pl.ds(at, SEG)] = d_normed.astype(BF16)
         scaled = tokens_ref[:, pl.ds(at, SEG)].astype(F32) * inv
         gain_ref[0:1, pl.ds(at, SEG)] += jnp.sum(d_normed * scaled, axis=0, keepdims=True)
-
-
-def run_back_norm(members, tokens, dz, dx, weights_z, weights_x):
+    keep_or_give(place_ref, dn_ref[...], keep_ref, give_ref)
+
+
+def run_back_norm(members, place, tokens, dz, dx, weights_z, weights_x):
     length = tokens.shape[0]
-    row = lambda i, t: (i, 0)
+    row = lambda i, t, p: (i, 0)
+    half = pl.BlockSpec((1, GROUP, D), lambda i, t, p: (i // 2, 0, 0))
+    halves_shape = jax.ShapeDtypeStruct((length // GROUP // 2, GROUP, D), BF16)
     return pl.pallas_call(
         back_norm,
         grid_spec=pltpu.PrefetchScalarGridSpec(
-            num_scalar_prefetch=1,
+            num_scalar_prefetch=2,
             grid=(length // GROUP,),
             in_specs=[
                 pl.BlockSpec((GROUP, D), row),
                 pl.BlockSpec((GROUP, dz.shape[1]), row),
                 pl.BlockSpec((GROUP, dx.shape[1]), row),
             ]
-            + [resident(w, 2) for w in weights_z + weights_x],
-            out_specs=[pl.BlockSpec((GROUP, D), row), pl.BlockSpec((8, D), lambda i, t: (0, 0))],
+            + [resident(w, 3) for w in weights_z + weights_x],
+            out_specs=[half, half, pl.BlockSpec((8, D), lambda i, t, p: (0, 0))],
+            scratch_shapes=[pltpu.VMEM((GROUP, D), BF16)],
         ),
-        out_shape=[
-            jax.ShapeDtypeStruct((length, D), BF16),
-            jax.ShapeDtypeStruct((8, D), F32),
-        ],
+        out_shape=[halves_shape, halves_shape, jax.ShapeDtypeStruct((8, D), F32)],
         compiler_params=pltpu.CompilerParams(vmem_limit_bytes=VMEM_LIMIT),
         cost_estimate=busy(18, 24),
         name="back_norm",
-    )(members, tokens, dz, dx, *weights_z, *weights_x)
+    )(members, place, tokens, dz, dx, *weights_z, *weights_x)
+
+
+def assemble_o(place_ref, o0, o1, o2, o3, out_ref):
+    for k, ref in enumerate((o0, o1, o2, o3)):
+
+        @pl.when(pl.program_id(0) == k)
+        def _():
+            out_ref[...] = ref[...].astype(F32)
+
+
+def run_assemble_o(place, shares):
+    m, (rows, cols) = len(shares), shares[0].shape
+    return pl.pallas_call(
+        assemble_o,
+        grid_spec=pltpu.PrefetchScalarGridSpec(
+            num_scalar_prefetch=1,
+            grid=(m,),
+            in_specs=[resident(share, 2) for share in shares],
+            out_specs=pl.BlockSpec((rows, cols), lambda i, t: (t[0] ^ i, 0)),
+        ),
+        out_shape=jax.ShapeDtypeStruct((m * rows, cols), F32),
+        compiler_params=pltpu.CompilerParams(vmem_limit_bytes=VMEM_LIMIT),
+        cost_estimate=busy(3, 3),
+        name="assemble_o",
+    )(place, *shares)
 
 
 def put_pairs(place_ref, refs, out_ref, g):
@@ -917,7 +1019,7 @@
         steps = jnp.zeros((HEADS, out_ref.shape[1]), F32)
         for k, x in enumerate(refs):
             total = total + x[width:core].astype(F32)
-            steps = steps + nn(order_ref[place_ref[0] ^ k], x[core : core + PAIR])
+            steps = steps + nn(order_ref[place_ref[0] ^ k], x[core : core + TAIL])
         out_ref[: 2 * STATE] = total
         out_ref[2 * STATE : 2 * STATE + HEADS] = steps
 
@@ -1011,11 +1113,6 @@
     all_tokens = lax.all_gather(tokens[0], "ctx", axis=0, tiled=True)
     seed = lax.all_gather(cotangent[0], "ctx", axis=0, tiled=True)
 
-    dt_bias_own, a_log_own = of_heads(dt_bias), of_heads(a_log)
-    skip_own = of_pairs(d_skip, 0)
-    a_neg = -jnp.exp(a_log_own)
-    heads_in = jnp.broadcast_to(jnp.concatenate([dt_bias_own, a_neg])[:, None], (2 * heads, 128))
-    skip_row = jnp.repeat(skip_own, HEADDIM)[None, :]
 
     columns = w_in.T
     total_cols = core_cols + PAIR
@@ -1037,13 +1134,16 @@
         small = jnp.concatenate([v.reshape(-1) for v in padded]).reshape(-1, SEG)
         block_x, block_z, block_o = run_pack(place_ref, columns, w_out, small, pairs)
         ring_x, ring_z, ring_o = Gather(block_x, n), Gather(block_z, n), Gather(block_o, n)
-        next_hop([ring_x], (), heads_in, skip_row)
-        for _ in range(n // 2 - 3):
+        next_hop([ring_x], ())
+        dt_bias, a_log, d_skip = next_hop([ring_x], (dt_bias, a_log, d_skip))
+        for _ in range(n // 2 - 4):
             next_hop([ring_x], ())
         next_hop([ring_x, ring_z], ())
         next_hop([ring_x], (), *arrivals(ring_z))
         parts_x = ring_x.parts()
-        all_tokens = next_hop([ring_z, ring_o], all_tokens, *arrivals(ring_x))
+        all_tokens, members_late, parts_late = next_hop(
+            [ring_z, ring_o], (all_tokens, members, parts_x), *arrivals(ring_x)
+        )
     else:
         members = jnp.arange(D // SEG, dtype=jnp.int32)
         block_x = jnp.concatenate(
@@ -1066,7 +1166,7 @@
         parts_o = parts_o[: pairs // 2] + [middle[:upper], middle[upper:]] + parts_o[pairs // 2 + 1 :]
 
     if ring:
-        kept = run_collect(members, parts_x)
+        kept = run_collect(members_late, parts_late)
         spans, at = [], 0
         for v, each in zip(smalls, small_rows):
             here = kept[:, at : at + v.shape[0] * each].reshape(n, v.shape[0], each * SEG)
@@ -1082,6 +1182,12 @@
     taps = jnp.concatenate([of_pairs(taps_full[:, :DI], 1), taps_full[:, DI:]], axis=1)
     taps = jnp.pad(taps, ((0, 8 - KW - 1), (0, 0)))
 
+    dt_bias_own, a_log_own = of_heads(dt_bias), of_heads(a_log)
+    skip_own = of_pairs(d_skip, 0)
+    a_neg = -jnp.exp(a_log_own)
+    heads_in = jnp.broadcast_to(jnp.concatenate([dt_bias_own, a_neg])[:, None], (2 * heads, 128))
+    skip_row = jnp.repeat(skip_own, HEADDIM)[None, :]
+
     normed, proj_x = run_front(members, all_tokens, parts_x)
     if ring:
         proj_x = next_hop([ring_z, ring_o], proj_x, *arrivals(ring_z, ring_o))
@@ -1099,9 +1205,8 @@
     mixed, dy, d_z, gate_cols = run_gate_back(sums, scaled, proj_z, ssd, act, gate_full)
 
     grads_o = tn(mixed, seed).astype(BF16)
-    carry = jnp.zeros((pairs, STATE, PAIR), F32)
-    halo = jnp.zeros((HALO, core_cols), F32)
-    conv_grads, head_grads, top, d_x, d_z_late, mixed_late = [], [], blocks - 1, None, d_z, mixed
+    conv_grads, head_grads, top, before = [], [], blocks - 1, None
+    d_z_late, mixed_late = d_z, mixed
     if ring:
         sum_o = Reduce(lambda o: lax.dynamic_slice_in_dim(grads_o, members[o] * PAIR, PAIR, 0), n)
         d_z_late, mixed_late = next_hop([sum_o], (d_z, mixed))
@@ -1115,17 +1220,18 @@
             if at > 0:
                 sum_z.join()
                 branch_own.middle()
-                dy, carry, branch_own.sent = next_hop(
-                    [sum_o, sum_z], (dy, carry, branch_own.sent)
+                dy, before, branch_own.sent = next_hop(
+                    [sum_o, sum_z], (dy, before, branch_own.sent)
                 )
                 branch_own.send_far()
             else:
-                dy, carry, branch = next_hop([sum_o, sum_z], (dy, carry, branch))
-                branch_own = CtxReduce(branch.reshape(m, piece, D), m)
+                dy, branch = next_hop([sum_o, sum_z], (dy, branch))
+                branch_own = CtxReduce(*by_core(branch.reshape(m, piece, D), m), m)
         span = blocks // 2
-        d_x, conv_part, head_part, carry, halo = run_mix_backward(
-            span, top, act, proj_x, taps, heads_in, skip_row, table, starts, dy, carry, halo, d_x
+        d_x, conv_part, head_part, *before = run_mix_backward(
+            span, top, act, proj_x, taps, heads_in, skip_row, table, starts, dy, before
         )
+        before = (d_x, *before)
         conv_grads.append(conv_part)
         head_grads.append(head_part)
         top -= span
@@ -1133,39 +1239,28 @@
     if ring:
         sum_o.join()
         sum_z.join()
-        d_x, normed_late, conv_grads, head_grads, gate_cols, branch_own.far = next_hop(
-            [sum_o, sum_z], (d_x, normed, conv_grads, head_grads, gate_cols, branch_own.far)
+        d_x, normed_late, branch_own.far = next_hop(
+            [sum_o, sum_z], (d_x, normed, branch_own.far)
         )
     else:
-        branch_own = CtxReduce(branch.reshape(m, piece, D), m)
+        branch_own = CtxReduce(*by_core(branch.reshape(m, piece, D), m), m)
         branch_own.middle()
         branch_own.send_far()
     grads_x = tn(d_x, normed_late).astype(BF16)
-    d_normed, d_gain = run_back_norm(
-        members, all_tokens, d_z, after(d_x, grads_x), parts_z, parts_x
+    kept, given, d_gain = run_back_norm(
+        members, place_ref, all_tokens, d_z, after(d_x, grads_x), parts_z, parts_x
     )
+    small = run_gather_small(conv_grads, head_grads, gate_cols, d_gain)
     if ring:
+        used = core_cols + TAIL
+        sum_x = Reduce(
+            lambda o: grads_x[:used, o * SEG : (o + 1) * SEG], n, run_cut(grads_x, used, n // 2)
+        )
         part_o = sum_o.join().astype(BF16)
         sum_z.join()
-        sum_a = Reduce(lambda o: grads_x[:cut, o * SEG : (o + 1) * SEG], n)
-        sum_b = Reduce(lambda o: grads_x[cut:, o * SEG : (o + 1) * SEG], n)
-        d_normed, d_gain, part_o, conv_grads, head_grads, gate_cols, branch_own.far = next_hop(
-            [sum_a, sum_b, sum_z],
-            (d_normed, d_gain, part_o, conv_grads, head_grads, gate_cols, branch_own.far),
+        kept, given, small, part_o, branch_own.far = next_hop(
+            [sum_x, sum_z], (kept, given, small, part_o, branch_own.far)
         )
-    d_own = CtxReduce(d_normed.reshape(m, piece, D), m)
-    d_own.middle()
-    d_own.send_far()
-
-    head_sums = jnp.sum(head_grads[0] + head_grads[1], axis=1)
-    d_skip_own = jnp.sum(gate_cols[1].reshape(pairs, 2, HEADDIM), axis=2).T.reshape(heads)
-    per_head = jnp.concatenate([head_sums[:heads], head_sums[heads:] * a_neg, d_skip_own])
-    conv_grads = (conv_grads[0] + conv_grads[1])[: KW + 1]
-    lines = [conv_grads, gate_cols[0:1], d_gain[0:1], per_head[None]]
-    wide = max(line.shape[1] for line in lines)
-    small = jnp.concatenate(
-        [jnp.pad(line, ((0, 0), (0, wide - line.shape[1]))) for line in lines], axis=0
-    )
     flip = 1
     steps = []
     while flip < n:
@@ -1177,26 +1272,27 @@
             small = small + lax.ppermute(small, "fsdp", ctx_route(n, steps.pop()))
         return small
 
+    d_own = CtxReduce(kept, given, m)
+    d_own.middle()
+    d_own.send_far()
     small = small_step(small)
     if ring:
-        sum_a.join()
-        sum_b.join()
+        sum_x.join()
         part_z = sum_z.join().astype(BF16)
         d_own.far, small, part_o, part_z, branch_own.far = next_hop(
-            [sum_a, sum_b], (d_own.far, small, part_o, part_z, branch_own.far)
+            [sum_x], (d_own.far, small, part_o, part_z, branch_own.far)
         )
         other_o = far_share(part_o, m)
     small = small_step(small)
     output = (tokens[0].astype(F32) + branch_own.total()).astype(BF16)[None]
     if ring:
-        sum_a.join()
-        sum_b.join()
+        sum_x.join()
         small, other_o, part_z, d_own.far = next_hop(
-            [sum_a, sum_b], (small, other_o, part_z, d_own.far), output
+            [sum_x], (small, other_o, part_z, d_own.far), output
         )
         shares_o, other_z = near_share(part_o, other_o, m), far_share(part_z, m)
-    while steps:
-        small = small_step(small)
+        grad_w_out = run_assemble_o(place_ref, shares_o)
+    small = small_step(small)
     own = tokens[0].astype(F32)
     inv = lax.rsqrt(jnp.mean(own * own, axis=-1, keepdims=True) + EPS)
     d_direct = d_own.total() * norm_full
@@ -1204,46 +1300,48 @@
     grad_tokens = (cotangent[0].astype(F32) + d_direct * inv - own * (inv * inv * inv * along))[None]
     if ring:
         for at in range(n // 2 - 3):
-            sum_a.join()
-            sum_b.join()
-            small, shares_o, part_z, other_z = next_hop(
-                [sum_a, sum_b], (small, shares_o, part_z, other_z), grad_tokens
+            sum_x.join()
+            small, part_z, other_z = next_hop(
+                [sum_x], (small, part_z, other_z), grad_tokens, grad_w_out
             )
+        shares_z = near_share(part_z, other_z, m)
+        held = run_assemble_z(place_ref, shares_z, w_in.shape[1])
+    while steps:
+        small = small_step(small)
     smalls_of = ctx_share(small, m)
+    if ring:
+        part_x = sum_x.join().astype(BF16)
+        part_a, part_b = part_x[:cut], part_x[cut:]
+        part_a, part_b, smalls_of = barrier((part_a, part_b, smalls_of))
     by_place = jnp.zeros((m,) + small.shape, F32)
     for k in range(m):
         by_place = lax.dynamic_update_slice(by_place, smalls_of[k][None], (place ^ k, 0, 0))
+
     mine = lax.axis_index("fsdp")
-
-    def own_columns(rows_first, rows_last, extra):
-        part = by_place[:, rows_first:rows_last, :width].reshape(m, -1, pairs, PAIR)
-        whole = part.transpose(1, 2, 0, 3).reshape(-1, DI)
-        if extra:
-            shared = jnp.sum(by_place[:, rows_first:rows_last, width:core_cols], axis=0)
-            whole = jnp.concatenate([whole, shared], axis=1)
-        each = whole.shape[1] // n
-        return lax.dynamic_slice_in_dim(whole, mine * each, each, 1)
-
-    grad_conv = own_columns(0, KW + 1, True)
-    grad_conv_w, grad_conv_b = grad_conv[:KW], grad_conv[KW]
-    grad_gate_gain = own_columns(KW + 1, KW + 2, False)[0]
-    grad_gain = jnp.sum(by_place[:, KW + 2, :D], axis=0)
-    grad_gain = lax.dynamic_slice_in_dim(grad_gain, mine * rows, rows, 0)
-    per_head = by_place[:, KW + 3, : 3 * heads]
-    per_head = per_head.reshape(m, 3, 2, pairs).transpose(1, 3, 0, 2).reshape(3, HEADS)
-    small_outputs = (grad_gain, grad_conv_w, grad_conv_b, per_head, grad_gate_gain)
-    if ring:
-        shares_z = near_share(part_z, other_z, m)
-        held = run_assemble_z(place_ref, shares_z, w_in.shape[1])
-        grad_w_out = jnp.zeros((m, PAIR, D), F32)
-        for k in range(m):
-            grad_w_out = lax.dynamic_update_slice(
-                grad_w_out, shares_o[k].astype(F32)[None], (place ^ k, 0, 0)
-            )
-        grad_w_out = grad_w_out.reshape(w_out.shape)
-        part_b, part_a = sum_b.join().astype(BF16), sum_a.join().astype(BF16)
-        part_a, part_b, held, small_outputs = barrier((part_a, part_b, held, small_outputs), grad_w_out)
-    else:
+    lines = [core_cols] * (KW + 1) + [width, width, D]
+    found, at = [], 0
+    for count in lines:
+        found.append(by_place[:, at : at + count // SEG].reshape(m, 1, count))
+        at += count // SEG
+    conv_lines = jnp.concatenate(found[: KW + 1], axis=1)
+
+    def interleaved(lines):
+        return lines.reshape(m, -1, pairs, PAIR).transpose(1, 2, 0, 3).reshape(-1, DI)
+
+    whole = jnp.concatenate(
+        [interleaved(conv_lines[:, :, :width]), jnp.sum(conv_lines[:, :, width:], axis=0)], axis=1
+    )
+    each = conv_b.shape[0]
+    grad_conv = lax.dynamic_slice_in_dim(whole, mine * each, each, 1)
+    each = gate_gain.shape[0]
+    grad_gate_gain = lax.dynamic_slice_in_dim(interleaved(found[KW + 1]), mine * each, each, 1)[0]
+    grad_gain = lax.dynamic_slice_in_dim(jnp.sum(found[KW + 3], axis=0)[0], mine * rows, rows, 0)
+    skips = jnp.sum(found[KW + 2].reshape(m, pairs, 2, HEADDIM), axis=3).reshape(m, 1, pairs, 2)
+    of_steps = jnp.sum(by_place[:, by_place.shape[1] - 2 * heads :], axis=2)
+    of_steps = of_steps.reshape(m, 2, 2, pairs).transpose(0, 1, 3, 2)
+    per_head = jnp.concatenate([of_steps, skips], axis=1).transpose(1, 2, 0, 3).reshape(3, HEADS)
+    grad_a_log = per_head[1] * -jnp.exp(a_log)
+    if not ring:
         part_z = lax.psum_scatter(grads_z.astype(F32), "fsdp", scatter_dimension=1, tiled=True)
         part_x = lax.psum_scatter(grads_x.astype(F32), "fsdp", scatter_dimension=1, tiled=True)
         whole_o = jnp.zeros((pairs, m, PAIR, D), F32)
@@ -1253,10 +1351,10 @@
         grad_w_out = lax.psum_scatter(whole_o.reshape(DI, D), "fsdp", scatter_dimension=0, tiled=True)
         grad_w_out = lax.psum(grad_w_out, "ctx")
         held = run_assemble_z(place_ref, ctx_share(part_z.astype(BF16), m), w_in.shape[1])
-        part_a, part_b = part_x[:cut].astype(BF16), part_x[cut:].astype(BF16)
+        part_x = part_x.astype(BF16)
+        part_a, part_b = part_x[:cut], part_x[cut : core_cols + TAIL]
     other_b, other_a = far_share(part_b, m), far_share(part_a, m)
-    grad_gain, grad_conv_w, grad_conv_b, per_head, grad_gate_gain = small_outputs
-    order = np.zeros((m, HEADS, PAIR), np.float32)
+    order = np.zeros((m, HEADS, TAIL), np.float32)
     for member in range(m):
         for h in range(heads):
             order[member, (h % pairs) * 2 * m + 2 * member + h // pairs, h] = 1.0
@@ -1269,10 +1367,10 @@
         grad_tokens,
         grad_gain,
         grad_w_in.T,
-        grad_conv_w,
-        grad_conv_b,
+        grad_conv[:KW],
+        grad_conv[KW],
         per_head[0],
-        per_head[1],
+        grad_a_log,
         per_head[2],
         grad_gate_gain,
         grad_w_out,

time: 496 us -> 476 us (0.960)
  waiting for transfers between devices: 137 us -> 117 us
  Pallas kernels: 143 us -> 152 us
  starting transfers between devices: 88.8 us -> 79.9 us
    ppermute x5, waiting for transfers between devices: 20.6 us -> 5.29 us  [far_share(): return lax.ppermute(block, 'ctx', ctx_route(m, 2))]
    pallas_call x2 -> x5, Pallas kernels: 40.6 us -> 48.4 us  [the longest x2 40.8 us: run_mix_backward(): pl.pallas_call(lambda *refs: mix_backward(top, follows, *refs), grid=(spa...]
    ppermute x56 -> x48, waiting for transfers between devices: 108 us -> 100 us  [send(): return lax.ppermute(block, 'fsdp', route)]
    ppermute x56 -> x48, starting transfers between devices: 43.5 us -> 37 us  [send(): return lax.ppermute(block, 'fsdp', route)]
    ppermute x3, waiting for transfers between devices: 2.9 us -> 9.19 us  [small_step(): small = small + lax.ppermute(small, 'fsdp', ctx_route(n, steps.pop()))]
    unnamed x104 -> x115, local copies, waits for them, and re-layouts: 7.49 us -> 13.8 us
    convert_element_type x8 -> x6, other arithmetic: 13.4 us -> 14 us  [join(): self.right, self.left = (right.astype(BF16), left.astype(BF16))]
    ppermute x4 -> x5, starting transfers between devices: 18.7 us -> 18.8 us  [the longest x3 14 us: ctx_sum(): lax.ppermute(values, 'ctx', ctx_route(m, flip))]
  transfers between devices with their start and end apart: 82 -> 75, of which waited for: 32 -> 27; matrix products, arithmetic and copies ran while one was open for 15% -> 14% of each run, Pallas kernels for 22% -> 26%
where the time goes in v3:
time: 476 us; the launch traced here: 469 us
  Pallas kernels  152 us (32%)
  waiting for transfers between devices  117 us (25%)
  starting transfers between devices  79.9 us (17%)
  other arithmetic  39.1 us (8%)
  local copies, waits for them, and re-layouts  33.9 us (7%)
  matrix products  26.1 us (5%)
  between operations  20.8 us (4%)
    ppermute x48, waiting for transfers between devices, send(): return lax.ppermute(block, 'fsdp', route)  100 us
    pallas_call x2, Pallas kernels, run_mix_backward(): pl.pallas_call(lambda *refs: mix_backward(top, follows, *refs), grid=(spa...  40.8 us
    ppermute x48, starting transfers between devices, send(): return lax.ppermute(block, 'fsdp', route)  37 us
    dot_general x3, matrix products, tn(): lax.dot_general(a, b, (((0,), (0,)), ((), ())), preferred_element_type=F32)  21.4 us
    pallas_call x1, Pallas kernels, run_back_norm(): pl.pallas_call(back_norm, grid_spec=pltpu.PrefetchScalarGridSpec(num_scal...  19.4 us
    pallas_call x1, Pallas kernels, run_mix_forward(): pl.pallas_call(mix_forward, grid=(blocks,), in_specs=[pl.BlockSpec((GROUP...  19.1 us
    pallas_call x1, Pallas kernels, run_gate_sums(): pl.pallas_call(gate_sums, grid_spec=pltpu.PrefetchScalarGridSpec(num_scal...  14.6 us
    ppermute x3, starting transfers between devices, ctx_sum(): lax.ppermute(values, 'ctx', ctx_route(m, flip))  14 us
  transfers between devices with their start and end apart: 75, of which 27 were waited for; matrix products, arithmetic and copies ran while one was open for 14% of the time, Pallas kernels for 26%

profile of v3, /device:TPU:1, one launch (start us, length us, event | category | flops | bytes accessed | tf_op | source)
XLA Modules:
  0.0 468.5 jit_solution(16041122310532548233)
XLA Ops:
  16.4 16.1 %collective-permute-done.refs_8_.refs_7_.refs_17_ = bf16[1408,256]{1,0:T(8,128)(2,1)S(1)} collective-permute-done((bf16[1408,256]{1,0:T(8,128)(2,1)}, bf16[1408,256]{1,0:T(8,128)(2,1)S(1)}, u32[]{:S(2)}, u32[]{:S(2)}) %collective-permute-start) | collective-permute-done | bytes 720928 | tf_op jit(solution)/shard_map/ppermute | solution.py:44
  34.9 14.5 %collective-permute-done.2.refs_7_.refs_6_.refs_16_ = bf16[1408,256]{1,0:T(8,128)(2,1)} collective-permute-done((bf16[1408,256]{1,0:T(8,128)(2,1)S(1)}, bf16[1408,256]{1,0:T(8,128)(2,1)}, u32[]{:S(2)}, u32[]{:S(2)}) %collective-permute-start.2) | collective-permute-done | bytes 720928 | tf_op jit(solution)/shard_map/ppermute | solution.py:44
  54.9 11.4 %collective-permute-done.7.refs_6_.refs_5_.refs_15_ = bf16[1408,256]{1,0:T(8,128)(2,1)S(1)} collective-permute-done((bf16[1408,256]{1,0:T(8,128)(2,1)}, bf16[1408,256]{1,0:T(8,128)(2,1)S(1)}, u32[]{:S(2)}, u32[]{:S(2)}) %collective-permute-start.7) | collective-permute-done | bytes 720928 | tf_op jit(solution)/shard_map/ppermute | solution.py:44
  68.1 9.4 %collective-permute-done.4.refs_8_ = bf16[1024,256]{1,0:T(8,128)(2,1)} collective-permute-done((bf16[1024,256]{1,0:T(8,128)(2,1)}, bf16[1024,256]{1,0:T(8,128)(2,1)}, u32[]{:S(2)}, u32[]{:S(2)}) %collective-permute-start.4) | collective-permute-done | bytes 524320 | tf_op jit(solution)/shard_map/ppermute | solution.py:44
  81.5 5.0 %collective-permute-done.9.refs_5_.refs_4_.refs_14_ = bf16[640,256]{1,0:T(8,128)(2,1)} collective-permute-done((bf16[640,256]{1,0:T(8,128)(2,1)}, bf16[640,256]{1,0:T(8,128)(2,1)}, u32[]{:S(2)}, u32[]{:S(2)}) %collective-permute-start.9) | collective-permute-done | bytes 327712 | tf_op jit(solution)/shard_map/ppermute | solution.py:44
  93.8 12.8 %front.1 = (bf16[1024,2048]{1,0:T(8,128)(2,1)}, bf16[1024,1408]{1,0:T(8,128)(2,1)}) custom-call(s32[8]{0:T(128)} %compare_select_fusion.2.members_ref, bf16[1024,2048]{1,0:T(8,128)(2,1)} %bitcast.121, bf16[1408,256]{1,0:T(8,128)(2,1)} %get-tuple-element.164.refs_0_.refs_9_, bf16[1408,256]{1,0:T(8,128)(2,1)} %copy-done.15, bf16[1408,256]{1,0:T(8,128)(2,1)} %copy-done.16, ...), custom_call_target="tpu_custom_call" | custom-call | flops 12000000000 | bytes 18000000 | tf_op jit(solution)/shard_map/front/pallas_call | solution.py:405
  115.7 19.1 %mix_forward.1 = (bf16[1024,1280]{1,0:T(8,128)(2,1)}, f32[4,128,128]{2,1,0:T(8,128)}, f32[1024,1024]{1,0:T(8,128)}, f32[4,8,128,128]{3,2,1,0:T(8,128)}) custom-call(bf16[1024,1408]{1,0:T(8,128)(2,1)} %get-tuple-element.162.proj_ref.refs_1_.refs_2_, f32[8,1280]{1,0:T(8,128)} %pad.14.taps_ref.refs_3_, f32[32,128]{1,0:T(8,128)} %broadcast_in_dim.38.heads_ref.refs_4_, ...), custom_call_target="tpu_custom_call" | custom-call | flops 17999998976 | bytes 15000000 | tf_op jit(solution)/shard_map/mix_forward/pallas_call | solution.py:557
  139.4 4.7 collective-permute-done.18.refs_6_
  149.6 8.6 %project.1.z_ref = bf16[1024,1024]{1,0:T(8,128)(2,1)} custom-call(bf16[1024,2048]{1,0:T(8,128)(2,1)} %get-tuple-element.217.normed_ref, bf16[1024,256]{1,0:T(8,128)(2,1)} %get-tuple-element.146.refs_0_, bf16[1024,256]{1,0:T(8,128)(2,1)} %collective-permute-done.5.refs_1_, bf16[1024,256]{1,0:T(8,128)(2,1)} %copy-done.38, bf16[1024,256]{1,0:T(8,128)(2,1)} %copy-done.26, ...), custom_call_target="tpu_custom_call" | custom-call | flops 8000000000 | bytes 10000000 | tf_op jit(solution)/shard_map/project/pallas_call | solution.py:436
  159.1 14.6 %gate_sums.1 = (bf16[1024,2048]{1,0:T(8,128)(2,1)}, f32[1024,1024]{1,0:T(8,128)}, f32[8,1024]{1,0:T(8,128)}) custom-call(s32[8]{0:T(128)} %compare_select_fusion.2.members_ref, bf16[1024,2048]{1,0:T(8,128)(2,1)} %bitcast.123, bf16[1024,1024]{1,0:T(8,128)(2,1)} %project.1.z_ref, f32[1024,1024]{1,0:T(8,128)} %get-tuple-element.175.y_ref, ...), custom_call_target="tpu_custom_call" | custom-call | flops 11000000512 | bytes 20000000 | tf_op jit(solution)/shard_map/gate_sums/pallas_call | solution.py:829
  173.6 12.3 %collective-permute-start.24 = (f32[8,1024]{1,0:T(8,128)}, f32[8,1024]{1,0:T(8,128)S(1)}, u32[]{:S(2)}, u32[]{:S(2)}) collective-permute-start(f32[8,1024]{1,0:T(8,128)} %get-tuple-element.184), channel_id=1, source_target_pairs={{0,1},{1,0},{2,3},{3,2},{4,5},{5,4},{6,7},{7,6},{8,9},{9,8},{10,11... | collective-permute-start | bytes 98312 | tf_op jit(solution)/shard_map/ppermute | solution.py:225
  196.1 10.9 %gate_back.1 = (bf16[1024,1024]{1,0:T(8,128)(2,1)}, bf16[1024,1024]{1,0:T(8,128)(2,1)}, bf16[1024,1024]{1,0:T(8,128)(2,1)}, f32[8,1024]{1,0:T(8,128)}) custom-call(f32[8,1024]{1,0:T(8,128)} %add_add_fusion.sums_ref, f32[1024,1024]{1,0:T(8,128)} %get-tuple-element.185.scaled_ref, bf16[1024,1024]{1,0:T(8,128)(2,1)} %project.1.z_ref, ...), custom_call_target="tpu_custom_call" | custom-call | flops 11000000512 | bytes 20000000 | tf_op jit(solution)/shard_map/gate_back/pallas_call | solution.py:885
  207.0 6.6 %convolution_convert_fusion.3 = bf16[1024,2048]{1,0:T(8,128)(2,1)S(1)} fusion(bf16[1024,1024]{1,0:T(8,128)(2,1)} %get-tuple-element.193, bf16[1,1024,2048]{2,1,0:T(8,128)(2,1)S(1)} %copy-done.35), kind=kOutput, calls=%fused_computation.5 | convolution fusion | flops 4297064448 | bytes 10485760 | tf_op jit(solution)/shard_map/dot_general | solution.py:238
  216.7 4.9 %convolution_convert_fusion.2 = bf16[1024,2048]{1,0:T(8,128)(2,1)S(1)} fusion(bf16[1024,1024]{1,0:T(8,128)(2,1)S(1)} %copy-done.51, bf16[1024,2048]{1,0:T(8,128)(2,1)S(1)} %copy-done.49), kind=kOutput, calls=%fused_computation.4 | convolution fusion | flops 4297064448 | bytes 10485760 | tf_op jit(solution)/shard_map/dot_general | solution.py:238
  223.2 4.7 %convolution_convert_fusion.1 = bf16[1024,2048]{1,0:T(8,128)(2,1)S(1)} fusion(bf16[1024,1024]{1,0:T(8,128)(2,1)S(1)} %copy-done.52, bf16[1024,2048]{1,0:T(8,128)(2,1)S(1)} %copy-done.53), kind=kOutput, calls=%fused_computation.3 | convolution fusion | flops 4297064448 | bytes 10485760 | tf_op jit(solution)/shard_map/dot_general | solution.py:234
  234.4 20.5 %mix_backward.2 = (bf16[1024,1408]{1,0:T(8,128)(2,1)}, f32[8,1280]{1,0:T(8,128)}, f32[32,256]{1,0:T(8,128)}, f32[8,128,128]{2,1,0:T(8,128)}, f32[8,1280]{1,0:T(8,128)}) custom-call(bf16[1024,1280]{1,0:T(8,128)(2,1)} %get-tuple-element.186.x_ref.refs_0_, bf16[1024,1408]{1,0:T(8,128)(2,1)} %get-tuple-element.162.proj_ref.refs_1_.refs_2_, ...), custom_call_target="tpu_custom_call" | custom-call | flops 24000000000 | bytes 10000000 | tf_op jit(solution)/shard_map/mix_backward/pallas_call | solution.py:739
  269.7 20.3 %mix_backward.3 = (bf16[1024,1408]{1,0:T(8,128)(2,1)}, f32[8,1280]{1,0:T(8,128)}, f32[32,256]{1,0:T(8,128)}, f32[8,128,128]{2,1,0:T(8,128)}, f32[8,1280]{1,0:T(8,128)}) custom-call(bf16[1024,1280]{1,0:T(8,128)(2,1)} %get-tuple-element.186.x_ref.refs_0_, ...), custom_call_target="tpu_custom_call", output_to_operand_aliasing={{0}: (11, {})} | custom-call | flops 24000000000 | bytes 10000000 | tf_op jit(solution)/shard_map/mix_backward/pallas_call | solution.py:739
  297.4 10.0 %convolution_convert_fusion.grads_ref = bf16[1408,2048]{1,0:T(8,128)(2,1)} fusion(bf16[1024,1408]{1,0:T(8,128)(2,1)} %get-tuple-element.222.dx_ref, bf16[1024,2048]{1,0:T(8,128)(2,1)S(1)} %copy-done.50), kind=kOutput, calls=%fused_computation | convolution fusion | flops 5908463616 | bytes 12845056 | tf_op jit(solution)/shard_map/dot_general | solution.py:238
  309.1 19.4 %back_norm.1 = (bf16[2,256,2048]{2,1,0:T(8,128)(2,1)}, bf16[2,256,2048]{2,1,0:T(8,128)(2,1)}, f32[8,2048]{1,0:T(8,128)}) custom-call(s32[8]{0:T(128)} %compare_select_fusion.2.members_ref, s32[1]{0:T(128)} %bitcast.2.place_ref, bf16[1024,2048]{1,0:T(8,128)(2,1)} %bitcast.122, bf16[1024,1024]{1,0:T(8,128)(2,1)} %get-tuple-element.191.dz_ref, ...), custom_call_target="tpu_custom_call" | custom-call | flops 17999998976 | bytes 24000000 | tf_op jit(solution)/shard_map/back_norm/pallas_call | solution.py:945
  348.0 16.1 %collective-permute-done.44 = bf16[544,256]{1,0:T(8,128)(2,1)S(1)} collective-permute-done((bf16[544,256]{1,0:T(8,128)(2,1)S(1)}, bf16[544,256]{1,0:T(8,128)(2,1)S(1)}, u32[]{:S(2)}, u32[]{:S(2)}) %collective-permute-start.44) | collective-permute-done | bytes 278560 | tf_op jit(solution)/shard_map/ppermute | solution.py:44
  379.8 8.5 %collective-permute-done.52 = f32[80,256]{1,0:T(8,128)S(1)} collective-permute-done((f32[80,256]{1,0:T(8,128)S(1)}, f32[80,256]{1,0:T(8,128)S(1)}, u32[]{:S(2)}, u32[]{:S(2)}) %collective-permute-start.52) | collective-permute-done | bytes 81952 | tf_op jit(solution)/shard_map/ppermute | solution.py:1272
  404.9 6.8 %collective-permute-done.54 = bf16[1312,256]{1,0:T(8,128)(2,1)S(1)} collective-permute-done((bf16[1312,256]{1,0:T(8,128)(2,1)S(1)}, bf16[1312,256]{1,0:T(8,128)(2,1)S(1)}, u32[]{:S(2)}, u32[]{:S(2)}) %collective-permute-start.54) | collective-permute-done | bytes 671776 | tf_op jit(solution)/shard_map/ppermute | solution.py:44
  422.3 5.1 %assemble_z.1.held_ref = f32[8512,256]{1,0:T(8,128)} custom-call(s32[1]{0:T(128)} %bitcast.2.place_ref, bf16[1024,256]{1,0:T(8,128)(2,1)} %add_convert_fusion.5.z0, bf16[1024,256]{1,0:T(8,128)(2,1)} %collective-permute-done.65.z1, bf16[1024,256]{1,0:T(8,128)(2,1)} %collective-permute-done.57.z2, bf16[1024,256]{1,0:T(8,128)(2,1)} %collective-permute-done.66.z3), custom_call_target="tpu_custom_call" | custom-call | flops 4000000000 | bytes 6000000 | tf_op jit(solution)/shard_map/assemble_z/pallas_call | solution.py:1030
  439.7 4.6 collective-permute-start.69
  (388 shorter events, 180.9 us)
Async XLA Ops:
  7.2 79.3 %all-gather.7.cloned.1.call-start = ((), (), s32[]{:S(2)}) async-start(), calls=%async_computation.1 | async-start | bytes 5242880 | tf_op jit(solution)/shard_map/all_gather | solution.py:1113
  7.9 150.3 %all-gather.5.cloned.1.call-start = ((), (), s32[]{:S(2)}) async-start(), calls=%async_computation | async-start | bytes 5242880 | tf_op jit(solution)/shard_map/all_gather | solution.py:1114
  52.7 24.9 %collective-permute-start.4 = (bf16[1024,256]{1,0:T(8,128)(2,1)}, bf16[1024,256]{1,0:T(8,128)(2,1)}, u32[]{:S(2)}, u32[]{:S(2)}) collective-permute-start(bf16[1024,256]{1,0:T(8,128)(2,1)} %get-tuple-element.146.refs_0_), channel_id=1, source_target_pairs={{0,8},{8,16},{16,24},{24,28},{28,20},{20,12},{12,4},{4,0},{1,9},{9... | collective-permute-start | bytes 1572872 | tf_op jit(solution)/shard_map/ppermute | solution.py:44
  54.0 24.6 %collective-permute-start.5 = (bf16[1024,256]{1,0:T(8,128)(2,1)}, bf16[1024,256]{1,0:T(8,128)(2,1)}, u32[]{:S(2)}, u32[]{:S(2)}) collective-permute-start(bf16[1024,256]{1,0:T(8,128)(2,1)} %get-tuple-element.146.refs_0_), channel_id=1, source_target_pairs={{8,0},{16,8},{24,16},{28,24},{20,28},{12,20},{4,12},{0,4},{9,1},{1... | collective-permute-start | bytes 1572872 | tf_op jit(solution)/shard_map/ppermute | solution.py:44
  112.1 22.8 %collective-permute-start.14 = (bf16[1024,256]{1,0:T(8,128)(2,1)S(1)}, bf16[1024,256]{1,0:T(8,128)(2,1)S(1)}, u32[]{:S(2)}, u32[]{:S(2)}) collective-permute-start(bf16[1024,256]{1,0:T(8,128)(2,1)S(1)} %collective-permute-done.10.refs_7_), channel_id=1, source_target_pairs={{0,8},{8,16},{16,24},{24,28},{28,20},{20,12},{12,4},{4,0},{1,9},{9... | collective-permute-start | bytes 1572872 | tf_op jit(solution)/shard_map/ppermute | solution.py:44
  112.4 22.5 %collective-permute-start.15 = (bf16[1024,256]{1,0:T(8,128)(2,1)S(1)}, bf16[1024,256]{1,0:T(8,128)(2,1)S(1)}, u32[]{:S(2)}, u32[]{:S(2)}) collective-permute-start(bf16[1024,256]{1,0:T(8,128)(2,1)S(1)} %collective-permute-done.11.refs_2_), channel_id=1, source_target_pairs={{8,0},{16,8},{24,16},{28,24},{20,28},{12,20},{4,12},{0,4},{9,1},{1... | collective-permute-start | bytes 1572872 | tf_op jit(solution)/shard_map/ppermute | solution.py:44
  230.2 30.8 %collective-permute-start.29 = (bf16[2,256,2048]{2,1,0:T(8,128)(2,1)S(1)}, bf16[2,256,2048]{2,1,0:T(8,128)(2,1)}, u32[]{:S(2)}, u32[]{:S(2)}) collective-permute-start(bf16[2,256,2048]{2,1,0:T(8,128)(2,1)S(1)} %dynamic-slice_bitcast_fusion), channel_id=1, source_target_pairs={{0,1},{1,0},{2,3},{3,2},{4,5},{5,4},{6,7},{7,6},{8,9},{9,8},{10,11... | collective-permute-start | bytes 6291464 | tf_op jit(solution)/shard_map/ppermute | solution.py:202
  231.3 23.6 %collective-permute-start.32 = (bf16[512,256]{1,0:T(8,128)(2,1)}, bf16[512,256]{1,0:T(8,128)(2,1)S(1)}, u32[]{:S(2)}, u32[]{:S(2)}) collective-permute-start(bf16[512,256]{1,0:T(8,128)(2,1)} %get-tuple-element.198), channel_id=1, source_target_pairs={{0,8},{8,16},{16,24},{24,28},{28,20},{20,12},{12,4},{4,0},{1,9},{9... | collective-permute-start | bytes 786440 | tf_op jit(solution)/shard_map/ppermute | solution.py:44
  232.1 22.8 %collective-permute-start.33 = (bf16[512,256]{1,0:T(8,128)(2,1)}, bf16[512,256]{1,0:T(8,128)(2,1)}, u32[]{:S(2)}, u32[]{:S(2)}) collective-permute-start(bf16[512,256]{1,0:T(8,128)(2,1)} %get-tuple-element.199), channel_id=1, source_target_pairs={{8,0},{16,8},{24,16},{28,24},{20,28},{12,20},{4,12},{0,4},{9,1},{1... | collective-permute-start | bytes 786440 | tf_op jit(solution)/shard_map/ppermute | solution.py:44
  232.8 25.0 %collective-permute-start.30 = (bf16[128,2048]{1,0:T(8,128)(2,1)S(1)}, bf16[128,2048]{1,0:T(8,128)(2,1)}, u32[]{:S(2)}, u32[]{:S(2)}) collective-permute-start(bf16[128,2048]{1,0:T(8,128)(2,1)S(1)} %pad_maximum_fusion.2), channel_id=1, source_target_pairs={{0,8},{8,16},{16,24},{24,28},{28,20},{20,12},{12,4},{4,0},{1,9},{9... | collective-permute-start | bytes 1572872 | tf_op jit(solution)/shard_map/ppermute | solution.py:44
  233.6 24.2 %collective-permute-start.31 = (bf16[128,2048]{1,0:T(8,128)(2,1)S(1)}, bf16[128,2048]{1,0:T(8,128)(2,1)}, u32[]{:S(2)}, u32[]{:S(2)}) collective-permute-start(bf16[128,2048]{1,0:T(8,128)(2,1)S(1)} %pad_maximum_fusion.3), channel_id=1, source_target_pairs={{8,0},{16,8},{24,16},{28,24},{20,28},{12,20},{4,12},{0,4},{9,1},{1... | collective-permute-start | bytes 1572872 | tf_op jit(solution)/shard_map/ppermute | solution.py:44
  265.6 24.5 %collective-permute-start.36 = (bf16[1024,256]{1,0:T(8,128)(2,1)}, bf16[1024,256]{1,0:T(8,128)(2,1)S(1)}, u32[]{:S(2)}, u32[]{:S(2)}) collective-permute-start(bf16[1024,256]{1,0:T(8,128)(2,1)} %pad_maximum_fusion.4), channel_id=1, source_target_pairs={{0,8},{8,16},{16,24},{24,28},{28,20},{20,12},{12,4},{4,0},{1,9},{9... | collective-permute-start | bytes 1572872 | tf_op jit(solution)/shard_map/ppermute | solution.py:44
  266.4 24.4 %collective-permute-start.37 = (bf16[1024,256]{1,0:T(8,128)(2,1)}, bf16[1024,256]{1,0:T(8,128)(2,1)}, u32[]{:S(2)}, u32[]{:S(2)}) collective-permute-start(bf16[1024,256]{1,0:T(8,128)(2,1)} %pad_maximum_fusion.5), channel_id=1, source_target_pairs={{8,0},{16,8},{24,16},{28,24},{20,28},{12,20},{4,12},{0,4},{9,1},{1... | collective-permute-start | bytes 1572872 | tf_op jit(solution)/shard_map/ppermute | solution.py:44
  267.1 26.3 %collective-permute-start.34 = (bf16[128,2048]{1,0:T(8,128)(2,1)}, bf16[128,2048]{1,0:T(8,128)(2,1)S(1)}, u32[]{:S(2)}, u32[]{:S(2)}) collective-permute-start(bf16[128,2048]{1,0:T(8,128)(2,1)} %get-tuple-element.206), channel_id=1, source_target_pairs={{0,8},{8,16},{16,24},{24,28},{28,20},{20,12},{12,4},{4,0},{1,9},{9... | collective-permute-start | bytes 1572872 | tf_op jit(solution)/shard_map/ppermute | solution.py:44
  267.9 25.5 %collective-permute-start.35 = (bf16[128,2048]{1,0:T(8,128)(2,1)S(1)}, bf16[128,2048]{1,0:T(8,128)(2,1)}, u32[]{:S(2)}, u32[]{:S(2)}) collective-permute-start(bf16[128,2048]{1,0:T(8,128)(2,1)S(1)} %get-tuple-element.207), channel_id=1, source_target_pairs={{8,0},{16,8},{24,16},{28,24},{20,28},{12,20},{4,12},{0,4},{9,1},{1... | collective-permute-start | bytes 1572872 | tf_op jit(solution)/shard_map/ppermute | solution.py:44
  268.5 27.4 %collective-permute-start.38 = (bf16[256,2048]{1,0:T(8,128)(2,1)S(1)}, bf16[256,2048]{1,0:T(8,128)(2,1)S(1)}, u32[]{:S(2)}, u32[]{:S(2)}) collective-permute-start(bf16[256,2048]{1,0:T(8,128)(2,1)S(1)} %fusion.6), channel_id=1, source_target_pairs={{0,2},{1,3},{2,0},{3,1},{4,6},{5,7},{6,4},{7,5},{8,10},{9,11},{10,... | collective-permute-start | bytes 3145736 | tf_op jit(solution)/shard_map/ppermute | solution.py:209
  295.9 38.1 %collective-permute-start.41 = (bf16[128,2048]{1,0:T(8,128)(2,1)}, bf16[128,2048]{1,0:T(8,128)(2,1)S(1)}, u32[]{:S(2)}, u32[]{:S(2)}) collective-permute-start(bf16[128,2048]{1,0:T(8,128)(2,1)} %get-tuple-element.231), channel_id=1, source_target_pairs={{0,8},{8,16},{16,24},{24,28},{28,20},{20,12},{12,4},{4,0},{1,9},{9... | collective-permute-start | bytes 1572872 | tf_op jit(solution)/shard_map/ppermute | solution.py:44
  296.8 37.3 %collective-permute-start.42 = (bf16[128,2048]{1,0:T(8,128)(2,1)S(1)}, bf16[128,2048]{1,0:T(8,128)(2,1)S(1)}, u32[]{:S(2)}, u32[]{:S(2)}) collective-permute-start(bf16[128,2048]{1,0:T(8,128)(2,1)S(1)} %get-tuple-element.232), channel_id=1, source_target_pairs={{8,0},{16,8},{24,16},{28,24},{20,28},{12,20},{4,12},{0,4},{9,1},{1... | collective-permute-start | bytes 1572872 | tf_op jit(solution)/shard_map/ppermute | solution.py:44
  307.4 24.7 %collective-permute-start.39 = (bf16[1024,256]{1,0:T(8,128)(2,1)}, bf16[1024,256]{1,0:T(8,128)(2,1)}, u32[]{:S(2)}, u32[]{:S(2)}) collective-permute-start(bf16[1024,256]{1,0:T(8,128)(2,1)} %get-tuple-element.220), channel_id=1, source_target_pairs={{0,8},{8,16},{16,24},{24,28},{28,20},{20,12},{12,4},{4,0},{1,9},{9... | collective-permute-start | bytes 1572872 | tf_op jit(solution)/shard_map/ppermute | solution.py:44
  308.2 23.9 %collective-permute-start.40 = (bf16[1024,256]{1,0:T(8,128)(2,1)S(1)}, bf16[1024,256]{1,0:T(8,128)(2,1)}, u32[]{:S(2)}, u32[]{:S(2)}) collective-permute-start(bf16[1024,256]{1,0:T(8,128)(2,1)S(1)} %get-tuple-element.221), channel_id=1, source_target_pairs={{8,0},{16,8},{24,16},{28,24},{20,28},{12,20},{4,12},{0,4},{9,1},{1... | collective-permute-start | bytes 1572872 | tf_op jit(solution)/shard_map/ppermute | solution.py:44
  343.0 25.1 %collective-permute-start.48 = (bf16[1024,256]{1,0:T(8,128)(2,1)S(1)}, bf16[1024,256]{1,0:T(8,128)(2,1)S(1)}, u32[]{:S(2)}, u32[]{:S(2)}) collective-permute-start(bf16[1024,256]{1,0:T(8,128)(2,1)S(1)} %get-tuple-element.240), channel_id=1, source_target_pairs={{0,8},{8,16},{16,24},{24,28},{28,20},{20,12},{12,4},{4,0},{1,9},{9... | collective-permute-start | bytes 1572872 | tf_op jit(solution)/shard_map/ppermute | solution.py:44
  343.2 24.9 %collective-permute-start.49 = (bf16[1024,256]{1,0:T(8,128)(2,1)S(1)}, bf16[1024,256]{1,0:T(8,128)(2,1)S(1)}, u32[]{:S(2)}, u32[]{:S(2)}) collective-permute-start(bf16[1024,256]{1,0:T(8,128)(2,1)S(1)} %get-tuple-element.241), channel_id=1, source_target_pairs={{8,0},{16,8},{24,16},{28,24},{20,28},{12,20},{4,12},{0,4},{9,1},{1... | collective-permute-start | bytes 1572872 | tf_op jit(solution)/shard_map/ppermute | solution.py:44
  347.7 23.8 %collective-permute-start.46 = (bf16[256,2048]{1,0:T(8,128)(2,1)S(1)}, bf16[256,2048]{1,0:T(8,128)(2,1)S(1)}, u32[]{:S(2)}, u32[]{:S(2)}) collective-permute-start(bf16[256,2048]{1,0:T(8,128)(2,1)S(1)} %fusion.7), channel_id=1, source_target_pairs={{0,2},{1,3},{2,0},{3,1},{4,6},{5,7},{6,4},{7,5},{8,10},{9,11},{10,... | collective-permute-start | bytes 3145736 | tf_op jit(solution)/shard_map/ppermute | solution.py:209
  374.0 25.3 %collective-permute-start.58 = (bf16[128,2048]{1,0:T(8,128)(2,1)}, bf16[128,2048]{1,0:T(8,128)(2,1)S(1)}, u32[]{:S(2)}, u32[]{:S(2)}) collective-permute-start(bf16[128,2048]{1,0:T(8,128)(2,1)} %add_convert_fusion.6.o0), channel_id=1, source_target_pairs={{0,1},{1,0},{2,3},{3,2},{4,5},{5,4},{6,7},{7,6},{8,9},{9,8},{10,11... | collective-permute-start | bytes 1572872 | tf_op jit(solution)/shard_map/ppermute | solution.py:157
  (105 other events, 1444.1 us)
Sparse Core Ops, SparseCore 0:
  9.6 36.9 all-gather.6
  48.1 34.4 all-gather.4

commit v4 on v3

--- a/solution.py
+++ b/solution.py
@@ -20,6 +20,7 @@
 HALO = 8
 SMALL = 32
 TAIL = 32
+ENDS = 64
 VMEM_LIMIT = 56 * 1024 * 1024
 F32 = jnp.float32
 BF16 = jnp.bfloat16
@@ -325,7 +326,7 @@
     have = lax.broadcasted_iota(jnp.int32, (2 * pairs, HEADS), 1)
     head = (want % pairs) * 2 * m + 2 * place + want // pairs
     rows[: 2 * pairs, :] = nn((have == head).astype(BF16), steps[...])
-    x_ref[core : core + PAIR, :] = rows[...].astype(BF16)
+    x_ref[core : core + ENDS, :] = rows[...].astype(BF16)
     for copy in copies[1:]:
         copy.wait()
 
@@ -334,7 +335,7 @@
     rows = columns.shape[1]
     core = pairs * PAIR + 2 * STATE
     anywhere = pl.BlockSpec(memory_space=pl.ANY)
-    shapes = [(core + PAIR, rows), (pairs * PAIR, rows), (PAIR, D)]
+    shapes = [(core + ENDS, rows), (pairs * PAIR, rows), (PAIR, D)]
     return pl.pallas_call(
         pack,
         grid_spec=pltpu.PrefetchScalarGridSpec(
@@ -344,7 +345,7 @@
             out_specs=[pl.BlockSpec(shape, lambda i, t: (0, 0)) for shape in shapes],
             scratch_shapes=[
                 pltpu.VMEM((HEADS, rows), BF16),
-                pltpu.VMEM((PAIR, rows), F32),
+                pltpu.VMEM((ENDS, rows), F32),
                 pltpu.SemaphoreType.DMA((2 * pairs + 3,)),
             ],
         ),
@@ -363,7 +364,7 @@
 def run_collect(members, parts):
     n = len(parts) - 1
     lasts = parts[: n // 2] + parts[n // 2 + 1 :]
-    at = lambda part: (part.shape[0] - PAIR + SMALL) // 32
+    at = lambda part: (part.shape[0] - ENDS + SMALL) // 32
     return pl.pallas_call(
         collect,
         grid_spec=pltpu.PrefetchScalarGridSpec(
@@ -387,7 +388,7 @@
         at = pl.multiple_of(members_ref[o] * SEG, SEG)
         cols = slice(o * SEG, (o + 1) * SEG)
         last = weights[o if o < D // SEG // 2 else o + 1]
-        row = last.shape[0] - PAIR + SMALL
+        row = last.shape[0] - ENDS + SMALL
         gain = last[row : row + 16, :].astype(F32)[0:1]
         part = tokens_ref[:, pl.ds(at, SEG)].astype(F32) * inv * gain
         normed_ref[:, cols] = part.astype(BF16)
@@ -509,7 +510,7 @@
 
     bs = activate(slice(width, width + STATE))
     cs = activate(slice(width + STATE, core))
-    raw = proj_ref[:, core : core + PAIR].astype(F32).T[:heads]
+    raw = proj_ref[:, core : core + ENDS].astype(F32).T[:heads]
     dt = softplus(raw + heads_ref[:heads, 0:1])
     upto = ones_where(lambda row, col: row <= col).astype(F32)
     cum = exact(dt * heads_ref[heads:, 0:1], upto)
@@ -718,13 +719,13 @@
     d_cum = touched * growth - tail_log + sum_j - dt * sum_i
     d_cum = d_cum + jnp.where(lanes(d_cum.shape) == GROUP - 1, d_last, 0.0)
     d_rate = exact(d_cum, ones_where(lambda row, col: row >= col).astype(F32))
-    raw = proj_ref[:, core : core + PAIR].astype(F32).T[:heads]
+    raw = proj_ref[:, core : core + ENDS].astype(F32).T[:heads]
     d_step = d_tail * jnp.exp(cum[:, GROUP - 1 :] - cum) + sum_i
     d_dt = (d_step + d_rate * a_neg) * sigmoid(raw + heads_ref[:heads, 0:1])
     dheads_ref[:heads, :] += d_dt
     dheads_ref[heads:, :] += d_rate * dt
-    filled = jnp.concatenate([d_dt, jnp.zeros((PAIR - heads, GROUP), F32)], axis=0)
-    dx_ref[:, core : core + PAIR] = filled.T.astype(BF16)
+    filled = jnp.concatenate([d_dt, jnp.zeros((ENDS - heads, GROUP), F32)], axis=0)
+    dx_ref[:, core : core + ENDS] = filled.T.astype(BF16)
 
 
 def run_mix_backward(span, top, act, proj, taps, heads_in, skip, table, starts, dy, before):
@@ -1115,7 +1116,7 @@
 
 
     columns = w_in.T
-    total_cols = core_cols + PAIR
+    total_cols = core_cols + ENDS
     cut = halves(total_cols)[0]
     place_ref = place.reshape(1).astype(jnp.int32)
     smalls = [norm_gain[None], gate_gain[None], conv_b[None], conv_w]
@@ -1151,7 +1152,7 @@
                 of_pairs(columns[DI : 2 * DI], 0),
                 columns[2 * DI : 2 * DI + 2 * STATE],
                 of_heads(columns[DI + CONV :]),
-                jnp.zeros((PAIR - heads, rows), BF16),
+                jnp.zeros((ENDS - heads, rows), BF16),
             ],
             axis=0,
         )

time: 476 us -> 473 us (level)
  no operation moved by 1% of the time
where the time goes in v4:
time: 473 us; the launch traced here: 466 us
  Pallas kernels  151 us (32%)
  waiting for transfers between devices  115 us (24%)
  starting transfers between devices  79.8 us (17%)
  other arithmetic  39.1 us (8%)
  local copies, waits for them, and re-layouts  33.7 us (7%)
  matrix products  25.8 us (5%)
  between operations  20.7 us (4%)
    ppermute x48, waiting for transfers between devices, send(): return lax.ppermute(block, 'fsdp', route)  98.6 us
    pallas_call x2, Pallas kernels, run_mix_backward(): pl.pallas_call(lambda *refs: mix_backward(top, follows, *refs), grid=(spa...  40.7 us
    ppermute x48, starting transfers between devices, send(): return lax.ppermute(block, 'fsdp', route)  37.1 us
    dot_general x3, matrix products, tn(): lax.dot_general(a, b, (((0,), (0,)), ((), ())), preferred_element_type=F32)  21.1 us
    pallas_call x1, Pallas kernels, run_back_norm(): pl.pallas_call(back_norm, grid_spec=pltpu.PrefetchScalarGridSpec(num_scal...  19.4 us
    pallas_call x1, Pallas kernels, run_mix_forward(): pl.pallas_call(mix_forward, grid=(blocks,), in_specs=[pl.BlockSpec((GROUP...  19.1 us
    pallas_call x1, Pallas kernels, run_gate_sums(): pl.pallas_call(gate_sums, grid_spec=pltpu.PrefetchScalarGridSpec(num_scal...  14.6 us
    convert_element_type x6, other arithmetic, join(): self.right, self.left = (right.astype(BF16), left.astype(BF16))  14 us
  transfers between devices with their start and end apart: 75, of which 27 were waited for; matrix products, arithmetic and copies ran while one was open for 14% of the time, Pallas kernels for 26%

profile of v4, /device:TPU:1, one launch (start us, length us, event | category | flops | bytes accessed | tf_op | source)
XLA Modules:
  0.0 465.7 jit_solution(2981518522705377015)
XLA Ops:
  16.4 15.4 %collective-permute-done.refs_8_.refs_7_.refs_17_ = bf16[1344,256]{1,0:T(8,128)(2,1)S(1)} collective-permute-done((bf16[1344,256]{1,0:T(8,128)(2,1)}, bf16[1344,256]{1,0:T(8,128)(2,1)S(1)}, u32[]{:S(2)}, u32[]{:S(2)}) %collective-permute-start) | collective-permute-done | bytes 688160 | tf_op jit(solution)/shard_map/ppermute | solution.py:45
  34.1 13.8 %collective-permute-done.2.refs_7_.refs_6_.refs_16_ = bf16[1344,256]{1,0:T(8,128)(2,1)} collective-permute-done((bf16[1344,256]{1,0:T(8,128)(2,1)S(1)}, bf16[1344,256]{1,0:T(8,128)(2,1)}, u32[]{:S(2)}, u32[]{:S(2)}) %collective-permute-start.2) | collective-permute-done | bytes 688160 | tf_op jit(solution)/shard_map/ppermute | solution.py:45
  53.5 10.7 %collective-permute-done.7.refs_6_.refs_5_.refs_15_ = bf16[1344,256]{1,0:T(8,128)(2,1)S(1)} collective-permute-done((bf16[1344,256]{1,0:T(8,128)(2,1)}, bf16[1344,256]{1,0:T(8,128)(2,1)S(1)}, u32[]{:S(2)}, u32[]{:S(2)}) %collective-permute-start.7) | collective-permute-done | bytes 688160 | tf_op jit(solution)/shard_map/ppermute | solution.py:45
  66.0 9.4 %collective-permute-done.4.refs_8_ = bf16[1024,256]{1,0:T(8,128)(2,1)} collective-permute-done((bf16[1024,256]{1,0:T(8,128)(2,1)}, bf16[1024,256]{1,0:T(8,128)(2,1)}, u32[]{:S(2)}, u32[]{:S(2)}) %collective-permute-start.4) | collective-permute-done | bytes 524320 | tf_op jit(solution)/shard_map/ppermute | solution.py:45
  79.3 4.6 collective-permute-done.9.refs_5_.refs_4_.refs_14_
  91.4 12.7 %front.1 = (bf16[1024,2048]{1,0:T(8,128)(2,1)}, bf16[1024,1344]{1,0:T(8,128)(2,1)}) custom-call(s32[8]{0:T(128)} %compare_select_fusion.2.members_ref, bf16[1024,2048]{1,0:T(8,128)(2,1)} %bitcast.121, bf16[1344,256]{1,0:T(8,128)(2,1)} %get-tuple-element.164.refs_0_.refs_9_, bf16[1344,256]{1,0:T(8,128)(2,1)} %copy-done.15, bf16[1344,256]{1,0:T(8,128)(2,1)} %copy-done.16, ...), custom_call_target="tpu_custom_call" | custom-call | flops 12000000000 | bytes 18000000 | tf_op jit(solution)/shard_map/front/pallas_call | solution.py:406
  112.7 19.1 %mix_forward.1 = (bf16[1024,1280]{1,0:T(8,128)(2,1)}, f32[4,128,128]{2,1,0:T(8,128)}, f32[1024,1024]{1,0:T(8,128)}, f32[4,8,128,128]{3,2,1,0:T(8,128)}) custom-call(bf16[1024,1344]{1,0:T(8,128)(2,1)} %get-tuple-element.162.proj_ref.refs_1_.refs_2_, f32[8,1280]{1,0:T(8,128)} %pad.14.taps_ref.refs_3_, f32[32,128]{1,0:T(8,128)} %broadcast_in_dim.38.heads_ref.refs_4_, ...), custom_call_target="tpu_custom_call" | custom-call | flops 17999998976 | bytes 15000000 | tf_op jit(solution)/shard_map/mix_forward/pallas_call | solution.py:558
  136.4 5.2 %collective-permute-done.18.refs_6_ = bf16[128,2048]{1,0:T(8,128)(2,1)S(1)} collective-permute-done((bf16[128,2048]{1,0:T(8,128)(2,1)}, bf16[128,2048]{1,0:T(8,128)(2,1)S(1)}, u32[]{:S(2)}, u32[]{:S(2)}) %collective-permute-start.18) | collective-permute-done | bytes 524320 | tf_op jit(solution)/shard_map/ppermute | solution.py:45
  147.3 8.6 %project.1.z_ref = bf16[1024,1024]{1,0:T(8,128)(2,1)} custom-call(bf16[1024,2048]{1,0:T(8,128)(2,1)} %get-tuple-element.217.normed_ref, bf16[1024,256]{1,0:T(8,128)(2,1)} %get-tuple-element.146.refs_0_, bf16[1024,256]{1,0:T(8,128)(2,1)} %collective-permute-done.5.refs_1_, bf16[1024,256]{1,0:T(8,128)(2,1)} %copy-done.38, bf16[1024,256]{1,0:T(8,128)(2,1)} %copy-done.26, ...), custom_call_target="tpu_custom_call" | custom-call | flops 8000000000 | bytes 10000000 | tf_op jit(solution)/shard_map/project/pallas_call | solution.py:437
  156.8 14.6 %gate_sums.1 = (bf16[1024,2048]{1,0:T(8,128)(2,1)}, f32[1024,1024]{1,0:T(8,128)}, f32[8,1024]{1,0:T(8,128)}) custom-call(s32[8]{0:T(128)} %compare_select_fusion.2.members_ref, bf16[1024,2048]{1,0:T(8,128)(2,1)} %bitcast.123, bf16[1024,1024]{1,0:T(8,128)(2,1)} %project.1.z_ref, f32[1024,1024]{1,0:T(8,128)} %get-tuple-element.175.y_ref, ...), custom_call_target="tpu_custom_call" | custom-call | flops 11000000512 | bytes 20000000 | tf_op jit(solution)/shard_map/gate_sums/pallas_call | solution.py:830
  171.4 11.9 %collective-permute-start.24 = (f32[8,1024]{1,0:T(8,128)}, f32[8,1024]{1,0:T(8,128)S(1)}, u32[]{:S(2)}, u32[]{:S(2)}) collective-permute-start(f32[8,1024]{1,0:T(8,128)} %get-tuple-element.184), channel_id=1, source_target_pairs={{0,1},{1,0},{2,3},{3,2},{4,5},{5,4},{6,7},{7,6},{8,9},{9,8},{10,11... | collective-permute-start | bytes 98312 | tf_op jit(solution)/shard_map/ppermute | solution.py:226
  193.2 10.9 %gate_back.1 = (bf16[1024,1024]{1,0:T(8,128)(2,1)}, bf16[1024,1024]{1,0:T(8,128)(2,1)}, bf16[1024,1024]{1,0:T(8,128)(2,1)}, f32[8,1024]{1,0:T(8,128)}) custom-call(f32[8,1024]{1,0:T(8,128)} %add_add_fusion.sums_ref, f32[1024,1024]{1,0:T(8,128)} %get-tuple-element.185.scaled_ref, bf16[1024,1024]{1,0:T(8,128)(2,1)} %project.1.z_ref, ...), custom_call_target="tpu_custom_call" | custom-call | flops 11000000512 | bytes 20000000 | tf_op jit(solution)/shard_map/gate_back/pallas_call | solution.py:886
  204.2 6.6 %convolution_convert_fusion.3 = bf16[1024,2048]{1,0:T(8,128)(2,1)S(1)} fusion(bf16[1024,1024]{1,0:T(8,128)(2,1)} %get-tuple-element.193, bf16[1,1024,2048]{2,1,0:T(8,128)(2,1)S(1)} %copy-done.35), kind=kOutput, calls=%fused_computation.5 | convolution fusion | flops 4297064448 | bytes 10485760 | tf_op jit(solution)/shard_map/dot_general | solution.py:239
  213.9 4.9 %convolution_convert_fusion.2 = bf16[1024,2048]{1,0:T(8,128)(2,1)S(1)} fusion(bf16[1024,1024]{1,0:T(8,128)(2,1)S(1)} %copy-done.51, bf16[1024,2048]{1,0:T(8,128)(2,1)S(1)} %copy-done.49), kind=kOutput, calls=%fused_computation.4 | convolution fusion | flops 4297064448 | bytes 10485760 | tf_op jit(solution)/shard_map/dot_general | solution.py:239
  220.3 4.7 %convolution_convert_fusion.1 = bf16[1024,2048]{1,0:T(8,128)(2,1)S(1)} fusion(bf16[1024,1024]{1,0:T(8,128)(2,1)S(1)} %copy-done.52, bf16[1024,2048]{1,0:T(8,128)(2,1)S(1)} %copy-done.53), kind=kOutput, calls=%fused_computation.3 | convolution fusion | flops 4297064448 | bytes 10485760 | tf_op jit(solution)/shard_map/dot_general | solution.py:235
  232.1 20.4 %mix_backward.2 = (bf16[1024,1344]{1,0:T(8,128)(2,1)}, f32[8,1280]{1,0:T(8,128)}, f32[32,256]{1,0:T(8,128)}, f32[8,128,128]{2,1,0:T(8,128)}, f32[8,1280]{1,0:T(8,128)}) custom-call(bf16[1024,1280]{1,0:T(8,128)(2,1)} %get-tuple-element.186.x_ref.refs_0_, bf16[1024,1344]{1,0:T(8,128)(2,1)} %get-tuple-element.162.proj_ref.refs_1_.refs_2_, ...), custom_call_target="tpu_custom_call" | custom-call | flops 24000000000 | bytes 10000000 | tf_op jit(solution)/shard_map/mix_backward/pallas_call | solution.py:740
  267.4 20.3 %mix_backward.3 = (bf16[1024,1344]{1,0:T(8,128)(2,1)}, f32[8,1280]{1,0:T(8,128)}, f32[32,256]{1,0:T(8,128)}, f32[8,128,128]{2,1,0:T(8,128)}, f32[8,1280]{1,0:T(8,128)}) custom-call(bf16[1024,1280]{1,0:T(8,128)(2,1)} %get-tuple-element.186.x_ref.refs_0_, ...), custom_call_target="tpu_custom_call", output_to_operand_aliasing={{0}: (11, {})} | custom-call | flops 24000000000 | bytes 10000000 | tf_op jit(solution)/shard_map/mix_backward/pallas_call | solution.py:740
  295.0 9.6 %convolution_convert_fusion.grads_ref = bf16[1344,2048]{1,0:T(8,128)(2,1)} fusion(bf16[1024,1344]{1,0:T(8,128)(2,1)} %get-tuple-element.222.dx_ref, bf16[1024,2048]{1,0:T(8,128)(2,1)S(1)} %copy-done.50), kind=kOutput, calls=%fused_computation | convolution fusion | flops 5639897088 | bytes 12451840 | tf_op jit(solution)/shard_map/dot_general | solution.py:239
  306.4 19.4 %back_norm.1 = (bf16[2,256,2048]{2,1,0:T(8,128)(2,1)}, bf16[2,256,2048]{2,1,0:T(8,128)(2,1)}, f32[8,2048]{1,0:T(8,128)}) custom-call(s32[8]{0:T(128)} %compare_select_fusion.2.members_ref, s32[1]{0:T(128)} %bitcast.2.place_ref, bf16[1024,2048]{1,0:T(8,128)(2,1)} %bitcast.122, bf16[1024,1024]{1,0:T(8,128)(2,1)} %get-tuple-element.191.dz_ref, ...), custom_call_target="tpu_custom_call" | custom-call | flops 17999998976 | bytes 24000000 | tf_op jit(solution)/shard_map/back_norm/pallas_call | solution.py:946
  345.3 16.0 %collective-permute-done.44 = bf16[544,256]{1,0:T(8,128)(2,1)S(1)} collective-permute-done((bf16[544,256]{1,0:T(8,128)(2,1)S(1)}, bf16[544,256]{1,0:T(8,128)(2,1)S(1)}, u32[]{:S(2)}, u32[]{:S(2)}) %collective-permute-start.44) | collective-permute-done | bytes 278560 | tf_op jit(solution)/shard_map/ppermute | solution.py:45
  377.0 8.4 %collective-permute-done.52 = f32[80,256]{1,0:T(8,128)S(1)} collective-permute-done((f32[80,256]{1,0:T(8,128)S(1)}, f32[80,256]{1,0:T(8,128)S(1)}, u32[]{:S(2)}, u32[]{:S(2)}) %collective-permute-start.52) | collective-permute-done | bytes 81952 | tf_op jit(solution)/shard_map/ppermute | solution.py:1273
  402.1 6.8 %collective-permute-done.54 = bf16[1312,256]{1,0:T(8,128)(2,1)S(1)} collective-permute-done((bf16[1312,256]{1,0:T(8,128)(2,1)S(1)}, bf16[1312,256]{1,0:T(8,128)(2,1)S(1)}, u32[]{:S(2)}, u32[]{:S(2)}) %collective-permute-start.54) | collective-permute-done | bytes 671776 | tf_op jit(solution)/shard_map/ppermute | solution.py:45
  419.5 5.1 %assemble_z.1.held_ref = f32[8512,256]{1,0:T(8,128)} custom-call(s32[1]{0:T(128)} %bitcast.2.place_ref, bf16[1024,256]{1,0:T(8,128)(2,1)} %add_convert_fusion.5.z0, bf16[1024,256]{1,0:T(8,128)(2,1)} %collective-permute-done.65.z1, bf16[1024,256]{1,0:T(8,128)(2,1)} %collective-permute-done.57.z2, bf16[1024,256]{1,0:T(8,128)(2,1)} %collective-permute-done.66.z3), custom_call_target="tpu_custom_call" | custom-call | flops 4000000000 | bytes 6000000 | tf_op jit(solution)/shard_map/assemble_z/pallas_call | solution.py:1031
  436.9 4.5 collective-permute-start.69
  (388 shorter events, 181.4 us)
Async XLA Ops:
  7.2 76.8 %all-gather.7.cloned.1.call-start = ((), (), s32[]{:S(2)}) async-start(), calls=%async_computation.1 | async-start | bytes 5242880 | tf_op jit(solution)/shard_map/all_gather | solution.py:1114
  7.9 148.1 %all-gather.5.cloned.1.call-start = ((), (), s32[]{:S(2)}) async-start(), calls=%async_computation | async-start | bytes 5242880 | tf_op jit(solution)/shard_map/all_gather | solution.py:1115
  51.3 24.2 %collective-permute-start.4 = (bf16[1024,256]{1,0:T(8,128)(2,1)}, bf16[1024,256]{1,0:T(8,128)(2,1)}, u32[]{:S(2)}, u32[]{:S(2)}) collective-permute-start(bf16[1024,256]{1,0:T(8,128)(2,1)} %get-tuple-element.146.refs_0_), channel_id=1, source_target_pairs={{0,8},{8,16},{16,24},{24,28},{28,20},{20,12},{12,4},{4,0},{1,9},{9... | collective-permute-start | bytes 1572872 | tf_op jit(solution)/shard_map/ppermute | solution.py:45
  52.6 23.9 %collective-permute-start.5 = (bf16[1024,256]{1,0:T(8,128)(2,1)}, bf16[1024,256]{1,0:T(8,128)(2,1)}, u32[]{:S(2)}, u32[]{:S(2)}) collective-permute-start(bf16[1024,256]{1,0:T(8,128)(2,1)} %get-tuple-element.146.refs_0_), channel_id=1, source_target_pairs={{8,0},{16,8},{24,16},{28,24},{20,28},{12,20},{4,12},{0,4},{9,1},{1... | collective-permute-start | bytes 1572872 | tf_op jit(solution)/shard_map/ppermute | solution.py:45
  109.1 22.7 %collective-permute-start.14 = (bf16[1024,256]{1,0:T(8,128)(2,1)S(1)}, bf16[1024,256]{1,0:T(8,128)(2,1)S(1)}, u32[]{:S(2)}, u32[]{:S(2)}) collective-permute-start(bf16[1024,256]{1,0:T(8,128)(2,1)S(1)} %collective-permute-done.10.refs_7_), channel_id=1, source_target_pairs={{0,8},{8,16},{16,24},{24,28},{28,20},{20,12},{12,4},{4,0},{1,9},{9... | collective-permute-start | bytes 1572872 | tf_op jit(solution)/shard_map/ppermute | solution.py:45
  110.2 21.7 %collective-permute-start.15 = (bf16[1024,256]{1,0:T(8,128)(2,1)S(1)}, bf16[1024,256]{1,0:T(8,128)(2,1)S(1)}, u32[]{:S(2)}, u32[]{:S(2)}) collective-permute-start(bf16[1024,256]{1,0:T(8,128)(2,1)S(1)} %collective-permute-done.11.refs_2_), channel_id=1, source_target_pairs={{8,0},{16,8},{24,16},{28,24},{20,28},{12,20},{4,12},{0,4},{9,1},{1... | collective-permute-start | bytes 1572872 | tf_op jit(solution)/shard_map/ppermute | solution.py:45
  227.7 31.0 %collective-permute-start.29 = (bf16[2,256,2048]{2,1,0:T(8,128)(2,1)S(1)}, bf16[2,256,2048]{2,1,0:T(8,128)(2,1)}, u32[]{:S(2)}, u32[]{:S(2)}) collective-permute-start(bf16[2,256,2048]{2,1,0:T(8,128)(2,1)S(1)} %dynamic-slice_bitcast_fusion), channel_id=1, source_target_pairs={{0,1},{1,0},{2,3},{3,2},{4,5},{5,4},{6,7},{7,6},{8,9},{9,8},{10,11... | collective-permute-start | bytes 6291464 | tf_op jit(solution)/shard_map/ppermute | solution.py:203
  229.0 23.6 %collective-permute-start.32 = (bf16[512,256]{1,0:T(8,128)(2,1)}, bf16[512,256]{1,0:T(8,128)(2,1)S(1)}, u32[]{:S(2)}, u32[]{:S(2)}) collective-permute-start(bf16[512,256]{1,0:T(8,128)(2,1)} %get-tuple-element.198), channel_id=1, source_target_pairs={{0,8},{8,16},{16,24},{24,28},{28,20},{20,12},{12,4},{4,0},{1,9},{9... | collective-permute-start | bytes 786440 | tf_op jit(solution)/shard_map/ppermute | solution.py:45
  229.9 22.7 %collective-permute-start.33 = (bf16[512,256]{1,0:T(8,128)(2,1)}, bf16[512,256]{1,0:T(8,128)(2,1)}, u32[]{:S(2)}, u32[]{:S(2)}) collective-permute-start(bf16[512,256]{1,0:T(8,128)(2,1)} %get-tuple-element.199), channel_id=1, source_target_pairs={{8,0},{16,8},{24,16},{28,24},{20,28},{12,20},{4,12},{0,4},{9,1},{1... | collective-permute-start | bytes 786440 | tf_op jit(solution)/shard_map/ppermute | solution.py:45
  230.5 24.9 %collective-permute-start.30 = (bf16[128,2048]{1,0:T(8,128)(2,1)S(1)}, bf16[128,2048]{1,0:T(8,128)(2,1)}, u32[]{:S(2)}, u32[]{:S(2)}) collective-permute-start(bf16[128,2048]{1,0:T(8,128)(2,1)S(1)} %pad_maximum_fusion.2), channel_id=1, source_target_pairs={{0,8},{8,16},{16,24},{24,28},{28,20},{20,12},{12,4},{4,0},{1,9},{9... | collective-permute-start | bytes 1572872 | tf_op jit(solution)/shard_map/ppermute | solution.py:45
  231.4 24.0 %collective-permute-start.31 = (bf16[128,2048]{1,0:T(8,128)(2,1)S(1)}, bf16[128,2048]{1,0:T(8,128)(2,1)}, u32[]{:S(2)}, u32[]{:S(2)}) collective-permute-start(bf16[128,2048]{1,0:T(8,128)(2,1)S(1)} %pad_maximum_fusion.3), channel_id=1, source_target_pairs={{8,0},{16,8},{24,16},{28,24},{20,28},{12,20},{4,12},{0,4},{9,1},{1... | collective-permute-start | bytes 1572872 | tf_op jit(solution)/shard_map/ppermute | solution.py:45
  263.2 24.5 %collective-permute-start.36 = (bf16[1024,256]{1,0:T(8,128)(2,1)}, bf16[1024,256]{1,0:T(8,128)(2,1)S(1)}, u32[]{:S(2)}, u32[]{:S(2)}) collective-permute-start(bf16[1024,256]{1,0:T(8,128)(2,1)} %pad_maximum_fusion.4), channel_id=1, source_target_pairs={{0,8},{8,16},{16,24},{24,28},{28,20},{20,12},{12,4},{4,0},{1,9},{9... | collective-permute-start | bytes 1572872 | tf_op jit(solution)/shard_map/ppermute | solution.py:45
  264.1 24.4 %collective-permute-start.37 = (bf16[1024,256]{1,0:T(8,128)(2,1)}, bf16[1024,256]{1,0:T(8,128)(2,1)}, u32[]{:S(2)}, u32[]{:S(2)}) collective-permute-start(bf16[1024,256]{1,0:T(8,128)(2,1)} %pad_maximum_fusion.5), channel_id=1, source_target_pairs={{8,0},{16,8},{24,16},{28,24},{20,28},{12,20},{4,12},{0,4},{9,1},{1... | collective-permute-start | bytes 1572872 | tf_op jit(solution)/shard_map/ppermute | solution.py:45
  264.7 26.3 %collective-permute-start.34 = (bf16[128,2048]{1,0:T(8,128)(2,1)}, bf16[128,2048]{1,0:T(8,128)(2,1)S(1)}, u32[]{:S(2)}, u32[]{:S(2)}) collective-permute-start(bf16[128,2048]{1,0:T(8,128)(2,1)} %get-tuple-element.206), channel_id=1, source_target_pairs={{0,8},{8,16},{16,24},{24,28},{28,20},{20,12},{12,4},{4,0},{1,9},{9... | collective-permute-start | bytes 1572872 | tf_op jit(solution)/shard_map/ppermute | solution.py:45
  265.6 25.4 %collective-permute-start.35 = (bf16[128,2048]{1,0:T(8,128)(2,1)S(1)}, bf16[128,2048]{1,0:T(8,128)(2,1)}, u32[]{:S(2)}, u32[]{:S(2)}) collective-permute-start(bf16[128,2048]{1,0:T(8,128)(2,1)S(1)} %get-tuple-element.207), channel_id=1, source_target_pairs={{8,0},{16,8},{24,16},{28,24},{20,28},{12,20},{4,12},{0,4},{9,1},{1... | collective-permute-start | bytes 1572872 | tf_op jit(solution)/shard_map/ppermute | solution.py:45
  266.2 27.4 %collective-permute-start.38 = (bf16[256,2048]{1,0:T(8,128)(2,1)S(1)}, bf16[256,2048]{1,0:T(8,128)(2,1)S(1)}, u32[]{:S(2)}, u32[]{:S(2)}) collective-permute-start(bf16[256,2048]{1,0:T(8,128)(2,1)S(1)} %fusion.6), channel_id=1, source_target_pairs={{0,2},{1,3},{2,0},{3,1},{4,6},{5,7},{6,4},{7,5},{8,10},{9,11},{10,... | collective-permute-start | bytes 3145736 | tf_op jit(solution)/shard_map/ppermute | solution.py:210
  293.6 37.7 %collective-permute-start.41 = (bf16[128,2048]{1,0:T(8,128)(2,1)}, bf16[128,2048]{1,0:T(8,128)(2,1)S(1)}, u32[]{:S(2)}, u32[]{:S(2)}) collective-permute-start(bf16[128,2048]{1,0:T(8,128)(2,1)} %get-tuple-element.231), channel_id=1, source_target_pairs={{0,8},{8,16},{16,24},{24,28},{28,20},{20,12},{12,4},{4,0},{1,9},{9... | collective-permute-start | bytes 1572872 | tf_op jit(solution)/shard_map/ppermute | solution.py:45
  294.4 36.9 %collective-permute-start.42 = (bf16[128,2048]{1,0:T(8,128)(2,1)S(1)}, bf16[128,2048]{1,0:T(8,128)(2,1)S(1)}, u32[]{:S(2)}, u32[]{:S(2)}) collective-permute-start(bf16[128,2048]{1,0:T(8,128)(2,1)S(1)} %get-tuple-element.232), channel_id=1, source_target_pairs={{8,0},{16,8},{24,16},{28,24},{20,28},{12,20},{4,12},{0,4},{9,1},{1... | collective-permute-start | bytes 1572872 | tf_op jit(solution)/shard_map/ppermute | solution.py:45
  304.7 24.6 %collective-permute-start.39 = (bf16[1024,256]{1,0:T(8,128)(2,1)}, bf16[1024,256]{1,0:T(8,128)(2,1)}, u32[]{:S(2)}, u32[]{:S(2)}) collective-permute-start(bf16[1024,256]{1,0:T(8,128)(2,1)} %get-tuple-element.220), channel_id=1, source_target_pairs={{0,8},{8,16},{16,24},{24,28},{28,20},{20,12},{12,4},{4,0},{1,9},{9... | collective-permute-start | bytes 1572872 | tf_op jit(solution)/shard_map/ppermute | solution.py:45
  305.5 23.8 %collective-permute-start.40 = (bf16[1024,256]{1,0:T(8,128)(2,1)S(1)}, bf16[1024,256]{1,0:T(8,128)(2,1)}, u32[]{:S(2)}, u32[]{:S(2)}) collective-permute-start(bf16[1024,256]{1,0:T(8,128)(2,1)S(1)} %get-tuple-element.221), channel_id=1, source_target_pairs={{8,0},{16,8},{24,16},{28,24},{20,28},{12,20},{4,12},{0,4},{9,1},{1... | collective-permute-start | bytes 1572872 | tf_op jit(solution)/shard_map/ppermute | solution.py:45
  340.2 25.0 %collective-permute-start.48 = (bf16[1024,256]{1,0:T(8,128)(2,1)S(1)}, bf16[1024,256]{1,0:T(8,128)(2,1)S(1)}, u32[]{:S(2)}, u32[]{:S(2)}) collective-permute-start(bf16[1024,256]{1,0:T(8,128)(2,1)S(1)} %get-tuple-element.240), channel_id=1, source_target_pairs={{0,8},{8,16},{16,24},{24,28},{28,20},{20,12},{12,4},{4,0},{1,9},{9... | collective-permute-start | bytes 1572872 | tf_op jit(solution)/shard_map/ppermute | solution.py:45
  340.5 24.8 %collective-permute-start.49 = (bf16[1024,256]{1,0:T(8,128)(2,1)S(1)}, bf16[1024,256]{1,0:T(8,128)(2,1)S(1)}, u32[]{:S(2)}, u32[]{:S(2)}) collective-permute-start(bf16[1024,256]{1,0:T(8,128)(2,1)S(1)} %get-tuple-element.241), channel_id=1, source_target_pairs={{8,0},{16,8},{24,16},{28,24},{20,28},{12,20},{4,12},{0,4},{9,1},{1... | collective-permute-start | bytes 1572872 | tf_op jit(solution)/shard_map/ppermute | solution.py:45
  344.9 23.8 %collective-permute-start.46 = (bf16[256,2048]{1,0:T(8,128)(2,1)S(1)}, bf16[256,2048]{1,0:T(8,128)(2,1)S(1)}, u32[]{:S(2)}, u32[]{:S(2)}) collective-permute-start(bf16[256,2048]{1,0:T(8,128)(2,1)S(1)} %fusion.7), channel_id=1, source_target_pairs={{0,2},{1,3},{2,0},{3,1},{4,6},{5,7},{6,4},{7,5},{8,10},{9,11},{10,... | collective-permute-start | bytes 3145736 | tf_op jit(solution)/shard_map/ppermute | solution.py:210
  371.3 25.3 %collective-permute-start.58 = (bf16[128,2048]{1,0:T(8,128)(2,1)}, bf16[128,2048]{1,0:T(8,128)(2,1)S(1)}, u32[]{:S(2)}, u32[]{:S(2)}) collective-permute-start(bf16[128,2048]{1,0:T(8,128)(2,1)} %add_convert_fusion.6.o0), channel_id=1, source_target_pairs={{0,1},{1,0},{2,3},{3,2},{4,5},{5,4},{6,7},{7,6},{8,9},{9,8},{10,11... | collective-permute-start | bytes 1572872 | tf_op jit(solution)/shard_map/ppermute | solution.py:158
  (105 other events, 1430.4 us)
Sparse Core Ops, SparseCore 0:
  9.6 36.9 all-gather.6
  48.1 34.4 all-gather.4

commit v5 on v4

--- a/solution.py
+++ b/solution.py
@@ -880,7 +880,7 @@
 
 def run_gate_back(sums, scaled, z, y, x, gain):
     length, width = y.shape
-    tile = PAIR
+    tile = 2 * PAIR
     col = pl.BlockSpec((length, tile), lambda i: (0, i))
     low = jax.ShapeDtypeStruct(y.shape, BF16)
     return pl.pallas_call(
@@ -896,7 +896,7 @@
         ],
         out_specs=[col, col, col, pl.BlockSpec((8, tile), lambda i: (0, i))],
         out_shape=[low, low, low, jax.ShapeDtypeStruct((8, width), F32)],
-        scratch_shapes=[pltpu.VMEM((2, length, PAIR), F32)],
+        scratch_shapes=[pltpu.VMEM((2, length, 2 * PAIR), F32)],
         compiler_params=pltpu.CompilerParams(vmem_limit_bytes=VMEM_LIMIT),
         cost_estimate=busy(11, 20),
         name="gate_back",

time: 473 us -> 472 us (level)
  no operation moved by 1% of the time
where the time goes in v5:
time: 472 us; the launch traced here: 464 us
  Pallas kernels  150 us (32%)
  waiting for transfers between devices  115 us (24%)
  starting transfers between devices  79.8 us (17%)
  other arithmetic  39.1 us (8%)
  local copies, waits for them, and re-layouts  33.7 us (7%)
  matrix products  25.8 us (5%)
  between operations  20.7 us (4%)
    ppermute x48, waiting for transfers between devices, send(): return lax.ppermute(block, 'fsdp', route)  98.6 us
    pallas_call x2, Pallas kernels, run_mix_backward(): pl.pallas_call(lambda *refs: mix_backward(top, follows, *refs), grid=(spa...  40.7 us
    ppermute x48, starting transfers between devices, send(): return lax.ppermute(block, 'fsdp', route)  37.1 us
    dot_general x3, matrix products, tn(): lax.dot_general(a, b, (((0,), (0,)), ((), ())), preferred_element_type=F32)  21.1 us
    pallas_call x1, Pallas kernels, run_back_norm(): pl.pallas_call(back_norm, grid_spec=pltpu.PrefetchScalarGridSpec(num_scal...  19.4 us
    pallas_call x1, Pallas kernels, run_mix_forward(): pl.pallas_call(mix_forward, grid=(blocks,), in_specs=[pl.BlockSpec((GROUP...  19.1 us
    pallas_call x1, Pallas kernels, run_gate_sums(): pl.pallas_call(gate_sums, grid_spec=pltpu.PrefetchScalarGridSpec(num_scal...  14.6 us
    convert_element_type x6, other arithmetic, join(): self.right, self.left = (right.astype(BF16), left.astype(BF16))  14 us
  transfers between devices with their start and end apart: 75, of which 27 were waited for; matrix products, arithmetic and copies ran while one was open for 14% of the time, Pallas kernels for 26%

profile of v5, /device:TPU:1, one launch (start us, length us, event | category | flops | bytes accessed | tf_op | source)
XLA Modules:
  0.0 464.5 jit_solution(5172142990664844701)
XLA Ops:
  16.4 15.4 %collective-permute-done.refs_8_.refs_7_.refs_17_ = bf16[1344,256]{1,0:T(8,128)(2,1)S(1)} collective-permute-done((bf16[1344,256]{1,0:T(8,128)(2,1)}, bf16[1344,256]{1,0:T(8,128)(2,1)S(1)}, u32[]{:S(2)}, u32[]{:S(2)}) %collective-permute-start) | collective-permute-done | bytes 688160 | tf_op jit(solution)/shard_map/ppermute | solution.py:45
  34.1 13.8 %collective-permute-done.2.refs_7_.refs_6_.refs_16_ = bf16[1344,256]{1,0:T(8,128)(2,1)} collective-permute-done((bf16[1344,256]{1,0:T(8,128)(2,1)S(1)}, bf16[1344,256]{1,0:T(8,128)(2,1)}, u32[]{:S(2)}, u32[]{:S(2)}) %collective-permute-start.2) | collective-permute-done | bytes 688160 | tf_op jit(solution)/shard_map/ppermute | solution.py:45
  53.5 10.7 %collective-permute-done.7.refs_6_.refs_5_.refs_15_ = bf16[1344,256]{1,0:T(8,128)(2,1)S(1)} collective-permute-done((bf16[1344,256]{1,0:T(8,128)(2,1)}, bf16[1344,256]{1,0:T(8,128)(2,1)S(1)}, u32[]{:S(2)}, u32[]{:S(2)}) %collective-permute-start.7) | collective-permute-done | bytes 688160 | tf_op jit(solution)/shard_map/ppermute | solution.py:45
  66.0 9.4 %collective-permute-done.4.refs_8_ = bf16[1024,256]{1,0:T(8,128)(2,1)} collective-permute-done((bf16[1024,256]{1,0:T(8,128)(2,1)}, bf16[1024,256]{1,0:T(8,128)(2,1)}, u32[]{:S(2)}, u32[]{:S(2)}) %collective-permute-start.4) | collective-permute-done | bytes 524320 | tf_op jit(solution)/shard_map/ppermute | solution.py:45
  79.3 4.6 collective-permute-done.9.refs_5_.refs_4_.refs_14_
  91.4 12.7 %front.1 = (bf16[1024,2048]{1,0:T(8,128)(2,1)}, bf16[1024,1344]{1,0:T(8,128)(2,1)}) custom-call(s32[8]{0:T(128)} %compare_select_fusion.2.members_ref, bf16[1024,2048]{1,0:T(8,128)(2,1)} %bitcast.121, bf16[1344,256]{1,0:T(8,128)(2,1)} %get-tuple-element.164.refs_0_.refs_9_, bf16[1344,256]{1,0:T(8,128)(2,1)} %copy-done.15, bf16[1344,256]{1,0:T(8,128)(2,1)} %copy-done.16, ...), custom_call_target="tpu_custom_call" | custom-call | flops 12000000000 | bytes 18000000 | tf_op jit(solution)/shard_map/front/pallas_call | solution.py:406
  112.7 19.1 %mix_forward.1 = (bf16[1024,1280]{1,0:T(8,128)(2,1)}, f32[4,128,128]{2,1,0:T(8,128)}, f32[1024,1024]{1,0:T(8,128)}, f32[4,8,128,128]{3,2,1,0:T(8,128)}) custom-call(bf16[1024,1344]{1,0:T(8,128)(2,1)} %get-tuple-element.162.proj_ref.refs_1_.refs_2_, f32[8,1280]{1,0:T(8,128)} %pad.14.taps_ref.refs_3_, f32[32,128]{1,0:T(8,128)} %broadcast_in_dim.38.heads_ref.refs_4_, ...), custom_call_target="tpu_custom_call" | custom-call | flops 17999998976 | bytes 15000000 | tf_op jit(solution)/shard_map/mix_forward/pallas_call | solution.py:558
  136.4 5.2 %collective-permute-done.18.refs_6_ = bf16[128,2048]{1,0:T(8,128)(2,1)S(1)} collective-permute-done((bf16[128,2048]{1,0:T(8,128)(2,1)}, bf16[128,2048]{1,0:T(8,128)(2,1)S(1)}, u32[]{:S(2)}, u32[]{:S(2)}) %collective-permute-start.18) | collective-permute-done | bytes 524320 | tf_op jit(solution)/shard_map/ppermute | solution.py:45
  147.3 8.6 %project.1.z_ref = bf16[1024,1024]{1,0:T(8,128)(2,1)} custom-call(bf16[1024,2048]{1,0:T(8,128)(2,1)} %get-tuple-element.217.normed_ref, bf16[1024,256]{1,0:T(8,128)(2,1)} %get-tuple-element.146.refs_0_, bf16[1024,256]{1,0:T(8,128)(2,1)} %collective-permute-done.5.refs_1_, bf16[1024,256]{1,0:T(8,128)(2,1)} %copy-done.38, bf16[1024,256]{1,0:T(8,128)(2,1)} %copy-done.26, ...), custom_call_target="tpu_custom_call" | custom-call | flops 8000000000 | bytes 10000000 | tf_op jit(solution)/shard_map/project/pallas_call | solution.py:437
  156.8 14.6 %gate_sums.1 = (bf16[1024,2048]{1,0:T(8,128)(2,1)}, f32[1024,1024]{1,0:T(8,128)}, f32[8,1024]{1,0:T(8,128)}) custom-call(s32[8]{0:T(128)} %compare_select_fusion.2.members_ref, bf16[1024,2048]{1,0:T(8,128)(2,1)} %bitcast.123, bf16[1024,1024]{1,0:T(8,128)(2,1)} %project.1.z_ref, f32[1024,1024]{1,0:T(8,128)} %get-tuple-element.175.y_ref, ...), custom_call_target="tpu_custom_call" | custom-call | flops 11000000512 | bytes 20000000 | tf_op jit(solution)/shard_map/gate_sums/pallas_call | solution.py:830
  171.4 11.9 %collective-permute-start.24 = (f32[8,1024]{1,0:T(8,128)}, f32[8,1024]{1,0:T(8,128)S(1)}, u32[]{:S(2)}, u32[]{:S(2)}) collective-permute-start(f32[8,1024]{1,0:T(8,128)} %get-tuple-element.184), channel_id=1, source_target_pairs={{0,1},{1,0},{2,3},{3,2},{4,5},{5,4},{6,7},{7,6},{8,9},{9,8},{10,11... | collective-permute-start | bytes 98312 | tf_op jit(solution)/shard_map/ppermute | solution.py:226
  193.2 9.7 %gate_back.1 = (bf16[1024,1024]{1,0:T(8,128)(2,1)}, bf16[1024,1024]{1,0:T(8,128)(2,1)}, bf16[1024,1024]{1,0:T(8,128)(2,1)}, f32[8,1024]{1,0:T(8,128)}) custom-call(f32[8,1024]{1,0:T(8,128)} %add_add_fusion.sums_ref, f32[1024,1024]{1,0:T(8,128)} %get-tuple-element.185.scaled_ref, bf16[1024,1024]{1,0:T(8,128)(2,1)} %project.1.z_ref, ...), custom_call_target="tpu_custom_call" | custom-call | flops 11000000512 | bytes 20000000 | tf_op jit(solution)/shard_map/gate_back/pallas_call | solution.py:886
  202.9 6.6 %convolution_convert_fusion.3 = bf16[1024,2048]{1,0:T(8,128)(2,1)S(1)} fusion(bf16[1024,1024]{1,0:T(8,128)(2,1)} %get-tuple-element.193, bf16[1,1024,2048]{2,1,0:T(8,128)(2,1)S(1)} %copy-done.35), kind=kOutput, calls=%fused_computation.5 | convolution fusion | flops 4297064448 | bytes 10485760 | tf_op jit(solution)/shard_map/dot_general | solution.py:239
  212.6 4.9 %convolution_convert_fusion.2 = bf16[1024,2048]{1,0:T(8,128)(2,1)S(1)} fusion(bf16[1024,1024]{1,0:T(8,128)(2,1)S(1)} %copy-done.51, bf16[1024,2048]{1,0:T(8,128)(2,1)S(1)} %copy-done.49), kind=kOutput, calls=%fused_computation.4 | convolution fusion | flops 4297064448 | bytes 10485760 | tf_op jit(solution)/shard_map/dot_general | solution.py:239
  219.1 4.7 %convolution_convert_fusion.1 = bf16[1024,2048]{1,0:T(8,128)(2,1)S(1)} fusion(bf16[1024,1024]{1,0:T(8,128)(2,1)S(1)} %copy-done.52, bf16[1024,2048]{1,0:T(8,128)(2,1)S(1)} %copy-done.53), kind=kOutput, calls=%fused_computation.3 | convolution fusion | flops 4297064448 | bytes 10485760 | tf_op jit(solution)/shard_map/dot_general | solution.py:235
  230.9 20.4 %mix_backward.2 = (bf16[1024,1344]{1,0:T(8,128)(2,1)}, f32[8,1280]{1,0:T(8,128)}, f32[32,256]{1,0:T(8,128)}, f32[8,128,128]{2,1,0:T(8,128)}, f32[8,1280]{1,0:T(8,128)}) custom-call(bf16[1024,1280]{1,0:T(8,128)(2,1)} %get-tuple-element.186.x_ref.refs_0_, bf16[1024,1344]{1,0:T(8,128)(2,1)} %get-tuple-element.162.proj_ref.refs_1_.refs_2_, ...), custom_call_target="tpu_custom_call" | custom-call | flops 24000000000 | bytes 10000000 | tf_op jit(solution)/shard_map/mix_backward/pallas_call | solution.py:740
  266.2 20.3 %mix_backward.3 = (bf16[1024,1344]{1,0:T(8,128)(2,1)}, f32[8,1280]{1,0:T(8,128)}, f32[32,256]{1,0:T(8,128)}, f32[8,128,128]{2,1,0:T(8,128)}, f32[8,1280]{1,0:T(8,128)}) custom-call(bf16[1024,1280]{1,0:T(8,128)(2,1)} %get-tuple-element.186.x_ref.refs_0_, ...), custom_call_target="tpu_custom_call", output_to_operand_aliasing={{0}: (11, {})} | custom-call | flops 24000000000 | bytes 10000000 | tf_op jit(solution)/shard_map/mix_backward/pallas_call | solution.py:740
  293.8 9.6 %convolution_convert_fusion.grads_ref = bf16[1344,2048]{1,0:T(8,128)(2,1)} fusion(bf16[1024,1344]{1,0:T(8,128)(2,1)} %get-tuple-element.222.dx_ref, bf16[1024,2048]{1,0:T(8,128)(2,1)S(1)} %copy-done.50), kind=kOutput, calls=%fused_computation | convolution fusion | flops 5639897088 | bytes 12451840 | tf_op jit(solution)/shard_map/dot_general | solution.py:239
  305.1 19.4 %back_norm.1 = (bf16[2,256,2048]{2,1,0:T(8,128)(2,1)}, bf16[2,256,2048]{2,1,0:T(8,128)(2,1)}, f32[8,2048]{1,0:T(8,128)}) custom-call(s32[8]{0:T(128)} %compare_select_fusion.2.members_ref, s32[1]{0:T(128)} %bitcast.2.place_ref, bf16[1024,2048]{1,0:T(8,128)(2,1)} %bitcast.122, bf16[1024,1024]{1,0:T(8,128)(2,1)} %get-tuple-element.191.dz_ref, ...), custom_call_target="tpu_custom_call" | custom-call | flops 17999998976 | bytes 24000000 | tf_op jit(solution)/shard_map/back_norm/pallas_call | solution.py:946
  344.0 16.0 %collective-permute-done.44 = bf16[544,256]{1,0:T(8,128)(2,1)S(1)} collective-permute-done((bf16[544,256]{1,0:T(8,128)(2,1)S(1)}, bf16[544,256]{1,0:T(8,128)(2,1)S(1)}, u32[]{:S(2)}, u32[]{:S(2)}) %collective-permute-start.44) | collective-permute-done | bytes 278560 | tf_op jit(solution)/shard_map/ppermute | solution.py:45
  375.8 8.5 %collective-permute-done.52 = f32[80,256]{1,0:T(8,128)S(1)} collective-permute-done((f32[80,256]{1,0:T(8,128)S(1)}, f32[80,256]{1,0:T(8,128)S(1)}, u32[]{:S(2)}, u32[]{:S(2)}) %collective-permute-start.52) | collective-permute-done | bytes 81952 | tf_op jit(solution)/shard_map/ppermute | solution.py:1273
  400.9 6.8 %collective-permute-done.54 = bf16[1312,256]{1,0:T(8,128)(2,1)S(1)} collective-permute-done((bf16[1312,256]{1,0:T(8,128)(2,1)S(1)}, bf16[1312,256]{1,0:T(8,128)(2,1)S(1)}, u32[]{:S(2)}, u32[]{:S(2)}) %collective-permute-start.54) | collective-permute-done | bytes 671776 | tf_op jit(solution)/shard_map/ppermute | solution.py:45
  418.3 5.1 %assemble_z.1.held_ref = f32[8512,256]{1,0:T(8,128)} custom-call(s32[1]{0:T(128)} %bitcast.2.place_ref, bf16[1024,256]{1,0:T(8,128)(2,1)} %add_convert_fusion.5.z0, bf16[1024,256]{1,0:T(8,128)(2,1)} %collective-permute-done.65.z1, bf16[1024,256]{1,0:T(8,128)(2,1)} %collective-permute-done.57.z2, bf16[1024,256]{1,0:T(8,128)(2,1)} %collective-permute-done.66.z3), custom_call_target="tpu_custom_call" | custom-call | flops 4000000000 | bytes 6000000 | tf_op jit(solution)/shard_map/assemble_z/pallas_call | solution.py:1031
  435.7 4.5 collective-permute-start.69
  (388 shorter events, 181.3 us)
Async XLA Ops:
  7.2 76.8 %all-gather.7.cloned.1.call-start = ((), (), s32[]{:S(2)}) async-start(), calls=%async_computation.1 | async-start | bytes 5242880 | tf_op jit(solution)/shard_map/all_gather | solution.py:1114
  7.9 148.1 %all-gather.5.cloned.1.call-start = ((), (), s32[]{:S(2)}) async-start(), calls=%async_computation | async-start | bytes 5242880 | tf_op jit(solution)/shard_map/all_gather | solution.py:1115
  51.3 24.2 %collective-permute-start.4 = (bf16[1024,256]{1,0:T(8,128)(2,1)}, bf16[1024,256]{1,0:T(8,128)(2,1)}, u32[]{:S(2)}, u32[]{:S(2)}) collective-permute-start(bf16[1024,256]{1,0:T(8,128)(2,1)} %get-tuple-element.146.refs_0_), channel_id=1, source_target_pairs={{0,8},{8,16},{16,24},{24,28},{28,20},{20,12},{12,4},{4,0},{1,9},{9... | collective-permute-start | bytes 1572872 | tf_op jit(solution)/shard_map/ppermute | solution.py:45
  52.6 23.9 %collective-permute-start.5 = (bf16[1024,256]{1,0:T(8,128)(2,1)}, bf16[1024,256]{1,0:T(8,128)(2,1)}, u32[]{:S(2)}, u32[]{:S(2)}) collective-permute-start(bf16[1024,256]{1,0:T(8,128)(2,1)} %get-tuple-element.146.refs_0_), channel_id=1, source_target_pairs={{8,0},{16,8},{24,16},{28,24},{20,28},{12,20},{4,12},{0,4},{9,1},{1... | collective-permute-start | bytes 1572872 | tf_op jit(solution)/shard_map/ppermute | solution.py:45
  109.1 22.7 %collective-permute-start.14 = (bf16[1024,256]{1,0:T(8,128)(2,1)S(1)}, bf16[1024,256]{1,0:T(8,128)(2,1)S(1)}, u32[]{:S(2)}, u32[]{:S(2)}) collective-permute-start(bf16[1024,256]{1,0:T(8,128)(2,1)S(1)} %collective-permute-done.10.refs_7_), channel_id=1, source_target_pairs={{0,8},{8,16},{16,24},{24,28},{28,20},{20,12},{12,4},{4,0},{1,9},{9... | collective-permute-start | bytes 1572872 | tf_op jit(solution)/shard_map/ppermute | solution.py:45
  110.2 21.7 %collective-permute-start.15 = (bf16[1024,256]{1,0:T(8,128)(2,1)S(1)}, bf16[1024,256]{1,0:T(8,128)(2,1)S(1)}, u32[]{:S(2)}, u32[]{:S(2)}) collective-permute-start(bf16[1024,256]{1,0:T(8,128)(2,1)S(1)} %collective-permute-done.11.refs_2_), channel_id=1, source_target_pairs={{8,0},{16,8},{24,16},{28,24},{20,28},{12,20},{4,12},{0,4},{9,1},{1... | collective-permute-start | bytes 1572872 | tf_op jit(solution)/shard_map/ppermute | solution.py:45
  226.4 31.0 %collective-permute-start.29 = (bf16[2,256,2048]{2,1,0:T(8,128)(2,1)S(1)}, bf16[2,256,2048]{2,1,0:T(8,128)(2,1)}, u32[]{:S(2)}, u32[]{:S(2)}) collective-permute-start(bf16[2,256,2048]{2,1,0:T(8,128)(2,1)S(1)} %dynamic-slice_bitcast_fusion), channel_id=1, source_target_pairs={{0,1},{1,0},{2,3},{3,2},{4,5},{5,4},{6,7},{7,6},{8,9},{9,8},{10,11... | collective-permute-start | bytes 6291464 | tf_op jit(solution)/shard_map/ppermute | solution.py:203
  227.8 23.6 %collective-permute-start.32 = (bf16[512,256]{1,0:T(8,128)(2,1)}, bf16[512,256]{1,0:T(8,128)(2,1)S(1)}, u32[]{:S(2)}, u32[]{:S(2)}) collective-permute-start(bf16[512,256]{1,0:T(8,128)(2,1)} %get-tuple-element.198), channel_id=1, source_target_pairs={{0,8},{8,16},{16,24},{24,28},{28,20},{20,12},{12,4},{4,0},{1,9},{9... | collective-permute-start | bytes 786440 | tf_op jit(solution)/shard_map/ppermute | solution.py:45
  228.7 22.7 %collective-permute-start.33 = (bf16[512,256]{1,0:T(8,128)(2,1)}, bf16[512,256]{1,0:T(8,128)(2,1)}, u32[]{:S(2)}, u32[]{:S(2)}) collective-permute-start(bf16[512,256]{1,0:T(8,128)(2,1)} %get-tuple-element.199), channel_id=1, source_target_pairs={{8,0},{16,8},{24,16},{28,24},{20,28},{12,20},{4,12},{0,4},{9,1},{1... | collective-permute-start | bytes 786440 | tf_op jit(solution)/shard_map/ppermute | solution.py:45
  229.4 24.7 %collective-permute-start.30 = (bf16[128,2048]{1,0:T(8,128)(2,1)S(1)}, bf16[128,2048]{1,0:T(8,128)(2,1)}, u32[]{:S(2)}, u32[]{:S(2)}) collective-permute-start(bf16[128,2048]{1,0:T(8,128)(2,1)S(1)} %pad_maximum_fusion.2), channel_id=1, source_target_pairs={{0,8},{8,16},{16,24},{24,28},{28,20},{20,12},{12,4},{4,0},{1,9},{9... | collective-permute-start | bytes 1572872 | tf_op jit(solution)/shard_map/ppermute | solution.py:45
  230.3 23.8 %collective-permute-start.31 = (bf16[128,2048]{1,0:T(8,128)(2,1)S(1)}, bf16[128,2048]{1,0:T(8,128)(2,1)}, u32[]{:S(2)}, u32[]{:S(2)}) collective-permute-start(bf16[128,2048]{1,0:T(8,128)(2,1)S(1)} %pad_maximum_fusion.3), channel_id=1, source_target_pairs={{8,0},{16,8},{24,16},{28,24},{20,28},{12,20},{4,12},{0,4},{9,1},{1... | collective-permute-start | bytes 1572872 | tf_op jit(solution)/shard_map/ppermute | solution.py:45
  261.9 24.5 %collective-permute-start.36 = (bf16[1024,256]{1,0:T(8,128)(2,1)}, bf16[1024,256]{1,0:T(8,128)(2,1)S(1)}, u32[]{:S(2)}, u32[]{:S(2)}) collective-permute-start(bf16[1024,256]{1,0:T(8,128)(2,1)} %pad_maximum_fusion.4), channel_id=1, source_target_pairs={{0,8},{8,16},{16,24},{24,28},{28,20},{20,12},{12,4},{4,0},{1,9},{9... | collective-permute-start | bytes 1572872 | tf_op jit(solution)/shard_map/ppermute | solution.py:45
  262.9 24.4 %collective-permute-start.37 = (bf16[1024,256]{1,0:T(8,128)(2,1)}, bf16[1024,256]{1,0:T(8,128)(2,1)}, u32[]{:S(2)}, u32[]{:S(2)}) collective-permute-start(bf16[1024,256]{1,0:T(8,128)(2,1)} %pad_maximum_fusion.5), channel_id=1, source_target_pairs={{8,0},{16,8},{24,16},{28,24},{20,28},{12,20},{4,12},{0,4},{9,1},{1... | collective-permute-start | bytes 1572872 | tf_op jit(solution)/shard_map/ppermute | solution.py:45
  263.5 26.3 %collective-permute-start.34 = (bf16[128,2048]{1,0:T(8,128)(2,1)}, bf16[128,2048]{1,0:T(8,128)(2,1)S(1)}, u32[]{:S(2)}, u32[]{:S(2)}) collective-permute-start(bf16[128,2048]{1,0:T(8,128)(2,1)} %get-tuple-element.206), channel_id=1, source_target_pairs={{0,8},{8,16},{16,24},{24,28},{28,20},{20,12},{12,4},{4,0},{1,9},{9... | collective-permute-start | bytes 1572872 | tf_op jit(solution)/shard_map/ppermute | solution.py:45
  264.3 25.4 %collective-permute-start.35 = (bf16[128,2048]{1,0:T(8,128)(2,1)S(1)}, bf16[128,2048]{1,0:T(8,128)(2,1)}, u32[]{:S(2)}, u32[]{:S(2)}) collective-permute-start(bf16[128,2048]{1,0:T(8,128)(2,1)S(1)} %get-tuple-element.207), channel_id=1, source_target_pairs={{8,0},{16,8},{24,16},{28,24},{20,28},{12,20},{4,12},{0,4},{9,1},{1... | collective-permute-start | bytes 1572872 | tf_op jit(solution)/shard_map/ppermute | solution.py:45
  264.9 27.4 %collective-permute-start.38 = (bf16[256,2048]{1,0:T(8,128)(2,1)S(1)}, bf16[256,2048]{1,0:T(8,128)(2,1)S(1)}, u32[]{:S(2)}, u32[]{:S(2)}) collective-permute-start(bf16[256,2048]{1,0:T(8,128)(2,1)S(1)} %fusion.6), channel_id=1, source_target_pairs={{0,2},{1,3},{2,0},{3,1},{4,6},{5,7},{6,4},{7,5},{8,10},{9,11},{10,... | collective-permute-start | bytes 3145736 | tf_op jit(solution)/shard_map/ppermute | solution.py:210
  292.3 37.7 %collective-permute-start.41 = (bf16[128,2048]{1,0:T(8,128)(2,1)}, bf16[128,2048]{1,0:T(8,128)(2,1)S(1)}, u32[]{:S(2)}, u32[]{:S(2)}) collective-permute-start(bf16[128,2048]{1,0:T(8,128)(2,1)} %get-tuple-element.231), channel_id=1, source_target_pairs={{0,8},{8,16},{16,24},{24,28},{28,20},{20,12},{12,4},{4,0},{1,9},{9... | collective-permute-start | bytes 1572872 | tf_op jit(solution)/shard_map/ppermute | solution.py:45
  293.2 36.9 %collective-permute-start.42 = (bf16[128,2048]{1,0:T(8,128)(2,1)S(1)}, bf16[128,2048]{1,0:T(8,128)(2,1)S(1)}, u32[]{:S(2)}, u32[]{:S(2)}) collective-permute-start(bf16[128,2048]{1,0:T(8,128)(2,1)S(1)} %get-tuple-element.232), channel_id=1, source_target_pairs={{8,0},{16,8},{24,16},{28,24},{20,28},{12,20},{4,12},{0,4},{9,1},{1... | collective-permute-start | bytes 1572872 | tf_op jit(solution)/shard_map/ppermute | solution.py:45
  303.4 24.6 %collective-permute-start.39 = (bf16[1024,256]{1,0:T(8,128)(2,1)}, bf16[1024,256]{1,0:T(8,128)(2,1)}, u32[]{:S(2)}, u32[]{:S(2)}) collective-permute-start(bf16[1024,256]{1,0:T(8,128)(2,1)} %get-tuple-element.220), channel_id=1, source_target_pairs={{0,8},{8,16},{16,24},{24,28},{28,20},{20,12},{12,4},{4,0},{1,9},{9... | collective-permute-start | bytes 1572872 | tf_op jit(solution)/shard_map/ppermute | solution.py:45
  304.3 23.8 %collective-permute-start.40 = (bf16[1024,256]{1,0:T(8,128)(2,1)S(1)}, bf16[1024,256]{1,0:T(8,128)(2,1)}, u32[]{:S(2)}, u32[]{:S(2)}) collective-permute-start(bf16[1024,256]{1,0:T(8,128)(2,1)S(1)} %get-tuple-element.221), channel_id=1, source_target_pairs={{8,0},{16,8},{24,16},{28,24},{20,28},{12,20},{4,12},{0,4},{9,1},{1... | collective-permute-start | bytes 1572872 | tf_op jit(solution)/shard_map/ppermute | solution.py:45
  339.0 25.0 %collective-permute-start.48 = (bf16[1024,256]{1,0:T(8,128)(2,1)S(1)}, bf16[1024,256]{1,0:T(8,128)(2,1)S(1)}, u32[]{:S(2)}, u32[]{:S(2)}) collective-permute-start(bf16[1024,256]{1,0:T(8,128)(2,1)S(1)} %get-tuple-element.240), channel_id=1, source_target_pairs={{0,8},{8,16},{16,24},{24,28},{28,20},{20,12},{12,4},{4,0},{1,9},{9... | collective-permute-start | bytes 1572872 | tf_op jit(solution)/shard_map/ppermute | solution.py:45
  339.2 24.8 %collective-permute-start.49 = (bf16[1024,256]{1,0:T(8,128)(2,1)S(1)}, bf16[1024,256]{1,0:T(8,128)(2,1)S(1)}, u32[]{:S(2)}, u32[]{:S(2)}) collective-permute-start(bf16[1024,256]{1,0:T(8,128)(2,1)S(1)} %get-tuple-element.241), channel_id=1, source_target_pairs={{8,0},{16,8},{24,16},{28,24},{20,28},{12,20},{4,12},{0,4},{9,1},{1... | collective-permute-start | bytes 1572872 | tf_op jit(solution)/shard_map/ppermute | solution.py:45
  343.7 23.8 %collective-permute-start.46 = (bf16[256,2048]{1,0:T(8,128)(2,1)S(1)}, bf16[256,2048]{1,0:T(8,128)(2,1)S(1)}, u32[]{:S(2)}, u32[]{:S(2)}) collective-permute-start(bf16[256,2048]{1,0:T(8,128)(2,1)S(1)} %fusion.7), channel_id=1, source_target_pairs={{0,2},{1,3},{2,0},{3,1},{4,6},{5,7},{6,4},{7,5},{8,10},{9,11},{10,... | collective-permute-start | bytes 3145736 | tf_op jit(solution)/shard_map/ppermute | solution.py:210
  370.0 25.3 %collective-permute-start.58 = (bf16[128,2048]{1,0:T(8,128)(2,1)}, bf16[128,2048]{1,0:T(8,128)(2,1)S(1)}, u32[]{:S(2)}, u32[]{:S(2)}) collective-permute-start(bf16[128,2048]{1,0:T(8,128)(2,1)} %add_convert_fusion.6.o0), channel_id=1, source_target_pairs={{0,1},{1,0},{2,3},{3,2},{4,5},{5,4},{6,7},{7,6},{8,9},{9,8},{10,11... | collective-permute-start | bytes 1572872 | tf_op jit(solution)/shard_map/ppermute | solution.py:158
  (105 other events, 1429.1 us)
Sparse Core Ops, SparseCore 0:
  9.6 36.9 all-gather.6
  48.1 34.4 all-gather.4

commit v6 on v5

--- a/solution.py
+++ b/solution.py
@@ -1248,10 +1248,7 @@
         branch_own.middle()
         branch_own.send_far()
     grads_x = tn(d_x, normed_late).astype(BF16)
-    kept, given, d_gain = run_back_norm(
-        members, place_ref, all_tokens, d_z, after(d_x, grads_x), parts_z, parts_x
-    )
-    small = run_gather_small(conv_grads, head_grads, gate_cols, d_gain)
+    d_x_late = d_x
     if ring:
         used = core_cols + TAIL
         sum_x = Reduce(
@@ -1259,9 +1256,15 @@
         )
         part_o = sum_o.join().astype(BF16)
         sum_z.join()
-        kept, given, small, part_o, branch_own.far = next_hop(
-            [sum_x, sum_z], (kept, given, small, part_o, branch_own.far)
+        d_x_late, part_o, branch_own.far = next_hop(
+            [sum_x, sum_z], (d_x, part_o, branch_own.far)
         )
+        other_o = far_share(part_o, m)
+    kept, given, d_gain = run_back_norm(
+        members, place_ref, all_tokens, d_z, d_x_late, parts_z, parts_x
+    )
+    small = run_gather_small(conv_grads, head_grads, gate_cols, d_gain)
+
     flip = 1
     steps = []
     while flip < n:
@@ -1273,17 +1276,15 @@
             small = small + lax.ppermute(small, "fsdp", ctx_route(n, steps.pop()))
         return small
 
+    if ring:
+        sum_x.join()
+        part_z = sum_z.join().astype(BF16)
+        kept, given, small, part_o, other_o, part_z, branch_own.far = next_hop(
+            [sum_x], (kept, given, small, part_o, other_o, part_z, branch_own.far)
+        )
     d_own = CtxReduce(kept, given, m)
     d_own.middle()
     d_own.send_far()
-    small = small_step(small)
-    if ring:
-        sum_x.join()
-        part_z = sum_z.join().astype(BF16)
-        d_own.far, small, part_o, part_z, branch_own.far = next_hop(
-            [sum_x], (d_own.far, small, part_o, part_z, branch_own.far)
-        )
-        other_o = far_share(part_o, m)
     small = small_step(small)
     output = (tokens[0].astype(F32) + branch_own.total()).astype(BF16)[None]
     if ring:
@@ -1306,14 +1307,16 @@
                 [sum_x], (small, part_z, other_z), grad_tokens, grad_w_out
             )
         shares_z = near_share(part_z, other_z, m)
-        held = run_assemble_z(place_ref, shares_z, w_in.shape[1])
     while steps:
         small = small_step(small)
-    smalls_of = ctx_share(small, m)
+    if not ring:
+        smalls_of = ctx_share(small, m)
     if ring:
         part_x = sum_x.join().astype(BF16)
         part_a, part_b = part_x[:cut], part_x[cut:]
-        part_a, part_b, smalls_of = barrier((part_a, part_b, smalls_of))
+        part_a, part_b, small, shares_z = barrier((part_a, part_b, small, shares_z))
+        smalls_of = ctx_share(small, m)
+        held = run_assemble_z(place_ref, shares_z, w_in.shape[1])
     by_place = jnp.zeros((m,) + small.shape, F32)
     for k in range(m):
         by_place = lax.dynamic_update_slice(by_place, smalls_of[k][None], (place ^ k, 0, 0))

time: 472 us -> 472 us (level)
  waiting for transfers between devices: 115 us -> 121 us
    ppermute x2, waiting for transfers between devices: 1.4 us -> 9.14 us  [send_far(): self.far = lax.ppermute(self.sent, 'ctx', ctx_route(self.m, 2))]
    ppermute x5, starting transfers between devices: 9.86 us -> 2.63 us  [near_share(): far = lax.ppermute(other, 'ctx', ctx_route(m, 1))]
    ppermute x48, waiting for transfers between devices: 98.6 us -> 93.8 us  [send(): return lax.ppermute(block, 'fsdp', route)]
    unnamed x115 -> x113, local copies, waits for them, and re-layouts: 13.6 us -> 15.2 us
  transfers between devices with their start and end apart: 75 -> 75, of which waited for: 27 -> 27; matrix products, arithmetic and copies ran while one was open for 14% -> 13% of each run, Pallas kernels for 26% -> 26%
where the time goes in v6:
time: 472 us; the launch traced here: 465 us
  Pallas kernels  150 us (32%)
  waiting for transfers between devices  121 us (26%)
  starting transfers between devices  76.3 us (16%)
  other arithmetic  39.1 us (8%)
  local copies, waits for them, and re-layouts  33.3 us (7%)
  matrix products  24.2 us (5%)
  between operations  20.7 us (4%)
    ppermute x48, waiting for transfers between devices, send(): return lax.ppermute(block, 'fsdp', route)  93.8 us
    pallas_call x2, Pallas kernels, run_mix_backward(): pl.pallas_call(lambda *refs: mix_backward(top, follows, *refs), grid=(spa...  40.8 us
    ppermute x48, starting transfers between devices, send(): return lax.ppermute(block, 'fsdp', route)  38.2 us
    dot_general x3, matrix products, tn(): lax.dot_general(a, b, (((0,), (0,)), ((), ())), preferred_element_type=F32)  19.5 us
    pallas_call x1, Pallas kernels, run_back_norm(): pl.pallas_call(back_norm, grid_spec=pltpu.PrefetchScalarGridSpec(num_scal...  19.3 us
    pallas_call x1, Pallas kernels, run_mix_forward(): pl.pallas_call(mix_forward, grid=(blocks,), in_specs=[pl.BlockSpec((GROUP...  19.1 us
    unnamed x113, local copies, waits for them, and re-layouts  15.2 us
    ppermute x3, starting transfers between devices, ctx_sum(): lax.ppermute(values, 'ctx', ctx_route(m, flip))  14.8 us
  transfers between devices with their start and end apart: 75, of which 27 were waited for; matrix products, arithmetic and copies ran while one was open for 13% of the time, Pallas kernels for 26%

profile of v6, /device:TPU:1, one launch (start us, length us, event | category | flops | bytes accessed | tf_op | source)
XLA Modules:
  0.0 464.8 jit_solution(8778138142472918422)
XLA Ops:
  16.4 15.4 %collective-permute-done.refs_8_.refs_7_.refs_17_ = bf16[1344,256]{1,0:T(8,128)(2,1)S(1)} collective-permute-done((bf16[1344,256]{1,0:T(8,128)(2,1)}, bf16[1344,256]{1,0:T(8,128)(2,1)S(1)}, u32[]{:S(2)}, u32[]{:S(2)}) %collective-permute-start) | collective-permute-done | bytes 688160 | tf_op jit(solution)/shard_map/ppermute | solution.py:45
  34.2 13.7 %collective-permute-done.2.refs_7_.refs_6_.refs_16_ = bf16[1344,256]{1,0:T(8,128)(2,1)S(1)} collective-permute-done((bf16[1344,256]{1,0:T(8,128)(2,1)S(1)}, bf16[1344,256]{1,0:T(8,128)(2,1)S(1)}, u32[]{:S(2)}, u32[]{:S(2)}) %collective-permute-start.2) | collective-permute-done | bytes 688160 | tf_op jit(solution)/shard_map/ppermute | solution.py:45
  53.4 10.4 %collective-permute-done.7.refs_6_.refs_5_.refs_15_ = bf16[1344,256]{1,0:T(8,128)(2,1)S(1)} collective-permute-done((bf16[1344,256]{1,0:T(8,128)(2,1)S(1)}, bf16[1344,256]{1,0:T(8,128)(2,1)S(1)}, u32[]{:S(2)}, u32[]{:S(2)}) %collective-permute-start.7) | collective-permute-done | bytes 688160 | tf_op jit(solution)/shard_map/ppermute | solution.py:45
  65.8 9.2 %collective-permute-done.4.refs_8_ = bf16[1024,256]{1,0:T(8,128)(2,1)} collective-permute-done((bf16[1024,256]{1,0:T(8,128)(2,1)}, bf16[1024,256]{1,0:T(8,128)(2,1)}, u32[]{:S(2)}, u32[]{:S(2)}) %collective-permute-start.4) | collective-permute-done | bytes 524320 | tf_op jit(solution)/shard_map/ppermute | solution.py:45
  90.9 12.7 %front.1 = (bf16[1024,2048]{1,0:T(8,128)(2,1)}, bf16[1024,1344]{1,0:T(8,128)(2,1)}) custom-call(s32[8]{0:T(128)} %compare_select_fusion.2.members_ref, bf16[1024,2048]{1,0:T(8,128)(2,1)} %bitcast.121, bf16[1344,256]{1,0:T(8,128)(2,1)} %get-tuple-element.164.refs_0_.refs_9_, bf16[1344,256]{1,0:T(8,128)(2,1)} %copy-done.15, bf16[1344,256]{1,0:T(8,128)(2,1)} %copy-done.17, ...), custom_call_target="tpu_custom_call" | custom-call | flops 12000000000 | bytes 18000000 | tf_op jit(solution)/shard_map/front/pallas_call | solution.py:406
  112.6 19.1 %mix_forward.1 = (bf16[1024,1280]{1,0:T(8,128)(2,1)}, f32[4,128,128]{2,1,0:T(8,128)}, f32[1024,1024]{1,0:T(8,128)}, f32[4,8,128,128]{3,2,1,0:T(8,128)}) custom-call(bf16[1024,1344]{1,0:T(8,128)(2,1)} %get-tuple-element.162.proj_ref.refs_1_.refs_2_, f32[8,1280]{1,0:T(8,128)} %pad.14.taps_ref.refs_3_, f32[32,128]{1,0:T(8,128)} %broadcast_in_dim.38.heads_ref.refs_4_, ...), custom_call_target="tpu_custom_call" | custom-call | flops 17999998976 | bytes 15000000 | tf_op jit(solution)/shard_map/mix_forward/pallas_call | solution.py:558
  136.3 4.8 %collective-permute-done.18.refs_6_ = bf16[128,2048]{1,0:T(8,128)(2,1)S(1)} collective-permute-done((bf16[128,2048]{1,0:T(8,128)(2,1)}, bf16[128,2048]{1,0:T(8,128)(2,1)S(1)}, u32[]{:S(2)}, u32[]{:S(2)}) %collective-permute-start.18) | collective-permute-done | bytes 524320 | tf_op jit(solution)/shard_map/ppermute | solution.py:45
  146.8 8.6 %project.1.z_ref = bf16[1024,1024]{1,0:T(8,128)(2,1)} custom-call(bf16[1024,2048]{1,0:T(8,128)(2,1)} %get-tuple-element.217.normed_ref, bf16[1024,256]{1,0:T(8,128)(2,1)} %get-tuple-element.146.refs_0_, bf16[1024,256]{1,0:T(8,128)(2,1)} %collective-permute-done.5.refs_1_, bf16[1024,256]{1,0:T(8,128)(2,1)} %copy-done.37, bf16[1024,256]{1,0:T(8,128)(2,1)} %copy-done.26, ...), custom_call_target="tpu_custom_call" | custom-call | flops 8000000000 | bytes 10000000 | tf_op jit(solution)/shard_map/project/pallas_call | solution.py:437
  156.2 14.6 %gate_sums.1 = (bf16[1024,2048]{1,0:T(8,128)(2,1)}, f32[1024,1024]{1,0:T(8,128)}, f32[8,1024]{1,0:T(8,128)}) custom-call(s32[8]{0:T(128)} %compare_select_fusion.2.members_ref, bf16[1024,2048]{1,0:T(8,128)(2,1)} %bitcast.123, bf16[1024,1024]{1,0:T(8,128)(2,1)} %project.1.z_ref, f32[1024,1024]{1,0:T(8,128)} %get-tuple-element.175.y_ref, ...), custom_call_target="tpu_custom_call" | custom-call | flops 11000000512 | bytes 20000000 | tf_op jit(solution)/shard_map/gate_sums/pallas_call | solution.py:830
  170.9 13.1 %collective-permute-start.24 = (f32[8,1024]{1,0:T(8,128)}, f32[8,1024]{1,0:T(8,128)S(1)}, u32[]{:S(2)}, u32[]{:S(2)}) collective-permute-start(f32[8,1024]{1,0:T(8,128)} %get-tuple-element.184), channel_id=1, source_target_pairs={{0,1},{1,0},{2,3},{3,2},{4,5},{5,4},{6,7},{7,6},{8,9},{9,8},{10,11... | collective-permute-start | bytes 98312 | tf_op jit(solution)/shard_map/ppermute | solution.py:226
  194.0 9.7 %gate_back.1 = (bf16[1024,1024]{1,0:T(8,128)(2,1)}, bf16[1024,1024]{1,0:T(8,128)(2,1)}, bf16[1024,1024]{1,0:T(8,128)(2,1)}, f32[8,1024]{1,0:T(8,128)}) custom-call(f32[8,1024]{1,0:T(8,128)} %add_add_fusion.sums_ref, f32[1024,1024]{1,0:T(8,128)} %get-tuple-element.185.scaled_ref, bf16[1024,1024]{1,0:T(8,128)(2,1)} %project.1.z_ref, ...), custom_call_target="tpu_custom_call" | custom-call | flops 11000000512 | bytes 20000000 | tf_op jit(solution)/shard_map/gate_back/pallas_call | solution.py:886
  203.7 6.6 %convolution_convert_fusion.3 = bf16[1024,2048]{1,0:T(8,128)(2,1)S(1)} fusion(bf16[1024,1024]{1,0:T(8,128)(2,1)} %get-tuple-element.193, bf16[1,1024,2048]{2,1,0:T(8,128)(2,1)S(1)} %copy-done.35), kind=kOutput, calls=%fused_computation.5 | convolution fusion | flops 4297064448 | bytes 10485760 | tf_op jit(solution)/shard_map/dot_general | solution.py:239
  213.4 4.9 %convolution_convert_fusion.2 = bf16[1024,2048]{1,0:T(8,128)(2,1)S(1)} fusion(bf16[1024,1024]{1,0:T(8,128)(2,1)S(1)} %copy-done.50, bf16[1024,2048]{1,0:T(8,128)(2,1)S(1)} %copy-done.48), kind=kOutput, calls=%fused_computation.4 | convolution fusion | flops 4297064448 | bytes 10485760 | tf_op jit(solution)/shard_map/dot_general | solution.py:239
  232.5 20.5 %mix_backward.2 = (bf16[1024,1344]{1,0:T(8,128)(2,1)}, f32[8,1280]{1,0:T(8,128)}, f32[32,256]{1,0:T(8,128)}, f32[8,128,128]{2,1,0:T(8,128)}, f32[8,1280]{1,0:T(8,128)}) custom-call(bf16[1024,1280]{1,0:T(8,128)(2,1)} %get-tuple-element.186.x_ref.refs_0_, bf16[1024,1344]{1,0:T(8,128)(2,1)} %get-tuple-element.162.proj_ref.refs_1_.refs_2_, ...), custom_call_target="tpu_custom_call" | custom-call | flops 24000000000 | bytes 10000000 | tf_op jit(solution)/shard_map/mix_backward/pallas_call | solution.py:740
  264.9 20.3 %mix_backward.3 = (bf16[1024,1344]{1,0:T(8,128)(2,1)}, f32[8,1280]{1,0:T(8,128)}, f32[32,256]{1,0:T(8,128)}, f32[8,128,128]{2,1,0:T(8,128)}, f32[8,1280]{1,0:T(8,128)}) custom-call(bf16[1024,1280]{1,0:T(8,128)(2,1)} %get-tuple-element.186.x_ref.refs_0_, ...), custom_call_target="tpu_custom_call", output_to_operand_aliasing={{0}: (11, {})} | custom-call | flops 24000000000 | bytes 10000000 | tf_op jit(solution)/shard_map/mix_backward/pallas_call | solution.py:740
  293.8 8.0 %convolution_convert_fusion.grads_ref = bf16[1344,2048]{1,0:T(8,128)(2,1)S(1)} fusion(bf16[1024,1344]{1,0:T(8,128)(2,1)} %get-tuple-element.227.dx_ref, bf16[1024,2048]{1,0:T(8,128)(2,1)S(1)} %copy-done.49), kind=kOutput, calls=%fused_computation | convolution fusion | flops 5639897088 | bytes 12451840 | tf_op jit(solution)/shard_map/dot_general | solution.py:239
  306.4 6.7 %collective-permute-done.39 = bf16[1024,256]{1,0:T(8,128)(2,1)} collective-permute-done((bf16[1024,256]{1,0:T(8,128)(2,1)}, bf16[1024,256]{1,0:T(8,128)(2,1)}, u32[]{:S(2)}, u32[]{:S(2)}) %collective-permute-start.39) | collective-permute-done | bytes 524320 | tf_op jit(solution)/shard_map/ppermute | solution.py:45
  321.2 19.3 %back_norm.1 = (bf16[2,256,2048]{2,1,0:T(8,128)(2,1)}, bf16[2,256,2048]{2,1,0:T(8,128)(2,1)}, f32[8,2048]{1,0:T(8,128)}) custom-call(s32[8]{0:T(128)} %compare_select_fusion.2.members_ref, s32[1]{0:T(128)} %bitcast.2.place_ref, bf16[1024,2048]{1,0:T(8,128)(2,1)} %bitcast.122, bf16[1024,1024]{1,0:T(8,128)(2,1)} %get-tuple-element.191.dz_ref, ...), custom_call_target="tpu_custom_call" | custom-call | flops 17999998976 | bytes 24000000 | tf_op jit(solution)/shard_map/back_norm/pallas_call | solution.py:946
  348.7 5.1 %collective-permute-start.48 = (bf16[2,256,2048]{2,1,0:T(8,128)(2,1)}, bf16[2,256,2048]{2,1,0:T(8,128)(2,1)}, u32[]{:S(2)}, u32[]{:S(2)}) collective-permute-start(bf16[2,256,2048]{2,1,0:T(8,128)(2,1)} %get-tuple-element.242), channel_id=1, source_target_pairs={{0,1},{1,0},{2,3},{3,2},{4,5},{5,4},{6,7},{7,6},{8,9},{9,8},{10,11... | collective-permute-start | bytes 6291464 | tf_op jit(solution)/shard_map/ppermute | solution.py:203
  363.7 8.8 %collective-permute-done.49 = bf16[1312,256]{1,0:T(8,128)(2,1)S(1)} collective-permute-done((bf16[1312,256]{1,0:T(8,128)(2,1)}, bf16[1312,256]{1,0:T(8,128)(2,1)S(1)}, u32[]{:S(2)}, u32[]{:S(2)}) %collective-permute-start.49) | collective-permute-done | bytes 671776 | tf_op jit(solution)/shard_map/ppermute | solution.py:45
  376.0 9.1 %collective-permute-done.52 = bf16[256,2048]{1,0:T(8,128)(2,1)S(1)} collective-permute-done((bf16[256,2048]{1,0:T(8,128)(2,1)S(1)}, bf16[256,2048]{1,0:T(8,128)(2,1)S(1)}, u32[]{:S(2)}, u32[]{:S(2)}) %collective-permute-start.52) | collective-permute-done | bytes 1048608 | tf_op jit(solution)/shard_map/ppermute | solution.py:210
  398.9 5.2 %collective-permute-done.53 = bf16[1312,256]{1,0:T(8,128)(2,1)S(1)} collective-permute-done((bf16[1312,256]{1,0:T(8,128)(2,1)S(1)}, bf16[1312,256]{1,0:T(8,128)(2,1)S(1)}, u32[]{:S(2)}, u32[]{:S(2)}) %collective-permute-start.53) | collective-permute-done | bytes 671776 | tf_op jit(solution)/shard_map/ppermute | solution.py:45
  411.3 12.9 %collective-permute-done.61 = f32[80,256]{1,0:T(8,128)S(1)} collective-permute-done((f32[80,256]{1,0:T(8,128)S(1)}, f32[80,256]{1,0:T(8,128)S(1)}, u32[]{:S(2)}, u32[]{:S(2)}) %collective-permute-start.61) | collective-permute-done | bytes 81952 | tf_op jit(solution)/shard_map/ppermute | solution.py:1276
  430.9 5.1 %assemble_z.1.held_ref = f32[8512,256]{1,0:T(8,128)} custom-call(s32[1]{0:T(128)} %bitcast.2.place_ref, bf16[1024,256]{1,0:T(8,128)(2,1)} %add_convert_fusion.5.z0, bf16[1024,256]{1,0:T(8,128)(2,1)} %copy-done.42, bf16[1024,256]{1,0:T(8,128)(2,1)} %copy-done.38, bf16[1024,256]{1,0:T(8,128)(2,1)} %copy-done.43), custom_call_target="tpu_custom_call" | custom-call | flops 4000000000 | bytes 6000000 | tf_op jit(solution)/shard_map/assemble_z/pallas_call | solution.py:1031
  (386 shorter events, 180.0 us)
Async XLA Ops:
  7.2 76.3 %all-gather.7.cloned.1.call-start = ((), (), s32[]{:S(2)}) async-start(), calls=%async_computation.1 | async-start | bytes 5242880 | tf_op jit(solution)/shard_map/all_gather | solution.py:1114
  7.9 147.5 %all-gather.5.cloned.1.call-start = ((), (), s32[]{:S(2)}) async-start(), calls=%async_computation | async-start | bytes 5242880 | tf_op jit(solution)/shard_map/all_gather | solution.py:1115
  51.2 23.8 %collective-permute-start.4 = (bf16[1024,256]{1,0:T(8,128)(2,1)}, bf16[1024,256]{1,0:T(8,128)(2,1)}, u32[]{:S(2)}, u32[]{:S(2)}) collective-permute-start(bf16[1024,256]{1,0:T(8,128)(2,1)} %get-tuple-element.146.refs_0_), channel_id=1, source_target_pairs={{0,8},{8,16},{16,24},{24,28},{28,20},{20,12},{12,4},{4,0},{1,9},{9... | collective-permute-start | bytes 1572872 | tf_op jit(solution)/shard_map/ppermute | solution.py:45
  52.5 23.8 %collective-permute-start.5 = (bf16[1024,256]{1,0:T(8,128)(2,1)}, bf16[1024,256]{1,0:T(8,128)(2,1)}, u32[]{:S(2)}, u32[]{:S(2)}) collective-permute-start(bf16[1024,256]{1,0:T(8,128)(2,1)} %get-tuple-element.146.refs_0_), channel_id=1, source_target_pairs={{8,0},{16,8},{24,16},{28,24},{20,28},{12,20},{4,12},{0,4},{9,1},{1... | collective-permute-start | bytes 1572872 | tf_op jit(solution)/shard_map/ppermute | solution.py:45
  109.0 22.7 %collective-permute-start.14 = (bf16[1024,256]{1,0:T(8,128)(2,1)S(1)}, bf16[1024,256]{1,0:T(8,128)(2,1)S(1)}, u32[]{:S(2)}, u32[]{:S(2)}) collective-permute-start(bf16[1024,256]{1,0:T(8,128)(2,1)S(1)} %collective-permute-done.10.refs_7_), channel_id=1, source_target_pairs={{0,8},{8,16},{16,24},{24,28},{28,20},{20,12},{12,4},{4,0},{1,9},{9... | collective-permute-start | bytes 1572872 | tf_op jit(solution)/shard_map/ppermute | solution.py:45
  228.1 28.0 %collective-permute-start.29 = (bf16[2,256,2048]{2,1,0:T(8,128)(2,1)S(1)}, bf16[2,256,2048]{2,1,0:T(8,128)(2,1)}, u32[]{:S(2)}, u32[]{:S(2)}) collective-permute-start(bf16[2,256,2048]{2,1,0:T(8,128)(2,1)S(1)} %dynamic-slice_bitcast_fusion), channel_id=1, source_target_pairs={{0,1},{1,0},{2,3},{3,2},{4,5},{5,4},{6,7},{7,6},{8,9},{9,8},{10,11... | collective-permute-start | bytes 6291464 | tf_op jit(solution)/shard_map/ppermute | solution.py:203
  229.3 23.6 %collective-permute-start.32 = (bf16[512,256]{1,0:T(8,128)(2,1)S(1)}, bf16[512,256]{1,0:T(8,128)(2,1)S(1)}, u32[]{:S(2)}, u32[]{:S(2)}) collective-permute-start(bf16[512,256]{1,0:T(8,128)(2,1)S(1)} %get-tuple-element.198), channel_id=1, source_target_pairs={{0,8},{8,16},{16,24},{24,28},{28,20},{20,12},{12,4},{4,0},{1,9},{9... | collective-permute-start | bytes 786440 | tf_op jit(solution)/shard_map/ppermute | solution.py:45
  229.6 23.4 %collective-permute-start.33 = (bf16[512,256]{1,0:T(8,128)(2,1)S(1)}, bf16[512,256]{1,0:T(8,128)(2,1)S(1)}, u32[]{:S(2)}, u32[]{:S(2)}) collective-permute-start(bf16[512,256]{1,0:T(8,128)(2,1)S(1)} %get-tuple-element.199), channel_id=1, source_target_pairs={{8,0},{16,8},{24,16},{28,24},{20,28},{12,20},{4,12},{0,4},{9,1},{1... | collective-permute-start | bytes 786440 | tf_op jit(solution)/shard_map/ppermute | solution.py:45
  231.0 22.2 %collective-permute-start.30 = (bf16[128,2048]{1,0:T(8,128)(2,1)}, bf16[128,2048]{1,0:T(8,128)(2,1)}, u32[]{:S(2)}, u32[]{:S(2)}) collective-permute-start(bf16[128,2048]{1,0:T(8,128)(2,1)} %pad_maximum_fusion.2), channel_id=1, source_target_pairs={{0,8},{8,16},{16,24},{24,28},{28,20},{20,12},{12,4},{4,0},{1,9},{9... | collective-permute-start | bytes 1572872 | tf_op jit(solution)/shard_map/ppermute | solution.py:45
  231.2 22.0 %collective-permute-start.31 = (bf16[128,2048]{1,0:T(8,128)(2,1)}, bf16[128,2048]{1,0:T(8,128)(2,1)}, u32[]{:S(2)}, u32[]{:S(2)}) collective-permute-start(bf16[128,2048]{1,0:T(8,128)(2,1)} %pad_maximum_fusion.3), channel_id=1, source_target_pairs={{8,0},{16,8},{24,16},{28,24},{20,28},{12,20},{4,12},{0,4},{9,1},{1... | collective-permute-start | bytes 1572872 | tf_op jit(solution)/shard_map/ppermute | solution.py:45
  260.7 24.5 %collective-permute-start.36 = (bf16[1024,256]{1,0:T(8,128)(2,1)S(1)}, bf16[1024,256]{1,0:T(8,128)(2,1)}, u32[]{:S(2)}, u32[]{:S(2)}) collective-permute-start(bf16[1024,256]{1,0:T(8,128)(2,1)S(1)} %pad_maximum_fusion.4), channel_id=1, source_target_pairs={{0,8},{8,16},{16,24},{24,28},{28,20},{20,12},{12,4},{4,0},{1,9},{9... | collective-permute-start | bytes 1572872 | tf_op jit(solution)/shard_map/ppermute | solution.py:45
  260.9 24.3 %collective-permute-start.37 = (bf16[1024,256]{1,0:T(8,128)(2,1)S(1)}, bf16[1024,256]{1,0:T(8,128)(2,1)}, u32[]{:S(2)}, u32[]{:S(2)}) collective-permute-start(bf16[1024,256]{1,0:T(8,128)(2,1)S(1)} %pad_maximum_fusion.5), channel_id=1, source_target_pairs={{8,0},{16,8},{24,16},{28,24},{20,28},{12,20},{4,12},{0,4},{9,1},{1... | collective-permute-start | bytes 1572872 | tf_op jit(solution)/shard_map/ppermute | solution.py:45
  262.2 25.6 %collective-permute-start.34 = (bf16[128,2048]{1,0:T(8,128)(2,1)}, bf16[128,2048]{1,0:T(8,128)(2,1)}, u32[]{:S(2)}, u32[]{:S(2)}) collective-permute-start(bf16[128,2048]{1,0:T(8,128)(2,1)} %get-tuple-element.206), channel_id=1, source_target_pairs={{0,8},{8,16},{16,24},{24,28},{28,20},{20,12},{12,4},{4,0},{1,9},{9... | collective-permute-start | bytes 1572872 | tf_op jit(solution)/shard_map/ppermute | solution.py:45
  262.4 25.3 %collective-permute-start.35 = (bf16[128,2048]{1,0:T(8,128)(2,1)S(1)}, bf16[128,2048]{1,0:T(8,128)(2,1)}, u32[]{:S(2)}, u32[]{:S(2)}) collective-permute-start(bf16[128,2048]{1,0:T(8,128)(2,1)S(1)} %get-tuple-element.207), channel_id=1, source_target_pairs={{8,0},{16,8},{24,16},{28,24},{20,28},{12,20},{4,12},{0,4},{9,1},{1... | collective-permute-start | bytes 1572872 | tf_op jit(solution)/shard_map/ppermute | solution.py:45
  263.6 27.0 %collective-permute-start.38 = (bf16[256,2048]{1,0:T(8,128)(2,1)S(1)}, bf16[256,2048]{1,0:T(8,128)(2,1)S(1)}, u32[]{:S(2)}, u32[]{:S(2)}) collective-permute-start(bf16[256,2048]{1,0:T(8,128)(2,1)S(1)} %fusion.6), channel_id=1, source_target_pairs={{0,2},{1,3},{2,0},{3,1},{4,6},{5,7},{6,4},{7,5},{8,10},{9,11},{10,... | collective-permute-start | bytes 3145736 | tf_op jit(solution)/shard_map/ppermute | solution.py:210
  290.7 25.3 %collective-permute-start.41 = (bf16[128,2048]{1,0:T(8,128)(2,1)}, bf16[128,2048]{1,0:T(8,128)(2,1)S(1)}, u32[]{:S(2)}, u32[]{:S(2)}) collective-permute-start(bf16[128,2048]{1,0:T(8,128)(2,1)} %get-tuple-element.222), channel_id=1, source_target_pairs={{0,8},{8,16},{16,24},{24,28},{28,20},{20,12},{12,4},{4,0},{1,9},{9... | collective-permute-start | bytes 1572872 | tf_op jit(solution)/shard_map/ppermute | solution.py:45
  291.1 24.9 %collective-permute-start.42 = (bf16[128,2048]{1,0:T(8,128)(2,1)}, bf16[128,2048]{1,0:T(8,128)(2,1)S(1)}, u32[]{:S(2)}, u32[]{:S(2)}) collective-permute-start(bf16[128,2048]{1,0:T(8,128)(2,1)} %get-tuple-element.223), channel_id=1, source_target_pairs={{8,0},{16,8},{24,16},{28,24},{20,28},{12,20},{4,12},{0,4},{9,1},{1... | collective-permute-start | bytes 1572872 | tf_op jit(solution)/shard_map/ppermute | solution.py:45
  318.1 28.2 %collective-permute-start.46 = (bf16[1024,256]{1,0:T(8,128)(2,1)}, bf16[1024,256]{1,0:T(8,128)(2,1)}, u32[]{:S(2)}, u32[]{:S(2)}) collective-permute-start(bf16[1024,256]{1,0:T(8,128)(2,1)} %get-tuple-element.237), channel_id=1, source_target_pairs={{0,8},{8,16},{16,24},{24,28},{28,20},{20,12},{12,4},{4,0},{1,9},{9... | collective-permute-start | bytes 1572872 | tf_op jit(solution)/shard_map/ppermute | solution.py:45
  318.4 27.9 %collective-permute-start.47 = (bf16[1024,256]{1,0:T(8,128)(2,1)}, bf16[1024,256]{1,0:T(8,128)(2,1)}, u32[]{:S(2)}, u32[]{:S(2)}) collective-permute-start(bf16[1024,256]{1,0:T(8,128)(2,1)} %get-tuple-element.238), channel_id=1, source_target_pairs={{8,0},{16,8},{24,16},{28,24},{20,28},{12,20},{4,12},{0,4},{9,1},{1... | collective-permute-start | bytes 1572872 | tf_op jit(solution)/shard_map/ppermute | solution.py:45
  319.6 22.6 %collective-permute-start.44 = (bf16[544,256]{1,0:T(8,128)(2,1)}, bf16[544,256]{1,0:T(8,128)(2,1)S(1)}, u32[]{:S(2)}, u32[]{:S(2)}) collective-permute-start(bf16[544,256]{1,0:T(8,128)(2,1)} %get-tuple-element.226), channel_id=1, source_target_pairs={{8,0},{16,8},{24,16},{28,24},{20,28},{12,20},{4,12},{0,4},{9,1},{1... | collective-permute-start | bytes 835592 | tf_op jit(solution)/shard_map/ppermute | solution.py:45
  320.7 23.4 %collective-permute-start.43 = (bf16[768,256]{1,0:T(8,128)(2,1)}, bf16[768,256]{1,0:T(8,128)(2,1)}, u32[]{:S(2)}, u32[]{:S(2)}) collective-permute-start(bf16[768,256]{1,0:T(8,128)(2,1)} %get-tuple-element.225), channel_id=1, source_target_pairs={{0,8},{8,16},{16,24},{24,28},{28,20},{20,12},{12,4},{4,0},{1,9},{9... | collective-permute-start | bytes 1179656 | tf_op jit(solution)/shard_map/ppermute | solution.py:45
  321.1 27.7 %collective-permute-start.45 = (bf16[128,2048]{1,0:T(8,128)(2,1)}, bf16[128,2048]{1,0:T(8,128)(2,1)}, u32[]{:S(2)}, u32[]{:S(2)}) collective-permute-start(bf16[128,2048]{1,0:T(8,128)(2,1)} %add_convert_fusion.6.o0), channel_id=1, source_target_pairs={{0,2},{1,3},{2,0},{3,1},{4,6},{5,7},{6,4},{7,5},{8,10},{9,11},{10,... | collective-permute-start | bytes 1572872 | tf_op jit(solution)/shard_map/ppermute | solution.py:154
  357.0 36.3 %collective-permute-start.57 = (bf16[128,2048]{1,0:T(8,128)(2,1)}, bf16[128,2048]{1,0:T(8,128)(2,1)S(1)}, u32[]{:S(2)}, u32[]{:S(2)}) collective-permute-start(bf16[128,2048]{1,0:T(8,128)(2,1)} %add_convert_fusion.6.o0), channel_id=1, source_target_pairs={{0,1},{1,0},{2,3},{3,2},{4,5},{5,4},{6,7},{7,6},{8,9},{9,8},{10,11... | collective-permute-start | bytes 1572872 | tf_op jit(solution)/shard_map/ppermute | solution.py:158
  360.7 24.4 %collective-permute-start.52 = (bf16[256,2048]{1,0:T(8,128)(2,1)S(1)}, bf16[256,2048]{1,0:T(8,128)(2,1)S(1)}, u32[]{:S(2)}, u32[]{:S(2)}) collective-permute-start(bf16[256,2048]{1,0:T(8,128)(2,1)S(1)} %fusion.7), channel_id=1, source_target_pairs={{0,2},{1,3},{2,0},{3,1},{4,6},{5,7},{6,4},{7,5},{8,10},{9,11},{10,... | collective-permute-start | bytes 3145736 | tf_op jit(solution)/shard_map/ppermute | solution.py:210
  (104 other events, 1413.1 us)
Sparse Core Ops, SparseCore 0:
  9.6 36.9 all-gather.6
  48.1 34.4 all-gather.4
